TPU v7x, 32 devices: a whole 2x2x4 slice. The times are simulated.
32 devices in a mesh: tensor: 2 (over x), expert: 8 (over z, y), replica: 2 (over core).
Axes of the slice: x: 2, y: 2, z: 4, core: 2. Of those that a mesh axis runs over, the one named last changes fastest.
Arguments:
- tokens: bfloat16 [6304, 768], P(('expert', 'replica')), may hold values from -6 to 6
- gains: float32 [2, 2, 768], replicated, may hold values from 0.5 to 1.5
- attn_qkv: bfloat16 [2, 3, 768, 768], P(None, None, None, 'tensor'), may hold values from -0.21875 to 0.21875
- attn_out: bfloat16 [2, 768, 768], P(None, 'tensor'), may hold values from -3 to 3
- router: bfloat16 [2, 768, 8], replicated, may hold values from -0.15625 to 0.15625
- expert_in: bfloat16 [2, 8, 768, 3072], P(None, 'expert', None, 'tensor'), may hold values from -0.21875 to 0.21875
- expert_out: bfloat16 [2, 8, 3072, 768], P(None, 'expert', 'tensor'), may hold values from -1.75 to 1.75
- routes: int32 [2, 6304, 2], P(None, ('expert', 'replica')), may hold values from 0 to 7, all different within a row; in each aligned block of 394 rows (0 to 393, 394 to 787, ..., all dimensions but the last counted through in order) at most 128 rows name the same one
- cotangent: bfloat16 [6304, 768], P(('expert', 'replica')), may hold values from -6 to 6
Outputs:
- mixed_out: bfloat16 [6304, 768], P(('expert', 'replica'))
- grad_tokens: float32 [6304, 768], P(('expert', 'replica'))
- grad_gains: float32 [2, 2, 768], replicated
- grad_attn_qkv: float32 [2, 3, 768, 768], P(None, None, None, 'tensor')
- grad_attn_out: float32 [2, 768, 768], P(None, 'tensor')
- grad_router: float32 [2, 768, 8], replicated
- grad_expert_in: float32 [2, 8, 768, 3072], P(None, 'expert', 'replica', 'tensor')
- grad_expert_out: float32 [2, 8, 3072, 768], P(None, 'expert', 'tensor', 'replica')
Inputs may be any that keep to these rules, and one draw needn't show every extreme that they name: In the tokens of one block of 394, no expert is named by more than 128 routes, and in every draw some expert by exactly 128; the two experts of a token differ.
All inputs are finite; a program needn't handle non-finite values.
Results may differ from a plain program's by a relative error of at most 0.02.
Values may be sent and summed in bfloat16 or wider, within the bound.
No kernel may reach another device: no remote copies, remote signals or barrier semaphores. Data moves between devices by JAX's collectives and lax.ppermute only.
A program may use at most 192 MiB of HBM per device.

v0:
```python
import jax
import jax.numpy as jnp
from jax import lax
from jax.sharding import PartitionSpec as P

HEAD_DIM = 64
SEQ = 197


EPSILON = 1e-06


def layer_norm(stream, gain):
    center = jnp.mean(stream, axis=-1, keepdims=True)
    shifted = stream - center
    spread = jnp.mean(shifted * shifted, axis=-1, keepdims=True)
    return shifted * lax.rsqrt(spread + EPSILON) * gain


def slot_index(route_ids, expert_count, capacity):
    labels = lax.broadcasted_iota(jnp.int32, (1, 1, expert_count), 2)
    route_hits = jnp.sum((route_ids[:, :, None] == labels).astype(jnp.int32), axis=1)
    before = jnp.cumsum(route_hits, axis=0) - route_hits
    return route_ids * capacity + jnp.take_along_axis(before, route_ids, axis=1)


def on_device(tokens, gains, attn_qkv, attn_out, router, expert_in, expert_out, routes, cotangent):
    row_count, model_width = tokens.shape
    layer_count = attn_qkv.shape[0]
    local_width = attn_qkv.shape[3]
    local_heads = local_width // HEAD_DIM
    image_count = row_count // SEQ
    expert_count = router.shape[2]
    capacity = 8 * (5 * row_count // (16 * expert_count) + 1)
    score_scale = HEAD_DIM ** (-0.5)
    residual = tokens.astype(jnp.float32)
    saved = []
    for layer_index in range(layer_count):
        normed, norm_pull = jax.vjp(layer_norm, residual, gains[layer_index, 0])
        normed_bf = normed.astype(jnp.bfloat16)
        projected = jnp.einsum(
            "td,cdf->ctf", normed_bf, attn_qkv[layer_index], preferred_element_type=jnp.float32
        ).astype(jnp.bfloat16)
        head_view = projected.reshape(3, image_count, SEQ, local_heads, HEAD_DIM)
        scores = (
            jnp.einsum(
                "bqhe,bkhe->bhqk", head_view[0], head_view[1], preferred_element_type=jnp.float32
            )
            * score_scale
        )
        row_max = jnp.max(scores, axis=-1, keepdims=True)
        exp_scores = jnp.exp(scores - row_max)
        exp_total = jnp.sum(exp_scores, axis=-1, keepdims=True)
        log_total = row_max + jnp.log(exp_total)
        attn_probs = (exp_scores / exp_total).astype(jnp.bfloat16)
        mixed_rows = jnp.einsum(
            "bhqk,bkhe->bqhe", attn_probs, head_view[2], preferred_element_type=jnp.float32
        )
        mixed_rows = mixed_rows.reshape(row_count, local_width).astype(jnp.bfloat16)
        attn_part = jnp.dot(mixed_rows, attn_out[layer_index], preferred_element_type=jnp.float32)
        residual = residual + lax.psum(attn_part, "tensor")
        moe_in, moe_pull = jax.vjp(layer_norm, residual, gains[layer_index, 1])
        moe_bf = moe_in.astype(jnp.bfloat16)
        gate_probs = jax.nn.softmax(
            jnp.dot(moe_bf, router[layer_index], preferred_element_type=jnp.float32), axis=-1
        )
        route_ids = routes[layer_index]
        slot_rows = slot_index(route_ids, expert_count, capacity).reshape(-1)
        picked = jnp.take_along_axis(gate_probs, route_ids, axis=1)
        send_buffer = jnp.zeros((expert_count * capacity, model_width), jnp.bfloat16)
        send_buffer = (
            send_buffer.at[slot_rows]
            .set(jnp.repeat(moe_bf, 2, axis=0))
            .reshape(expert_count, capacity, model_width)
        )
        received = lax.all_to_all(send_buffer, "expert", split_axis=0, concat_axis=0, tiled=True)
        source_count = received.shape[0]
        flat_in = received.reshape(-1, model_width)
        pre_act = jnp.dot(flat_in, expert_in[layer_index, 0], preferred_element_type=jnp.float32)
        activation = jax.nn.gelu(pre_act).astype(jnp.bfloat16)
        expert_part = jnp.dot(
            activation, expert_out[layer_index, 0], preferred_element_type=jnp.float32
        )
        expert_part = expert_part.reshape(source_count, capacity, model_width)
        returned = lax.all_to_all(expert_part, "expert", split_axis=0, concat_axis=0, tiled=True)
        chosen = returned.reshape(-1, model_width)[slot_rows].reshape(row_count, 2, model_width)
        moe_part = jnp.sum(picked[:, :, None] * chosen, axis=1)
        residual = residual + lax.psum(moe_part, "tensor")
        kept_act = pre_act
        saved.append(
            (
                normed_bf,
                norm_pull,
                head_view,
                log_total,
                mixed_rows,
                moe_bf,
                moe_pull,
                gate_probs,
                route_ids,
                slot_rows,
                picked,
                received,
                kept_act,
                chosen,
            )
        )
    mixed_out = residual.astype(jnp.bfloat16)
    upstream = cotangent.astype(jnp.float32)
    raw_grads = [None] * layer_count
    labels = lax.broadcasted_iota(jnp.int32, (1, 1, expert_count), 2)
    for layer_index in reversed(range(layer_count)):
        (
            normed_bf,
            norm_pull,
            head_view,
            log_total,
            mixed_rows,
            moe_bf,
            moe_pull,
            gate_probs,
            route_ids,
            slot_rows,
            picked,
            received,
            kept_act,
            chosen,
        ) = saved[layer_index]
        slot_grad = (
            (picked[:, :, None] * upstream[:, None, :])
            .astype(jnp.bfloat16)
            .reshape(-1, model_width)
        )
        grad_send = jnp.zeros((expert_count * capacity, model_width), jnp.bfloat16)
        grad_send = (
            grad_send.at[slot_rows].set(slot_grad).reshape(expert_count, capacity, model_width)
        )
        grad_recv = lax.all_to_all(grad_send, "expert", split_axis=0, concat_axis=0, tiled=True)
        source_count = grad_recv.shape[0]
        grad_recv = grad_recv.reshape(-1, model_width)
        flat_in = received.reshape(-1, model_width)
        pre_act = kept_act
        activation, gelu_pull = jax.vjp(jax.nn.gelu, pre_act)
        act_grad = jnp.einsum(
            "sd,fd->sf", grad_recv, expert_out[layer_index, 0], preferred_element_type=jnp.float32
        )
        pre_grad = gelu_pull(act_grad)[0].astype(jnp.bfloat16)
        grad_w_out = jnp.einsum(
            "sf,sd->fd",
            activation.astype(jnp.bfloat16),
            grad_recv,
            preferred_element_type=jnp.float32,
        )
        grad_w_in = jnp.einsum("sd,sf->df", flat_in, pre_grad, preferred_element_type=jnp.float32)
        input_grad = jnp.einsum(
            "sf,df->sd", pre_grad, expert_in[layer_index, 0], preferred_element_type=jnp.float32
        )
        input_grad = input_grad.reshape(source_count, capacity, model_width)
        home_grad = lax.all_to_all(input_grad, "expert", split_axis=0, concat_axis=0, tiled=True)
        row_grad = jnp.sum(
            home_grad.reshape(-1, model_width)[slot_rows].reshape(row_count, 2, model_width), axis=1
        )
        gate_dot = jnp.sum(upstream[:, None, :] * chosen, axis=-1)
        row_grad, gate_dot = lax.psum((row_grad, gate_dot), "tensor")
        prob_grad = jnp.sum(
            gate_dot[:, :, None] * (route_ids[:, :, None] == labels).astype(jnp.float32), axis=1
        )
        logit_grad = gate_probs * (
            prob_grad - jnp.sum(prob_grad * gate_probs, axis=-1, keepdims=True)
        )
        logit_grad = logit_grad.astype(jnp.bfloat16)
        grad_router = jnp.einsum(
            "td,te->de", moe_bf, logit_grad, preferred_element_type=jnp.float32
        )
        norm_grad = row_grad + jnp.einsum(
            "te,de->td", logit_grad, router[layer_index], preferred_element_type=jnp.float32
        )
        resid_grad, gain_two = moe_pull(norm_grad)
        upstream = upstream + resid_grad
        out_grad = upstream.astype(jnp.bfloat16)
        grad_attn_out = jnp.einsum(
            "tf,td->fd", mixed_rows, out_grad, preferred_element_type=jnp.float32
        )
        mixed_grad = jnp.einsum(
            "td,fd->tf", out_grad, attn_out[layer_index], preferred_element_type=jnp.float32
        )
        mixed_grad = mixed_grad.astype(jnp.bfloat16).reshape(
            image_count, SEQ, local_heads, HEAD_DIM
        )
        scores = (
            jnp.einsum(
                "bqhe,bkhe->bhqk", head_view[0], head_view[1], preferred_element_type=jnp.float32
            )
            * score_scale
        )
        attn_probs = jnp.exp(scores - log_total)
        value_grad = jnp.einsum(
            "bhqk,bqhe->bkhe",
            attn_probs.astype(jnp.bfloat16),
            mixed_grad,
            preferred_element_type=jnp.float32,
        )
        prob_grad = jnp.einsum(
            "bqhe,bkhe->bhqk", mixed_grad, head_view[2], preferred_element_type=jnp.float32
        )
        score_grad = attn_probs * (
            prob_grad - jnp.sum(prob_grad * attn_probs, axis=-1, keepdims=True)
        )
        score_grad = score_grad.astype(jnp.bfloat16)
        query_grad = (
            jnp.einsum(
                "bhqk,bkhe->bqhe", score_grad, head_view[1], preferred_element_type=jnp.float32
            )
            * score_scale
        )
        key_grad = (
            jnp.einsum(
                "bhqk,bqhe->bkhe", score_grad, head_view[0], preferred_element_type=jnp.float32
            )
            * score_scale
        )
        proj_grad = (
            jnp.stack([query_grad, key_grad, value_grad])
            .reshape(3, row_count, local_width)
            .astype(jnp.bfloat16)
        )
        grad_qkv = jnp.einsum(
            "td,ctf->cdf", normed_bf, proj_grad, preferred_element_type=jnp.float32
        )
        norm_grad = jnp.einsum(
            "ctf,cdf->td", proj_grad, attn_qkv[layer_index], preferred_element_type=jnp.float32
        )
        norm_grad = lax.psum(norm_grad, "tensor")
        resid_grad, gain_one = norm_pull(norm_grad)
        upstream = upstream + resid_grad
        gain_pair = jnp.stack([gain_one, gain_two])
        raw_grads[layer_index] = (
            grad_w_in,
            grad_w_out,
            grad_qkv,
            grad_attn_out,
            grad_router,
            gain_pair,
        )
    stacked = [jnp.stack([item[position] for item in raw_grads]) for position in range(6)]
    grad_in_all, grad_out_all = (
        lax.psum_scatter(stacked[0], "replica", scatter_dimension=1, tiled=True),
        lax.psum_scatter(stacked[1], "replica", scatter_dimension=2, tiled=True),
    )
    grad_qkv_all, grad_proj_all, grad_router_all, grad_gain_all = lax.psum(
        (stacked[2], stacked[3], stacked[4], stacked[5]), ("expert", "replica")
    )
    return (
        mixed_out,
        upstream,
        grad_gain_all,
        grad_qkv_all,
        grad_proj_all,
        grad_router_all,
        grad_in_all[:, None],
        grad_out_all[:, None],
    )


def solution(mesh):
    return jax.shard_map(
        on_device,
        mesh=mesh,
        in_specs=(
            P(("expert", "replica"), None),
            P(),
            P(None, None, None, "tensor"),
            P(None, "tensor", None),
            P(),
            P(None, "expert", None, "tensor"),
            P(None, "expert", "tensor", None),
            P(None, ("expert", "replica"), None),
            P(("expert", "replica"), None),
        ),
        out_specs=(
            P(("expert", "replica"), None),
            P(("expert", "replica"), None),
            P(),
            P(None, None, None, "tensor"),
            P(None, "tensor", None),
            P(),
            P(None, "expert", "replica", "tensor"),
            P(None, "expert", "tensor", "replica"),
        ),
        check_vma=False,
    )
```

profile of v0, /device:TPU:0, one launch (start us, length us, event | category | flops | bytes accessed | tf_op | source)
XLA Modules:
  0.0 1209.6 jit_solution(15359523138905654827)
XLA Ops:
  24.5 8.1 gather_fusion.5
  33.1 35.5 %all-reduce.14.cloned.1.call-done = f32[394,768]{1,0:T(8,128)} async-done(((f32[394,768]{1,0:T(8,128)}), f32[394,768]{1,0:T(8,128)}) %all-reduce.14.cloned.1.call-update) | async-done | bytes 1210384 | tf_op jit(solution)/shard_map/psum | solution.py:61
  73.3 6.1 scatter_custom_fusion
  79.4 42.6 %all_to_all.40 = bf16[8,128,768]{2,1,0:T(8,128)(2,1)S(1)} all-to-all(bf16[8,128,768]{2,1,0:T(8,128)(2,1)S(1)} %bitcast.271), channel_id=1, replica_groups=mesh['tensor'=2,'expert'=8,'replica'=2] {'expert'}, dimensions={0} | all-to-all | bytes 3145728 | tf_op jit(solution)/shard_map/all_to_all | solution.py:76
  122.0 7.6 multiply_convert_fusion.1
  129.6 4.3 fusion.20
  133.9 3.8 all-to-all-start.1
  139.7 8.3 gather_fusion.4
  150.6 57.4 %all-to-all-done.1 = f32[8,128,768]{2,1,0:T(8,128)S(1)} async-done(((f32[8,128,768]{2,1,0:T(8,128)}), f32[8,128,768]{2,1,0:T(8,128)S(1)}, u32[]{:S(2)}, u32[]{:S(2)}) %all-to-all-start.1) | async-done | bytes 3145760 | tf_op jit(solution)/shard_map/all_to_all | solution.py:85
  208.0 3.8 gather_fusion
  211.8 3.1 reshape.413
  216.3 3.9 multiply_reduce_fusion.5
  221.5 41.1 %all-reduce.16.cloned.1.call-done = f32[394,768]{1,0:T(8,128)} async-done(((f32[394,768]{1,0:T(8,128)}), f32[394,768]{1,0:T(8,128)}) %all-reduce.16.cloned.1.call-update) | async-done | bytes 1210384 | tf_op jit(solution)/shard_map/psum | solution.py:88
  279.7 8.1 gather_fusion.7
  288.3 33.4 %all-reduce.18.cloned.1.call-done = f32[394,768]{1,0:T(8,128)} async-done(((f32[394,768]{1,0:T(8,128)}), f32[394,768]{1,0:T(8,128)}) %all-reduce.18.cloned.1.call-update) | async-done | bytes 1210384 | tf_op jit(solution)/shard_map/psum | solution.py:61
  326.6 7.5 scatter_custom_fusion.1
  334.1 5.8 all-to-all-start.2
  342.0 4.1 mul.501
  346.4 8.1 gather_fusion.6
  355.0 10.8 scatter_custom_fusion.2
  365.7 11.1 all-to-all-done.2
  376.9 4.5 all-to-all-start.4
  381.4 7.5 multiply_convert_fusion
  388.9 29.1 %all-to-all-done.4 = bf16[8,128,768]{2,1,0:T(8,128)(2,1)} async-done(((bf16[8,128,768]{2,1,0:T(8,128)(2,1)}), bf16[8,128,768]{2,1,0:T(8,128)(2,1)}, u32[]{:S(2)}, u32[]{:S(2)}) %all-to-all-start.4) | async-done | bytes 1572896 | tf_op jit(solution)/shard_map/all_to_all | solution.py:138
  418.0 8.5 fusion.13
  428.2 4.3 fusion.16
  432.5 3.7 all-to-all-start.5
  436.1 6.9 fusion.18
  443.0 64.0 %all-to-all-done.5 = f32[8,128,768]{2,1,0:T(8,128)S(1)} async-done(((f32[8,128,768]{2,1,0:T(8,128)}), f32[8,128,768]{2,1,0:T(8,128)S(1)}, u32[]{:S(2)}, u32[]{:S(2)}) %all-to-all-start.5) | async-done | bytes 3145760 | tf_op jit(solution)/shard_map/all_to_all | solution.py:159
  508.7 3.6 all-to-all-start.3
  512.4 6.9 gather_fusion.2
  519.2 4.0 reshape.425
  523.2 5.6 reduce_sum.406
  531.1 52.1 %all-to-all-done.3 = f32[8,128,768]{2,1,0:T(8,128)S(1)} async-done(((f32[8,128,768]{2,1,0:T(8,128)}), f32[8,128,768]{2,1,0:T(8,128)S(1)}, u32[]{:S(2)}, u32[]{:S(2)}) %all-to-all-start.3) | async-done | bytes 3145760 | tf_op jit(solution)/shard_map/all_to_all | solution.py:85
  583.2 3.8 gather_fusion.1
  587.0 4.1 reshape.421
  591.1 8.1 multiply_reduce_fusion.3
  599.2 9.9 psum.103
  625.0 3.5 fusion.71
  629.0 42.9 %all-reduce.22.cloned.1.call-done = f32[394,768]{1,0:T(8,128)} async-done(((f32[394,768]{1,0:T(8,128)}), f32[394,768]{1,0:T(8,128)}) %all-reduce.22.cloned.1.call-update) | async-done | bytes 1210384 | tf_op jit(solution)/shard_map/psum | solution.py:233
  678.7 3.2 mul.539
  681.9 8.9 scatter_custom_fusion.3
  690.8 42.5 %all_to_all.41 = bf16[8,128,768]{2,1,0:T(8,128)(2,1)S(1)} all-to-all(bf16[8,128,768]{2,1,0:T(8,128)(2,1)} %bitcast.270), channel_id=1, replica_groups=mesh['tensor'=2,'expert'=8,'replica'=2] {'expert'}, dimensions={0} | all-to-all | bytes 3145728 | tf_op jit(solution)/shard_map/all_to_all | solution.py:138
  733.3 9.1 fusion.6
  745.1 74.1 %all_to_all.42 = f32[8,128,768]{2,1,0:T(8,128)S(1)} all-to-all(f32[8,128,768]{2,1,0:T(8,128)S(1)} %fusion.14), channel_id=1, replica_groups=mesh['tensor'=2,'expert'=8,'replica'=2] {'expert'}, dimensions={0} | all-to-all | bytes 6291456 | tf_op jit(solution)/shard_map/all_to_all | solution.py:159
  819.2 3.8 gather_fusion.3
  823.0 4.0 reshape.430
  827.0 5.7 reduce_sum.415
  832.9 3.1 multiply_reduce_fusion.2
  836.0 14.5 %psum.106 = f32[394,2]{1,0:T(8,128)S(1)} all-reduce(f32[394,2]{1,0:T(8,128)S(1)} %multiply_reduce_fusion.2), channel_id=1, replica_groups=mesh['tensor'=2,'expert'=8,'replica'=2] {'tensor'}, use_global_device_ids=true, to_apply=%region_47.50 | all-reduce | flops 788 | bytes 6304 | tf_op jit(solution)/shard_map/psum | solution.py:164
  850.8 27.6 %all-reduce.24.cloned.1.call-done = f32[394,768]{1,0:T(8,128)} async-done(((f32[394,768]{1,0:T(8,128)}), f32[394,768]{1,0:T(8,128)}) %all-reduce.24.cloned.1.call-update) | async-done | bytes 1210384 | tf_op jit(solution)/shard_map/psum | solution.py:164
  893.2 3.9 fusion.68
  905.3 3.4 pad_maximum_fusion.2
  908.9 5.2 convolution_bitcast_fusion
  916.9 4.2 pad_maximum_fusion.1
  921.4 5.2 convolution_bitcast_fusion.2
  929.3 4.5 pad_maximum_fusion
  935.3 32.9 %all-reduce.28.cloned.1.call-done = (f32[394,768]{1,0:T(8,128)}, f32[394,768]{1,0:T(8,128)}) async-done(((f32[394,768]{1,0:T(8,128)}, f32[394,768]{1,0:T(8,128)}), (f32[394,768]{1,0:T(8,128)}, f32[394,768]{1,0:T(8,128)})) %all-reduce.28.cloned.1.call-update) | async-done | bytes 2420752 | tf_op jit(solution)/shard_map/psum | solution.py:88
  970.7 65.3 %all-reduce.2 = (f32[2,2,768]{2,1,0:T(2,128)}, f32[2,768,8]{1,2,0:T(8,128)}) all-reduce(f32[2,2,768]{2,1,0:T(2,128)S(1)} %pad_maximum_fusion.5, f32[2,768,8]{1,2,0:T(8,128)S(1)} %pad_maximum_fusion.4), channel_id=1, replica_groups=mesh['tensor'=2,'expert'=8,'replica'=2] {'expert','replica'}, use_global_device_ids=true, to_apply=%region_60.63 | all-reduce | flops 15360 | bytes 122880 | tf_op jit(solution)/shard_map/psum | solution.py:250
  1036.0 3.4 add_add_fusion.4
  1039.5 118.8 %all-reduce.26.cloned.1.call-done = (f32[2,3,768,384]{2,3,1,0:T(8,128)}, f32[2,384,768]{2,1,0:T(8,128)}) async-done(((f32[2,3,768,384]{2,3,1,0:T(8,128)}, f32[2,384,768]{2,1,0:T(8,128)}), (f32[2,3,768,384]{2,3,1,0:T(8,128)}, f32[2,384,768]{2,1,0:T(8,128)})) %all-reduce.26.cloned.1.call-update) | async-done | bytes 9437200 | tf_op jit(solution)/shard_map/psum | solution.py:250
  1158.3 8.2 copy.267
  1166.5 12.7 %reduce-scatter.5.cloned.1.call-done = f32[2,1536,384]{2,1,0:T(8,128)} async-done(((f32[2,1536,768]{2,1,0:T(8,128)}), f32[2,1536,384]{2,1,0:T(8,128)}) %reduce-scatter.5.cloned.1.call-update) | async-done | bytes 4718608 | tf_op jit(solution)/shard_map/reduce_scatter | solution.py:248
  1179.1 22.0 %reduce-scatter.3.cloned.1.call-done = f32[2,384,1536]{2,1,0:T(8,128)} async-done(((f32[2,768,1536]{2,1,0:T(8,128)}), f32[2,384,1536]{2,1,0:T(8,128)}) %reduce-scatter.3.cloned.1.call-update) | async-done | bytes 4718608 | tf_op jit(solution)/shard_map/reduce_scatter | solution.py:247
  (459 shorter events, 119.6 us)
Async XLA Ops:
  7.2 61.4 %all-reduce.14.cloned.1.call-start = ((), (), s32[]{:S(2)}) async-start(), calls=%async_computation.10 | async-start | bytes 2457600 | tf_op jit(solution)/shard_map/psum | solution.py:61
  8.5 5.6 copy-start.94
  11.3 59.1 %copy-start.85 = (f32[768]{0:T(1024)}, f32[768]{0:T(1024)S(1)}, u32[]{:S(2)}) copy-start(f32[768]{0:T(1024)S(1)} %get-tuple-element.61) | copy-start | bytes 9220
  24.5 44.1 %copy-start.14 = (bf16[394,768]{1,0:T(8,128)(2,1)S(1)}, bf16[394,768]{1,0:T(8,128)(2,1)}, u32[]{:S(2)}) copy-start(bf16[394,768]{1,0:T(8,128)(2,1)} %param.13) | copy-start | bytes 1815556
  33.1 104.6 %copy-start.116 = (s32[788]{0:T(1024)}, s32[788]{0:T(1024)S(1)}, u32[]{:S(2)}) copy-start(s32[788]{0:T(1024)S(1)} %fusion.150) | copy-start | bytes 9460
  79.4 50.2 %slice-start = ((s8[4718592]{0:T(1024)(128)(4,1)}), s8[4194304]{0:T(1024)(128)(4,1)S(1)}, s32[]{:S(2)}) async-start(s8[4718592]{0:T(1024)(128)(4,1)} %bitcast.280), calls=%async_computation.20 | async-start | bytes 8388608
  122.0 7.6 copy-start.32
  122.0 7.6 slice-start.1
  133.9 74.1 %all-to-all-start.1 = ((f32[8,128,768]{2,1,0:T(8,128)}), f32[8,128,768]{2,1,0:T(8,128)S(1)}, u32[]{:S(2)}, u32[]{:S(2)}) async-start(f32[8,128,768]{2,1,0:T(8,128)} %fusion.20), calls=%async_computation.1 | async-start | bytes 6291456 | tf_op jit(solution)/shard_map/all_to_all | solution.py:85
  137.7 124.9 %all-reduce.16.cloned.1.call-start = ((), (), s32[]{:S(2)}) async-start(), calls=%async_computation.11 | async-start | bytes 2457600 | tf_op jit(solution)/shard_map/psum | solution.py:88
  137.7 70.2 %copy-start.100 = (s32[1024]{0:T(1024)}, s32[1024]{0:T(1024)S(1)}, u32[]{:S(2)}) copy-start(s32[1024]{0:T(1024)S(1)} %pad_clamp_fusion.1) | copy-start | bytes 12292
  139.7 8.4 copy-start.106
  220.3 42.3 %copy-start.9 = (f32[394,768]{1,0:T(8,128)S(1)}, f32[394,768]{1,0:T(8,128)}, u32[]{:S(2)}) copy-start(f32[394,768]{1,0:T(8,128)} %copy-done.8) | copy-start | bytes 3631108
  220.3 101.4 %all-reduce.18.cloned.1.call-start = ((), (), s32[]{:S(2)}) async-start(), calls=%async_computation.12 | async-start | bytes 2457600 | tf_op jit(solution)/shard_map/psum | solution.py:61
  221.5 43.1 %copy-start.83 = (f32[768]{0:T(1024)S(1)}, f32[768]{0:T(1024)}, u32[]{:S(2)}) copy-start(f32[768]{0:T(1024)} %get-tuple-element.63) | copy-start | bytes 9220
  264.2 57.4 %copy-start.11 = (f32[394,768]{1,0:T(8,128)}, f32[394,768]{1,0:T(8,128)S(1)}, u32[]{:S(2)}) copy-start(f32[394,768]{1,0:T(8,128)S(1)} %get-tuple-element.79) | copy-start | bytes 3631108
  267.0 5.7 copy-start.45
  288.3 36.0 %copy-start.87 = (f32[768]{0:T(1024)S(1)}, f32[768]{0:T(1024)}, u32[]{:S(2)}) copy-start(f32[768]{0:T(1024)} %get-tuple-element.60) | copy-start | bytes 9220
  324.4 21.6 %copy-start.30 = (bf16[394,768]{1,0:T(8,128)(2,1)}, bf16[394,768]{1,0:T(8,128)(2,1)S(1)}, u32[]{:S(2)}) copy-start(bf16[394,768]{1,0:T(8,128)(2,1)S(1)} %multiply_convert_fusion.6) | copy-start | bytes 1815556
  334.1 5.9 copy-start.24
  334.1 42.8 %all-to-all-start.2 = ((bf16[8,128,768]{2,1,0:T(8,128)(2,1)}), bf16[8,128,768]{2,1,0:T(8,128)(2,1)S(1)}, u32[]{:S(2)}, u32[]{:S(2)}) async-start(bf16[8,128,768]{2,1,0:T(8,128)(2,1)} %bitcast.268), calls=%async_computation.2 | async-start | bytes 3145728 | tf_op jit(solution)/shard_map/all_to_all | solution.py:76
  376.9 12.0 copy-start.34
  376.9 41.2 %all-to-all-start.4 = ((bf16[8,128,768]{2,1,0:T(8,128)(2,1)}), bf16[8,128,768]{2,1,0:T(8,128)(2,1)}, u32[]{:S(2)}, u32[]{:S(2)}) async-start(bf16[8,128,768]{2,1,0:T(8,128)(2,1)} %bitcast.269), calls=%async_computation.4 | async-start | bytes 3145728 | tf_op jit(solution)/shard_map/all_to_all | solution.py:138
  381.4 46.8 %slice-start.2 = ((s8[4718592]{0:T(1024)(128)(4,1)}), s8[524288]{0:T(1024)(128)(4,1)S(1)}, s32[]{:S(2)}) async-start(s8[4718592]{0:T(1024)(128)(4,1)} %bitcast.282), calls=%async_computation.22 | async-start | bytes 1048576
  418.0 10.1 slice-start.3
  432.5 74.5 %all-to-all-start.5 = ((f32[8,128,768]{2,1,0:T(8,128)}), f32[8,128,768]{2,1,0:T(8,128)S(1)}, u32[]{:S(2)}, u32[]{:S(2)}) async-start(f32[8,128,768]{2,1,0:T(8,128)} %fusion.16), calls=%async_computation.5 | async-start | bytes 6291456 | tf_op jit(solution)/shard_map/all_to_all | solution.py:159
  508.7 74.5 %all-to-all-start.3 = ((f32[8,128,768]{2,1,0:T(8,128)}), f32[8,128,768]{2,1,0:T(8,128)S(1)}, u32[]{:S(2)}, u32[]{:S(2)}) async-start(f32[8,128,768]{2,1,0:T(8,128)} %fusion.18), calls=%async_computation.3 | async-start | bytes 6291456 | tf_op jit(solution)/shard_map/all_to_all | solution.py:85
  512.3 97.0 %all-reduce.20.cloned.1.call-start = ((), (), s32[]{:S(2)}) async-start(), calls=%async_computation.13 | async-start | bytes 2457600 | tf_op jit(solution)/shard_map/psum | solution.py:164
  528.9 143.0 %all-reduce.22.cloned.1.call-start = ((), (), s32[]{:S(2)}) async-start(), calls=%async_computation.14 | async-start | bytes 2457600 | tf_op jit(solution)/shard_map/psum | solution.py:233
  591.1 18.1 %copy-start.99 = (s32[394,2]{0,1:T(2,128)S(1)}, s32[394,2]{0,1:T(2,128)}, u32[]{:S(2)}) copy-start(s32[394,2]{0,1:T(2,128)} %copy-done.98) | copy-start | bytes 9460
  591.1 18.2 %copy-start.6 = (f32[394,768]{1,0:T(8,128)S(1)}, f32[394,768]{1,0:T(8,128)}, u32[]{:S(2)}) copy-start(f32[394,768]{1,0:T(8,128)} %copy-done.5) | copy-start | bytes 3631108
  625.0 46.9 %copy-start.84 = (f32[768]{0:T(1024)S(1)}, f32[768]{0:T(1024)}, u32[]{:S(2)}) copy-start(f32[768]{0:T(1024)} %get-tuple-element.63) | copy-start | bytes 9220
  625.0 46.9 %copy-start.89 = (f32[394]{0:T(512)S(1)}, f32[394]{0:T(512)}, u32[]{:S(2)}) copy-start(f32[394]{0:T(512)} %copy-done.88) | copy-start | bytes 4732
  625.0 46.9 %copy-start.103 = (f32[394]{0:T(512)S(1)}, f32[394]{0:T(512)}, u32[]{:S(2)}) copy-start(f32[394]{0:T(512)} %copy-done.102) | copy-start | bytes 4732
  628.6 43.3 %copy-start.12 = (f32[394,768]{1,0:T(8,128)S(1)}, f32[394,768]{1,0:T(8,128)}, u32[]{:S(2)}) copy-start(f32[394,768]{1,0:T(8,128)} %copy-done.11) | copy-start | bytes 3631108
  628.6 45.2 %copy-start.113 = (f32[394]{0:T(512)S(1)}, f32[394]{0:T(512)}, u32[]{:S(2)}) copy-start(f32[394]{0:T(512)} %copy-done.112) | copy-start | bytes 4732
  628.6 249.8 %all-reduce.24.cloned.1.call-start = ((), (), s32[]{:S(2)}) async-start(), calls=%async_computation.15 | async-start | bytes 2457600 | tf_op jit(solution)/shard_map/psum | solution.py:164
  681.9 60.6 %slice-start.4 = ((s8[4718592]{0:T(1024)(128)(4,1)}), s8[524288]{0:T(1024)(128)(4,1)S(1)}, s32[]{:S(2)}) async-start(s8[4718592]{0:T(1024)(128)(4,1)} %bitcast.284), calls=%async_computation.24 | async-start | bytes 1048576
  733.3 9.1 copy-start.61
  733.3 9.1 slice-start.5
  745.1 74.1 %copy-start.101 = (s32[1024]{0:T(1024)S(1)}, s32[1024]{0:T(1024)}, u32[]{:S(2)}) copy-start(s32[1024]{0:T(1024)} %copy-done.100) | copy-start | bytes 12292
  827.0 5.8 copy-start.71
  827.0 5.8 copy-start.80
  827.0 5.8 copy-start.18
  832.7 135.4 %all-reduce.28.cloned.1.call-start = ((), (), s32[]{:S(2)}) async-start(), calls=%async_computation.19 | async-start | bytes 4915200 | tf_op jit(solution)/shard_map/psum | solution.py:88
  832.8 17.8 %copy-start.97 = (s32[394,2]{0,1:T(2,128)S(1)}, s32[394,2]{0,1:T(2,128)}, u32[]{:S(2)}) copy-start(s32[394,2]{0,1:T(2,128)} %copy-done.96) | copy-start | bytes 9460
  832.9 17.8 %copy-start.69 = (f32[394,8]{0,1:T(8,128)S(1)}, f32[394,8]{0,1:T(8,128)}, u32[]{:S(2)}) copy-start(f32[394,8]{0,1:T(8,128)} %copy-done.68) | copy-start | bytes 37828
  832.9 17.8 %copy-start.93 = (f32[394]{0:T(512)S(1)}, f32[394]{0:T(512)}, u32[]{:S(2)}) copy-start(f32[394]{0:T(512)} %copy-done.92) | copy-start | bytes 4732
  832.9 17.8 %copy-start.107 = (f32[394]{0:T(512)S(1)}, f32[394]{0:T(512)}, u32[]{:S(2)}) copy-start(f32[394]{0:T(512)} %copy-done.106) | copy-start | bytes 4732
  832.9 45.5 %copy-start.10 = (f32[394,768]{1,0:T(8,128)S(1)}, f32[394,768]{1,0:T(8,128)}, u32[]{:S(2)}) copy-start(f32[394,768]{1,0:T(8,128)} %copy-done.8) | copy-start | bytes 3631108
  832.9 45.5 %copy-start.86 = (f32[768]{0:T(1024)S(1)}, f32[768]{0:T(1024)}, u32[]{:S(2)}) copy-start(f32[768]{0:T(1024)} %copy-done.85) | copy-start | bytes 9220
  832.9 45.5 %copy-start.91 = (f32[394]{0:T(512)S(1)}, f32[394]{0:T(512)}, u32[]{:S(2)}) copy-start(f32[394]{0:T(512)} %copy-done.90) | copy-start | bytes 4732
  832.9 45.5 %copy-start.105 = (f32[394]{0:T(512)S(1)}, f32[394]{0:T(512)}, u32[]{:S(2)}) copy-start(f32[394]{0:T(512)} %copy-done.104) | copy-start | bytes 4732
  850.8 29.5 %copy-start.111 = (f32[394]{0:T(512)S(1)}, f32[394]{0:T(512)}, u32[]{:S(2)}) copy-start(f32[394]{0:T(512)} %copy-done.110) | copy-start | bytes 4732
  897.1 261.2 %all-reduce.26.cloned.1.call-start = ((), (), s32[]{:S(2)}) async-start(), calls=%async_computation.18 | async-start | bytes 18874368 | tf_op jit(solution)/shard_map/psum | solution.py:250
  908.8 5.3 copy-start.62
  908.8 270.3 %reduce-scatter.5.cloned.1.call-start = ((), (), s32[]{:S(2)}) async-start(), calls=%async_computation.17 | async-start | bytes 14155776 | tf_op jit(solution)/shard_map/reduce_scatter | solution.py:248
  908.8 5.3 copy-start.120
  921.2 5.5 copy-start.33
  921.2 280.0 %reduce-scatter.3.cloned.1.call-start = ((), (), s32[]{:S(2)}) async-start(), calls=%async_computation.16 | async-start | bytes 14155776 | tf_op jit(solution)/shard_map/reduce_scatter | solution.py:247
  921.4 5.2 copy-start.55
  934.9 35.1 %copy-start.109 = (f32[394]{0:T(512)S(1)}, f32[394]{0:T(512)}, u32[]{:S(2)}) copy-start(f32[394]{0:T(512)} %copy-done.108) | copy-start | bytes 4732
  968.2 67.8 %copy-start.7 = (f32[394,768]{1,0:T(8,128)S(1)}, f32[394,768]{1,0:T(8,128)}, u32[]{:S(2)}) copy-start(f32[394,768]{1,0:T(8,128)} %copy-done.5) | copy-start | bytes 3631108
  1158.3 42.9 %copy-start.56 = (f32[2,384,768]{2,1,0:T(8,128)S(1)}, f32[2,384,768]{2,1,0:T(8,128)}, u32[]{:S(2)}) copy-start(f32[2,384,768]{2,1,0:T(8,128)} %get-tuple-element.116) | copy-start | bytes 7077892
  (78 other events, 137.3 us)
Sparse Core Ops, SparseCore 0:
  21.9 46.6 all-reduce.13
  220.4 42.0 all-reduce.15
  277.6 43.9 all-reduce.17
  529.0 44.3 all-reduce.19
  628.7 43.1 all-reduce.21
  832.9 45.4 all-reduce.23
  897.2 70.9 all-reduce.27
  972.5 185.7 all-reduce.25
  1161.2 17.8 reduce-scatter.4
  1181.9 19.1 reduce-scatter.2
where the time goes:
time: 1220 us; the launch traced here: 1210 us
  waiting for transfers between devices  581 us (48%)
  blocking collectives  249 us (20%)
  local copies, waits for them, and re-layouts  154 us (13%)
  matrix products  98.9 us (8%)
  other arithmetic  88.1 us (7%)
  starting transfers between devices  22.7 us (2%)
  between operations  16.4 us (1%)
    psum x1, waiting for transfers between devices, on_device(): lax.psum((stacked[2], stacked[3], stacked[4], stacked[5]), ('expert', 're...  119 us
    all_to_all x2, waiting for transfers between devices, on_device(): lax.all_to_all(expert_part, 'expert', split_axis=0, concat_axis=0, tiled=...  109 us
    all_to_all x1, blocking collectives, on_device(): lax.all_to_all(input_grad, 'expert', split_axis=0, concat_axis=0, tiled=T...  74.1 us
    psum x2, waiting for transfers between devices, on_device(): residual = residual + lax.psum(moe_part, 'tensor')  74 us
    psum x2, waiting for transfers between devices, on_device(): residual = residual + lax.psum(attn_part, 'tensor')  68.9 us
    psum x1, blocking collectives, on_device(): lax.psum((stacked[2], stacked[3], stacked[4], stacked[5]), ('expert', 're...  65.3 us
    all_to_all x1, waiting for transfers between devices, on_device(): lax.all_to_all(input_grad, 'expert', split_axis=0, concat_axis=0, tiled=T...  64 us
    psum x1, waiting for transfers between devices, on_device(): norm_grad = lax.psum(norm_grad, 'tensor')  42.9 us
  transfers between devices with their start and end apart: 15, of which 14 were waited for; matrix products, arithmetic and copies ran while one was open for 13% of the time, Pallas kernels for 0%

commit v1 on v0

v1 whole, which is shorter than its diff:
```python
import functools

import jax
import jax.numpy as jnp
from jax import lax
from jax.experimental import pallas as pl
from jax.experimental.pallas import tpu as pltpu
from jax.sharding import PartitionSpec as P

HEAD_DIM = 64
SEQ = 197
PAD = 208
PAIR = 2 * HEAD_DIM
EPSILON = 1e-06
GELU_A = 0.7978845608028654
GELU_B = 0.044715
F32 = jnp.float32
BF16 = jnp.bfloat16
NT = (((1,), (1,)), ((), ()))
TN = (((0,), (0,)), ((), ()))


def mm(a, b):
    return jnp.dot(a, b, preferred_element_type=F32)


def mm_nt(a, b):
    return lax.dot_general(a, b, NT, preferred_element_type=F32)


def mm_tn(a, b):
    return lax.dot_general(a, b, TN, preferred_element_type=F32)


def normalize(stream):
    shifted = stream - jnp.mean(stream, axis=-1, keepdims=True)
    scale = lax.rsqrt(jnp.mean(shifted * shifted, axis=-1, keepdims=True) + EPSILON)
    return shifted * scale, scale


def norm_back(stream, gain, out_grad):
    xhat, scale = normalize(stream)
    u = out_grad * gain
    mean_u = jnp.mean(u, axis=-1, keepdims=True)
    mean_ux = jnp.mean(u * xhat, axis=-1, keepdims=True)
    return scale * (u - mean_u - xhat * mean_ux), jnp.sum(out_grad * xhat, axis=0, keepdims=True)


def both(own_ref, got_ref):
    return own_ref[...].astype(F32) + got_ref[...].astype(F32)


VMEM_SPEC = pl.BlockSpec(memory_space=pltpu.VMEM)
SMEM_SPEC = pl.BlockSpec(memory_space=pltpu.SMEM)
ANY_SPEC = pl.BlockSpec(memory_space=pl.ANY)


def call(body, outs, args, specs, scratch=(), flops=0, limit=40):
    outs = [jax.ShapeDtypeStruct(s, d) for s, d in outs]
    size = sum(o.size * o.dtype.itemsize for o in outs)
    size += sum(a.size * a.dtype.itemsize for a in args)
    return pl.pallas_call(
        body,
        grid=(1,),
        out_shape=outs,
        in_specs=specs,
        out_specs=[VMEM_SPEC] * len(outs),
        scratch_shapes=list(scratch),
        compiler_params=pltpu.CompilerParams(vmem_limit_bytes=limit << 20),
        cost_estimate=pl.CostEstimate(flops=flops, bytes_accessed=size, transcendentals=0),
    )(*args)


def layer_spec(shape, layer):
    return pl.BlockSpec(shape, lambda step: (layer,) + (0,) * (len(shape) - 1))


def place_kernel(slot_half, where_ref, routes_ref, place_ref):
    layers, _, rows = routes_ref.shape
    experts = place_ref.shape[1] // slot_half
    first = where_ref[0] * slot_half
    before_of = lax.broadcasted_iota(jnp.int32, (rows, rows), 0) < lax.broadcasted_iota(
        jnp.int32, (rows, rows), 1
    )
    earlier = jnp.where(before_of, 1.0, 0.0).astype(BF16)
    labels = lax.broadcasted_iota(jnp.int32, (experts, rows), 0)
    slots = lax.broadcasted_iota(jnp.int32, (slot_half, rows), 0)
    for layer in range(layers):
        named = (labels == routes_ref[layer, 0:1, :]) | (labels == routes_ref[layer, 1:2, :])
        count = mm(jnp.where(named, 1.0, 0.0).astype(BF16), earlier)
        slot = jnp.where(named, count.astype(jnp.int32) - first, -1)
        for e in range(experts):
            hit = slots == slot[e : e + 1, :]
            place_ref[layer, e * slot_half : (e + 1) * slot_half, :] = jnp.where(
                hit, 1.0, 0.0
            ).astype(BF16)


def pack_kernel(place_ref, rows_ref, out_ref):
    out_ref[...] = mm(place_ref[0], rows_ref[...]).astype(BF16)


def unpack_kernel(place_ref, got_ref, out_ref):
    out_ref[...] = mm_tn(place_ref[0], got_ref[...]).astype(BF16)


def pair_masks():
    lane = lax.broadcasted_iota(jnp.int32, (PAD, PAIR), 1)
    return lane < HEAD_DIM


def softmax_rows(q, k):
    scores = mm_nt(q, k) * HEAD_DIM ** (-0.5)
    column = lax.broadcasted_iota(jnp.int32, scores.shape, 1)
    scores = jnp.where(column < SEQ, scores, -1e30)
    top = jnp.max(scores, axis=-1, keepdims=True)
    weights = jnp.exp(scores - top)
    return weights / jnp.sum(weights, axis=-1, keepdims=True)


def attend_kernel(first, *refs):
    if first:
        tokens_ref, gain_ref, qkv_ref, wo_ref, h_ref, a_ref, proj_ref, mixed_ref, out_ref = refs
        h = tokens_ref[...].astype(F32)
    else:
        mid_ref, own_ref, got_ref, gain_ref, qkv_ref, wo_ref = refs[:6]
        h_ref, a_ref, proj_ref, mixed_ref, out_ref = refs[6:]
        h = mid_ref[...] + both(own_ref, got_ref)
    h_ref[...] = h
    a = (normalize(h)[0] * gain_ref[0, 0:1, :]).astype(BF16)
    a_ref[...] = a
    for c in range(3):
        proj_ref[c] = mm(a, qkv_ref[0, c]).astype(BF16)
    low = pair_masks()
    zero = jnp.zeros((PAD, PAIR), BF16)
    for image in range(a.shape[0] // PAD):
        rows = slice(image * PAD, (image + 1) * PAD)
        for pair in range(proj_ref.shape[2] // PAIR):
            lanes = slice(pair * PAIR, (pair + 1) * PAIR)
            q, k, v = (proj_ref[c, rows, lanes] for c in range(3))
            p0 = softmax_rows(jnp.where(low, q, zero), k).astype(BF16)
            p1 = softmax_rows(jnp.where(low, zero, q), k).astype(BF16)
            mixed_ref[rows, lanes] = jnp.where(low, mm(p0, v), mm(p1, v)).astype(BF16)
    out_ref[...] = mm(mixed_ref[...], wo_ref[0]).astype(BF16)


def route_kernel(h_ref, own_ref, got_ref, gain_ref, place_ref, mid_ref, send_ref):
    mid = h_ref[...] + both(own_ref, got_ref)
    mid_ref[...] = mid
    z = (normalize(mid)[0] * gain_ref[0, 1:2, :]).astype(BF16)
    send_ref[...] = mm(place_ref[0], z).astype(BF16)


def weight_copies(layer, core, win_own, win_a, win_b, wout_own, wout_a, wout_b, win, wout, sems):
    part = win.shape[2]
    copies = []
    for c in range(2):
        copies.append((win_own.at[layer, 0, :, pl.ds(c * part, part)], win.at[c]))
        copies.append((wout_own.at[layer, 0, pl.ds(c * part, part), :], wout.at[c]))
    copies.append((win_a, win.at[2 + core]))
    copies.append((wout_a, wout.at[2 + core]))
    copies.append((win_b, win.at[3 - core]))
    copies.append((wout_b, wout.at[3 - core]))
    return [pltpu.make_async_copy(s, d, sems.at[i]) for i, (s, d) in enumerate(copies)]


def expert_kernel(
    layer, where_ref, x_ref, router_ref, win_own, win_a, win_b, wout_own, wout_a, wout_b,
    out_ref, act_ref, slope_ref, gate_ref, win, wout, total, sems,
):
    copies = weight_copies(
        layer, where_ref[2], win_own, win_a, win_b, wout_own, wout_a, wout_b, win, wout, sems
    )
    for copy in copies:
        copy.start()
    x = x_ref[...]
    part = win.shape[2]
    logits = mm_nt(x, router_ref[...])
    gate = jnp.exp(logits - jnp.max(logits, axis=-1, keepdims=True))
    gate = gate / jnp.sum(gate, axis=-1, keepdims=True)
    gate_ref[...] = gate
    mine = lax.broadcasted_iota(jnp.int32, gate.shape, 1) == where_ref[1]
    share = jnp.sum(jnp.where(mine, gate, 0.0), axis=-1, keepdims=True)
    for c in range(4):
        if c == 2:
            for copy in copies[4:]:
                copy.wait()
        if c < 2:
            copies[2 * c].wait()
        pre = mm(x, win[c])
        square = pre * pre
        bent = jnp.tanh(GELU_A * pre * (1.0 + GELU_B * square))
        half = 0.5 * (1.0 + bent)
        act = (pre * half).astype(BF16)
        slope = half + (0.5 * GELU_A) * pre * (1.0 - bent * bent) * (1.0 + 3 * GELU_B * square)
        act_ref[:, c * part : (c + 1) * part] = act
        slope_ref[:, c * part : (c + 1) * part] = slope.astype(BF16)
        if c < 2:
            copies[2 * c + 1].wait()
        term = mm(act, wout[c])
        if c == 0:
            total[...] = term
        elif c < 3:
            total[...] += term
        else:
            out_ref[...] = (share * (total[...] + term)).astype(BF16)


def expert_back_kernel(
    layer, where_ref, g_ref, x_ref, act_ref, slope_ref, gate_ref, router_ref,
    win_own, win_a, win_b, wout_own, wout_a, wout_b,
    out_ref, pre_grad_ref, scaled_ref, router_grad_ref, win, wout, total, sems,
):
    copies = weight_copies(
        layer, where_ref[2], win_own, win_a, win_b, wout_own, wout_a, wout_b, win, wout, sems
    )
    for copy in copies:
        copy.start()
    g = g_ref[...]
    part = win.shape[2]
    gate = gate_ref[...]
    mine = lax.broadcasted_iota(jnp.int32, gate.shape, 1) == where_ref[1]
    share = jnp.sum(jnp.where(mine, gate, 0.0), axis=-1, keepdims=True)
    scaled_ref[...] = (share * g.astype(F32)).astype(BF16)
    dot = jnp.zeros(share.shape, F32)
    for c in range(4):
        cols = slice(c * part, (c + 1) * part)
        if c == 2:
            for copy in copies[4:]:
                copy.wait()
        if c < 2:
            copies[2 * c + 1].wait()
        u = mm_nt(g, wout[c])
        dot = dot + jnp.sum(u * act_ref[:, cols].astype(F32), axis=-1, keepdims=True)
        pre_grad = (share * u * slope_ref[:, cols].astype(F32)).astype(BF16)
        pre_grad_ref[:, cols] = pre_grad
        if c < 2:
            copies[2 * c].wait()
        term = mm_nt(pre_grad, win[c])
        if c == 0:
            total[...] = term
        else:
            total[...] += term
    logit_grad = (dot * share * (jnp.where(mine, 1.0, 0.0) - gate)).astype(BF16)
    router_grad_ref[...] = mm_tn(logit_grad, x_ref[...])
    out_ref[...] = (total[...] + mm(logit_grad, router_ref[...])).astype(BF16)


def attend_back_kernel(
    own_ref, got_ref, mid_ref, gain_ref, g_ref, a_ref, proj_ref, mixed_ref, qkv_ref, wo_ref,
    g_out_ref, gain_grad_ref, weight_grad_ref, out_ref, back_ref, mixed_grad_ref,
):
    h_grad, gain_grad_ref[...] = norm_back(
        mid_ref[...], gain_ref[0, 1:2, :], both(own_ref, got_ref)
    )
    g = g_ref[...].astype(F32) + h_grad
    g_out_ref[...] = g
    out_grad = g.astype(BF16)
    width = proj_ref.shape[2]
    depth = a_ref.shape[1]
    mixed_grad_ref[...] = mm_nt(out_grad, wo_ref[0]).astype(BF16)
    low = pair_masks()
    zero = jnp.zeros((PAD, PAIR), BF16)
    for image in range(g.shape[0] // PAD):
        rows = slice(image * PAD, (image + 1) * PAD)
        for pair in range(width // PAIR):
            lanes = slice(pair * PAIR, (pair + 1) * PAIR)
            q, k, v = (proj_ref[c, rows, lanes] for c in range(3))
            dm = mixed_grad_ref[rows, lanes]
            parts = []
            for side in range(2):
                def pick(t, side=side):
                    return jnp.where(low, t, zero) if side == 0 else jnp.where(low, zero, t)

                probs = softmax_rows(pick(q), k)
                prob_grad = mm_nt(pick(dm), v)
                row = jnp.sum(prob_grad * probs, axis=-1, keepdims=True)
                score_grad = (probs * (prob_grad - row)).astype(BF16)
                parts.append(
                    (
                        mm(score_grad, k) * HEAD_DIM ** (-0.5),
                        mm_tn(score_grad, q) * HEAD_DIM ** (-0.5),
                        mm_tn(probs.astype(BF16), dm),
                    )
                )
            for c in range(3):
                back_ref[c, rows, lanes] = jnp.where(low, parts[0][c], parts[1][c]).astype(BF16)
    total = mm_nt(back_ref[0], qkv_ref[0, 0])
    total += mm_nt(back_ref[1], qkv_ref[0, 1])
    total += mm_nt(back_ref[2], qkv_ref[0, 2])
    out_ref[...] = total.astype(BF16)
    for c in range(3):
        weight_grad_ref[c * depth : (c + 1) * depth, :] = mm_tn(a_ref[...], back_ref[c]).astype(BF16)
    proj_grad = mm_tn(mixed_ref[...], out_grad)
    for c in range(depth // width):
        start = 3 * depth + c * width
        weight_grad_ref[start : start + width, :] = proj_grad[
            :, c * width : (c + 1) * width
        ].astype(BF16)


def stream_back_kernel(pack, *refs):
    if pack:
        own_ref, got_ref, h_ref, gain_ref, g_ref, place_ref, g_out_ref, gain_grad_ref, send_ref = refs
    else:
        own_ref, got_ref, h_ref, gain_ref, g_ref, g_out_ref, gain_grad_ref = refs
    h_grad, gain_grad_ref[...] = norm_back(h_ref[...], gain_ref[0, 0:1, :], both(own_ref, got_ref))
    g = g_ref[...] + h_grad
    g_out_ref[...] = g
    if pack:
        send_ref[...] = mm(place_ref[0], g.astype(BF16)).astype(BF16)


def swap(value, axis):
    return lax.ppermute(value, axis, [(0, 1), (1, 0)])


def on_device(tokens, gains, attn_qkv, attn_out, router, expert_in, expert_out, routes, cotangent):
    row_count, width = tokens.shape
    layers = attn_qkv.shape[0]
    local = attn_qkv.shape[3]
    images = row_count // SEQ
    rows = images * PAD
    experts = router.shape[2]
    hidden = expert_in.shape[3]
    part = hidden // 2
    capacity = 8 * (5 * row_count // (16 * experts) + 1)
    slot_half = capacity // 2
    slots = experts * slot_half
    side = lax.axis_index("tensor")
    core = lax.axis_index("replica")
    where = jnp.stack([side, lax.axis_index("expert"), core]).astype(jnp.int32)

    def spread(array):
        array = array.reshape(images, SEQ, width)
        return jnp.pad(array, ((0, 0), (0, PAD - SEQ), (0, 0))).reshape(rows, width)

    def gathered(array):
        return array.reshape(images, PAD, width)[:, :SEQ].reshape(row_count, width)

    def exchange(block):
        block = block.reshape(experts, slot_half, width)
        return lax.all_to_all(block, "expert", 0, 0, tiled=True).reshape(slots, width)

    whole = []
    for layer in range(layers):
        piece_in = lax.dynamic_slice(
            expert_in, (layer, 0, 0, core * part), (1, 1, width, part)
        ).reshape(width, part)
        piece_out = lax.dynamic_slice(
            expert_out, (layer, 0, core * part, 0), (1, 1, part, width)
        ).reshape(part, width)
        in_a, out_a = swap(piece_in, "tensor"), swap(piece_out, "tensor")
        whole.append((expert_in, in_a, swap(in_a, "replica"), expert_out, out_a, swap(out_a, "replica")))

    routes_t = jnp.swapaxes(routes, 1, 2).reshape(layers, 2, images, SEQ)
    routes_t = jnp.pad(
        routes_t, ((0, 0), (0, 0), (0, 0), (0, PAD - SEQ)), constant_values=-1
    ).reshape(layers, 2, rows)
    [place] = call(
        functools.partial(place_kernel, slot_half),
        [((layers, slots, rows), BF16)],
        (where, routes_t),
        [SMEM_SPEC, VMEM_SPEC],
        flops=2 * layers * rows * rows * experts,
    )
    router_t = jnp.swapaxes(router, 1, 2)

    def place_spec(layer):
        return layer_spec((1, slots, rows), layer)

    def gain_spec(layer):
        return layer_spec((1, 2, width), layer)

    pack_flops = 2 * slots * rows * width
    weight_scratch = [
        pltpu.VMEM((4, width, part), BF16),
        pltpu.VMEM((4, part, width), BF16),
        pltpu.VMEM((slots, width), F32),
        pltpu.SemaphoreType.DMA((8,)),
    ]
    expert_flops = 8 * slots * width * hidden

    upstream = spread(cotangent)
    last = layers - 1
    [send] = call(
        pack_kernel,
        [((slots, width), BF16)],
        (place, upstream),
        [place_spec(last), VMEM_SPEC],
        flops=pack_flops,
    )
    received_grad = exchange(send)

    stream_args = (spread(tokens),)
    saved = []
    for layer in range(layers):
        h, a, proj, mixed, term = call(
            functools.partial(attend_kernel, layer == 0),
            [
                ((rows, width), F32),
                ((rows, width), BF16),
                ((3, rows, local), BF16),
                ((rows, local), BF16),
                ((rows, width), BF16),
            ],
            (*stream_args, gains, attn_qkv, attn_out),
            [
                *([VMEM_SPEC] * len(stream_args)),
                gain_spec(layer),
                layer_spec((1, 3, width, local), layer),
                layer_spec((1, local, width), layer),
            ],
            flops=8 * rows * width * local + 4 * rows * PAD * local,
        )
        mid, send = call(
            route_kernel,
            [((rows, width), F32), ((slots, width), BF16)],
            (h, term, swap(term, "tensor"), gains, place),
            [VMEM_SPEC] * 3 + [gain_spec(layer), place_spec(layer)],
            flops=pack_flops,
        )
        received = exchange(send)
        reply, act, slope, gate = call(
            functools.partial(expert_kernel, layer),
            [
                ((slots, width), BF16),
                ((slots, 2 * hidden), BF16),
                ((slots, 2 * hidden), BF16),
                ((slots, experts), F32),
            ],
            (where, received, router_t[layer], *whole[layer]),
            [SMEM_SPEC, VMEM_SPEC, VMEM_SPEC] + [ANY_SPEC] * 6,
            weight_scratch,
            flops=expert_flops,
            limit=56,
        )
        returned = exchange(reply)
        [term] = call(
            unpack_kernel,
            [((rows, width), BF16)],
            (place, returned),
            [place_spec(layer), VMEM_SPEC],
            flops=pack_flops,
        )
        stream_args = (mid, term, swap(term, "tensor"))
        saved.append((h, a, proj, mixed, mid, received, act, slope, gate))
    mid, own, got = stream_args
    mixed_out = gathered((mid + (own.astype(F32) + got.astype(F32))).astype(BF16))

    grads = [None] * layers
    for layer in reversed(range(layers)):
        h, a, proj, mixed, mid, received, act, slope, gate = saved[layer]
        reply, pre_grad, scaled, router_grad = call(
            functools.partial(expert_back_kernel, layer),
            [
                ((slots, width), BF16),
                ((slots, 2 * hidden), BF16),
                ((slots, width), BF16),
                ((experts, width), F32),
            ],
            (where, received_grad, received, act, slope, gate, router_t[layer], *whole[layer]),
            [SMEM_SPEC] + [VMEM_SPEC] * 6 + [ANY_SPEC] * 6,
            weight_scratch,
            flops=expert_flops,
            limit=56,
        )
        returned = exchange(reply)

        half = width // 2

        def columns(array, which):
            return lax.dynamic_slice_in_dim(array, which * half, half, axis=1)

        def dot_t(left, right):
            return lax.dot_general(left, right, TN, preferred_element_type=F32)

        x_mine, x_other = columns(received, core), columns(received, 1 - core)
        s_mine, s_other = columns(scaled, core), columns(scaled, 1 - core)
        in_got = swap(dot_t(x_other, pre_grad).astype(BF16), "replica").astype(F32)
        out_got = swap(dot_t(act, s_other).astype(BF16), "replica").astype(F32)
        in_far = (dot_t(x_mine, pre_grad[:, hidden:]) + in_got[:, hidden:]).astype(BF16)
        out_far = (dot_t(act[:, hidden:], s_mine) + out_got[hidden:]).astype(BF16)
        in_far, out_far = swap(in_far, "tensor"), swap(out_far, "tensor")
        grad_in = dot_t(x_mine, pre_grad[:, :hidden]) + in_got[:, :hidden] + in_far.astype(F32)
        grad_out = dot_t(act[:, :hidden], s_mine) + out_got[:hidden] + out_far.astype(F32)

        [term] = call(
            unpack_kernel,
            [((rows, width), BF16)],
            (place, returned),
            [place_spec(layer), VMEM_SPEC],
            flops=pack_flops,
        )
        upstream, gain_two, weight_grad, term = call(
            attend_back_kernel,
            [
                ((rows, width), F32),
                ((1, width), F32),
                ((4 * width, local), BF16),
                ((rows, width), BF16),
            ],
            (term, swap(term, "tensor"), mid, gains, upstream, a, proj, mixed, attn_qkv, attn_out),
            [VMEM_SPEC] * 3
            + [gain_spec(layer)]
            + [VMEM_SPEC] * 4
            + [layer_spec((1, 3, width, local), layer), layer_spec((1, local, width), layer)],
            [pltpu.VMEM((3, rows, local), BF16), pltpu.VMEM((rows, local), BF16)],
            flops=16 * rows * width * local + 10 * rows * PAD * local,
        )
        halves = weight_grad.reshape(2, 2 * width, local)
        got = swap(lax.dynamic_index_in_dim(halves, 1 - core, keepdims=False), "replica")
        mine = lax.dynamic_index_in_dim(halves, core, keepdims=False)
        mine = (mine.astype(F32) + got.astype(F32)).astype(BF16)
        mine = mine.reshape(experts, 2 * width // experts, local)
        mine = lax.all_to_all(mine, "expert", 0, 0, tiled=True)
        mine = jnp.sum(mine.astype(F32), axis=0, keepdims=True).astype(BF16)
        mine = jnp.broadcast_to(mine, (experts, 2 * width // experts, local))
        mine = lax.all_to_all(mine, "expert", 0, 0, tiled=True).reshape(2 * width, local)
        got = swap(mine, "replica")
        lower = jnp.where(core == 0, mine, got).astype(F32)
        upper = jnp.where(core == 0, got, mine).astype(F32)
        grad_qkv = jnp.concatenate([lower, upper[:width]]).reshape(3, width, local)
        grad_proj = jnp.concatenate([upper[width : width + local], upper[width + local :]], axis=1)

        got = swap(term, "tensor")
        if layer > 0:
            upstream, gain_one, send = call(
                functools.partial(stream_back_kernel, True),
                [((rows, width), F32), ((1, width), F32), ((slots, width), BF16)],
                (term, got, h, gains, upstream, place),
                [VMEM_SPEC] * 3 + [gain_spec(layer), VMEM_SPEC, place_spec(layer - 1)],
                flops=pack_flops,
            )
            received_grad = exchange(send)
        else:
            upstream, gain_one = call(
                functools.partial(stream_back_kernel, False),
                [((rows, width), F32), ((1, width), F32)],
                (term, got, h, gains, upstream),
                [VMEM_SPEC] * 3 + [gain_spec(layer), VMEM_SPEC],
            )
        gain_pair = jnp.where(side == 0, jnp.concatenate([gain_one, gain_two]), 0.0)
        small = jnp.concatenate([router_grad, gain_pair])
        grads[layer] = (small, grad_qkv, grad_proj, grad_in, grad_out)

    small, grad_qkv, grad_proj, grad_in, grad_out = (
        jnp.stack([item[position] for item in grads]) for position in range(5)
    )
    small = lax.psum(small, ("tensor", "expert", "replica"))
    return (
        mixed_out,
        gathered(upstream),
        small[:, experts:],
        grad_qkv,
        grad_proj,
        jnp.swapaxes(small[:, :experts], 1, 2),
        grad_in[:, None],
        grad_out[:, None],
    )


def solution(mesh):
    return jax.shard_map(
        on_device,
        mesh=mesh,
        in_specs=(
            P(("expert", "replica"), None),
            P(),
            P(None, None, None, "tensor"),
            P(None, "tensor", None),
            P(),
            P(None, "expert", None, "tensor"),
            P(None, "expert", "tensor", None),
            P(None, ("expert", "replica"), None),
            P(("expert", "replica"), None),
        ),
        out_specs=(
            P(("expert", "replica"), None),
            P(("expert", "replica"), None),
            P(),
            P(None, None, None, "tensor"),
            P(None, "tensor", None),
            P(),
            P(None, "expert", "replica", "tensor"),
            P(None, "expert", "tensor", "replica"),
        ),
        check_vma=False,
    )
```

time: 1220 us -> 680 us (0.56)
  waiting for transfers between devices: 581 us -> 243 us
  local copies, waits for them, and re-layouts: 154 us -> 40.9 us
  blocking collectives: 249 us -> 146 us
  Pallas kernels: 0 us -> 100 us
  matrix products: 98.9 us -> 42 us
  other arithmetic: 88.1 us -> 32.4 us
  starting transfers between devices: 22.7 us -> 67.2 us
  between operations: 16.4 us -> 1.74 us
    psum x8 -> x0, waiting for transfers between devices: 332 us -> none  [the longest x1 119 us: on_device(): lax.psum((stacked[2], stacked[3], stacked[4], stacked[5]), ('expert', 're...]
    ppermute x0 -> x28, waiting for transfers between devices: none -> 182 us  [swap(): return lax.ppermute(value, axis, [(0, 1), (1, 0)])]
    all_to_all x5 -> x9, waiting for transfers between devices: 214 us -> 61.1 us  [the longest x5 41.7 us: exchange(): lax.all_to_all(block, 'expert', 0, 0, tiled=True).reshape(slots, width)]
    pallas_call x0 -> x18, Pallas kernels: none -> 100 us  [call(): pl.pallas_call(body, grid=(1,), out_shape=outs, in_specs=specs, out_specs...]
    all_to_all x3, blocking collectives: 159 us -> 72.2 us  [exchange(): lax.all_to_all(block, 'expert', 0, 0, tiled=True).reshape(slots, width)]
    dot_general x42 -> x12, matrix products: 98.9 us -> 42 us  [dot_t(): return lax.dot_general(left, right, TN, preferred_element_type=F32)]
    gather x14 -> x0, local copies, waits for them, and re-layouts: 52.6 us -> none  [the longest x6 17.8 us: on_device(): picked = jnp.take_along_axis(gate_probs, route_ids, axis=1)]
    reduce_sum x29 -> x2, other arithmetic: 41.6 us -> 2.88 us  [on_device(): mine = jnp.sum(mine.astype(F32), axis=0, keepdims=True).astype(BF16)]
  transfers between devices with their start and end apart: 15 -> 37, of which waited for: 14 -> 17; matrix products, arithmetic and copies ran while one was open for 13% -> 12% of each run, Pallas kernels for 0% -> 6%
where the time goes in v1:
time: 680 us; the launch traced here: 674 us
  waiting for transfers between devices  243 us (36%)
  blocking collectives  146 us (21%)
  Pallas kernels  100 us (15%)
  starting transfers between devices  67.2 us (10%)
  matrix products  42 us (6%)
  local copies, waits for them, and re-layouts  40.9 us (6%)
  other arithmetic  32.4 us (5%)
    ppermute x28, waiting for transfers between devices, swap(): return lax.ppermute(value, axis, [(0, 1), (1, 0)])  182 us
    pallas_call x18, Pallas kernels, call(): pl.pallas_call(body, grid=(1,), out_shape=outs, in_specs=specs, out_specs...  100 us
    psum x1, blocking collectives, on_device(): small = lax.psum(small, ('tensor', 'expert', 'replica'))  74.1 us
    all_to_all x3, blocking collectives, exchange(): lax.all_to_all(block, 'expert', 0, 0, tiled=True).reshape(slots, width)  72.2 us
    dot_general x12, matrix products, dot_t(): return lax.dot_general(left, right, TN, preferred_element_type=F32)  42 us
    all_to_all x5, waiting for transfers between devices, exchange(): lax.all_to_all(block, 'expert', 0, 0, tiled=True).reshape(slots, width)  41.7 us
    all_to_all x5, starting transfers between devices, exchange(): lax.all_to_all(block, 'expert', 0, 0, tiled=True).reshape(slots, width)  24.4 us
    ppermute x28, starting transfers between devices, swap(): return lax.ppermute(value, axis, [(0, 1), (1, 0)])  23.5 us
  transfers between devices with their start and end apart: 37, of which 17 were waited for; matrix products, arithmetic and copies ran while one was open for 12% of the time, Pallas kernels for 6%

profile of v1, /device:TPU:0, one launch (start us, length us, event | category | flops | bytes accessed | tf_op | source)
XLA Modules:
  0.0 673.9 jit_solution(520808181386248142)
XLA Ops:
  0.6 3.3 dynamic-slice_bitcast_fusion.3
  4.0 2.9 collective-permute-start.1
  8.6 2.3 reshape.136
  13.3 5.2 shard_map.152
  25.6 46.5 %collective-permute-done.got_ref = bf16[416,768]{1,0:T(8,128)(2,1)S(1)} collective-permute-done((bf16[416,768]{1,0:T(8,128)(2,1)}, bf16[416,768]{1,0:T(8,128)(2,1)S(1)}, u32[]{:S(2)}, u32[]{:S(2)}) %collective-permute-start) | collective-permute-done | bytes 639008 | tf_op jit(solution)/shard_map/ppermute | solution.py:315
  73.4 3.0 shard_map.154
  76.4 6.3 all-to-all-start
  83.9 18.1 %all-to-all-done = bf16[8,64,768]{2,1,0:T(8,128)(2,1)S(1)} async-done(((bf16[8,64,768]{2,1,0:T(8,128)(2,1)}), bf16[8,64,768]{2,1,0:T(8,128)(2,1)S(1)}, u32[]{:S(2)}, u32[]{:S(2)}) %all-to-all-start) | async-done | bytes 786464 | tf_op jit(solution)/shard_map/all_to_all | solution.py:343
  102.9 13.6 %shard_map.155 = (bf16[512,768]{1,0:T(8,128)(2,1)}, bf16[512,3072]{1,0:T(8,128)(2,1)}, bf16[512,3072]{1,0:T(8,128)(2,1)}, f32[512,8]{1,0:T(8,128)}) custom-call(s32[3]{0:T(128)} %copy-done.38, bf16[512,768]{1,0:T(8,128)(2,1)} %bitcast.108, bf16[8,768]{1,0:T(8,128)(2,1)} %get-tuple-element.123.router_ref, bf16[2,1,768,1536]{3,2,1,0:T(8,128)(2,1)} %win_own.7, ...), custom_call_target="tpu_custom_call" | custom-call | flops 4831838208 | bytes 22048780 | tf_op jit(solution)/shard_map/pallas_call | solution.py:62
  116.5 24.3 %all_to_all.60 = bf16[8,64,768]{2,1,0:T(8,128)(2,1)S(1)} all-to-all(bf16[8,64,768]{2,1,0:T(8,128)(2,1)} %bitcast.121), channel_id=1, replica_groups=mesh['tensor'=2,'expert'=8,'replica'=2] {'expert'}, dimensions={0} | all-to-all | bytes 1572864 | tf_op jit(solution)/shard_map/all_to_all | solution.py:343
  142.9 13.4 %collective-permute-done.5.refs_2_ = bf16[416,768]{1,0:T(8,128)(2,1)S(1)} collective-permute-done((bf16[416,768]{1,0:T(8,128)(2,1)S(1)}, bf16[416,768]{1,0:T(8,128)(2,1)S(1)}, u32[]{:S(2)}, u32[]{:S(2)}) %collective-permute-start.5) | collective-permute-done | bytes 639008 | tf_op jit(solution)/shard_map/ppermute | solution.py:315
  156.3 4.4 shard_map.157
  165.1 13.8 %collective-permute-done.6.got_ref = bf16[416,768]{1,0:T(8,128)(2,1)S(1)} collective-permute-done((bf16[416,768]{1,0:T(8,128)(2,1)S(1)}, bf16[416,768]{1,0:T(8,128)(2,1)S(1)}, u32[]{:S(2)}, u32[]{:S(2)}) %collective-permute-start.6) | collective-permute-done | bytes 639008 | tf_op jit(solution)/shard_map/ppermute | solution.py:315
  178.9 1.9 shard_map.158
  183.0 4.5 all-to-all-start.2
  187.5 16.8 %collective-permute-done.7.win_a = bf16[768,768]{1,0:T(8,128)(2,1)} collective-permute-done((bf16[768,768]{1,0:T(8,128)(2,1)}, bf16[768,768]{1,0:T(8,128)(2,1)}, u32[]{:S(2)}, u32[]{:S(2)}) %collective-permute-start.7) | collective-permute-done | bytes 1179680 | tf_op jit(solution)/shard_map/ppermute | solution.py:315
  204.3 21.9 %collective-permute-done.9.wout_a = bf16[768,768]{1,0:T(8,128)(2,1)} collective-permute-done((bf16[768,768]{1,0:T(8,128)(2,1)}, bf16[768,768]{1,0:T(8,128)(2,1)}, u32[]{:S(2)}, u32[]{:S(2)}) %collective-permute-start.9) | collective-permute-done | bytes 1179680 | tf_op jit(solution)/shard_map/ppermute | solution.py:315
  227.8 5.8 all-to-all-start.4
  233.6 13.5 %shard_map.159 = (bf16[512,768]{1,0:T(8,128)(2,1)}, bf16[512,3072]{1,0:T(8,128)(2,1)}, bf16[512,3072]{1,0:T(8,128)(2,1)}, f32[512,8]{1,0:T(8,128)}) custom-call(s32[3]{0:T(128)} %copy-done.38, bf16[512,768]{1,0:T(8,128)(2,1)} %bitcast.14.x_ref, bf16[8,768]{1,0:T(8,128)(2,1)} %get-tuple-element.122.router_ref, bf16[2,1,768,1536]{3,2,1,0:T(8,128)(2,1)} %win_own.7, ...), custom_call_target="tpu_custom_call" | custom-call | flops 4831838208 | bytes 22048780 | tf_op jit(solution)/shard_map/pallas_call | solution.py:62
  247.2 7.0 %all-to-all-done.4 = bf16[8,64,768]{2,1,0:T(8,128)(2,1)} async-done(((bf16[8,64,768]{2,1,0:T(8,128)(2,1)}), bf16[8,64,768]{2,1,0:T(8,128)(2,1)}, u32[]{:S(2)}, u32[]{:S(2)}) %all-to-all-start.4) | async-done | bytes 786464 | tf_op jit(solution)/shard_map/all_to_all | solution.py:343
  254.2 13.9 %shard_map.162 = (bf16[512,768]{1,0:T(8,128)(2,1)}, bf16[512,3072]{1,0:T(8,128)(2,1)}, bf16[512,768]{1,0:T(8,128)(2,1)}, f32[8,768]{1,0:T(8,128)}) custom-call(s32[3]{0:T(128)} %copy-done.38, bf16[512,768]{1,0:T(8,128)(2,1)} %bitcast.23.g_ref, bf16[512,768]{1,0:T(8,128)(2,1)} %bitcast.14.x_ref, bf16[512,3072]{1,0:T(8,128)(2,1)} %get-tuple-element.61.act_ref, ...), custom_call_target="tpu_custom_call" | custom-call | flops 4831838208 | bytes 26791948 | tf_op jit(solution)/shard_map/pallas_call | solution.py:62
  268.1 24.2 %all_to_all.61 = bf16[8,64,768]{2,1,0:T(8,128)(2,1)S(1)} all-to-all(bf16[8,64,768]{2,1,0:T(8,128)(2,1)} %bitcast.120), channel_id=1, replica_groups=mesh['tensor'=2,'expert'=8,'replica'=2] {'expert'}, dimensions={0} | all-to-all | bytes 1572864 | tf_op jit(solution)/shard_map/all_to_all | solution.py:343
  294.4 13.4 %collective-permute-done.12.got_ref = bf16[416,768]{1,0:T(8,128)(2,1)S(1)} collective-permute-done((bf16[416,768]{1,0:T(8,128)(2,1)S(1)}, bf16[416,768]{1,0:T(8,128)(2,1)S(1)}, u32[]{:S(2)}, u32[]{:S(2)}) %collective-permute-start.12) | collective-permute-done | bytes 639008 | tf_op jit(solution)/shard_map/ppermute | solution.py:315
  307.8 10.4 %shard_map.164 = (f32[416,768]{1,0:T(8,128)S(1)}, f32[1,768]{1,0:T(1,128)S(1)}, bf16[3072,384]{1,0:T(8,128)(2,1)S(1)}, bf16[416,768]{1,0:T(8,128)(2,1)S(1)}) custom-call(bf16[416,768]{1,0:T(8,128)(2,1)S(1)} %shard_map.163.own_ref, bf16[416,768]{1,0:T(8,128)(2,1)S(1)} %collective-permute-done.12.got_ref, f32[416,768]{1,0:T(8,128)S(1)} %copy-done.11, ...), custom_call_target="tpu_custom_call" | custom-call | flops 2295201792 | bytes 14121984 | tf_op jit(solution)/shard_map/pallas_call | solution.py:62
  319.8 12.5 %collective-permute-done.13.refs_1_ = bf16[416,768]{1,0:T(8,128)(2,1)S(1)} collective-permute-done((bf16[416,768]{1,0:T(8,128)(2,1)S(1)}, bf16[416,768]{1,0:T(8,128)(2,1)S(1)}, u32[]{:S(2)}, u32[]{:S(2)}) %collective-permute-start.13) | collective-permute-done | bytes 639008 | tf_op jit(solution)/shard_map/ppermute | solution.py:315
  334.8 23.7 %all_to_all.62 = bf16[8,64,768]{2,1,0:T(8,128)(2,1)} all-to-all(bf16[8,64,768]{2,1,0:T(8,128)(2,1)S(1)} %bitcast.101), channel_id=1, replica_groups=mesh['tensor'=2,'expert'=8,'replica'=2] {'expert'}, dimensions={0} | all-to-all | bytes 1572864 | tf_op jit(solution)/shard_map/all_to_all | solution.py:343
  358.5 13.8 %shard_map.166 = (bf16[512,768]{1,0:T(8,128)(2,1)}, bf16[512,3072]{1,0:T(8,128)(2,1)}, bf16[512,768]{1,0:T(8,128)(2,1)}, f32[8,768]{1,0:T(8,128)}) custom-call(s32[3]{0:T(128)} %copy-done.38, bf16[512,768]{1,0:T(8,128)(2,1)} %bitcast.116, bf16[512,768]{1,0:T(8,128)(2,1)} %bitcast.109, bf16[512,3072]{1,0:T(8,128)(2,1)} %get-tuple-element.71.act_ref, ...), custom_call_target="tpu_custom_call" | custom-call | flops 4831838208 | bytes 26791948 | tf_op jit(solution)/shard_map/pallas_call | solution.py:62
  372.3 3.6 all-to-all-start.7
  375.9 2.4 dynamic-slice_bitcast_fusion
  378.3 16.6 %all-to-all-done.7 = bf16[8,64,768]{2,1,0:T(8,128)(2,1)S(1)} async-done(((bf16[8,64,768]{2,1,0:T(8,128)(2,1)}), bf16[8,64,768]{2,1,0:T(8,128)(2,1)S(1)}, u32[]{:S(2)}, u32[]{:S(2)}) %all-to-all-start.7) | async-done | bytes 786464 | tf_op jit(solution)/shard_map/all_to_all | solution.py:343
  394.9 4.2 all-to-all-start.3
  402.0 3.1 fusion.12
  405.0 10.7 %collective-permute-done.14.got_ref = bf16[416,768]{1,0:T(8,128)(2,1)} collective-permute-done((bf16[416,768]{1,0:T(8,128)(2,1)}, bf16[416,768]{1,0:T(8,128)(2,1)}, u32[]{:S(2)}, u32[]{:S(2)}) %collective-permute-start.14) | collective-permute-done | bytes 639008 | tf_op jit(solution)/shard_map/ppermute | solution.py:315
  417.8 12.3 %shard_map.168 = (f32[416,768]{1,0:T(8,128)S(1)}, f32[1,768]{1,0:T(1,128)S(1)}, bf16[3072,384]{1,0:T(8,128)(2,1)S(1)}, bf16[416,768]{1,0:T(8,128)(2,1)S(1)}) custom-call(bf16[416,768]{1,0:T(8,128)(2,1)} %shard_map.167.own_ref, bf16[416,768]{1,0:T(8,128)(2,1)} %collective-permute-done.14.got_ref, f32[416,768]{1,0:T(8,128)S(1)} %copy-done.14, ...), custom_call_target="tpu_custom_call" | custom-call | flops 2295201792 | bytes 14760960 | tf_op jit(solution)/shard_map/pallas_call | solution.py:62
  433.4 6.1 all-to-all-start.10
  440.6 5.3 convolution_convert_fusion
  445.9 3.9 convolution_convert_fusion.2
  451.6 14.3 %all-to-all-done.10 = bf16[8,192,384]{2,1,0:T(8,128)(2,1)} async-done(((bf16[8,192,384]{2,1,0:T(8,128)(2,1)}), bf16[8,192,384]{2,1,0:T(8,128)(2,1)}, u32[]{:S(2)}, u32[]{:S(2)}) %all-to-all-start.10) | async-done | bytes 1179680 | tf_op jit(solution)/shard_map/all_to_all | solution.py:516
  466.0 3.6 all-to-all-start.8
  469.5 4.8 convolution_convert_fusion.3
  474.4 2.1 convert_element_type.138
  477.2 3.3 convolution_convert_fusion.1
  481.0 2.1 fusion.11
  486.9 4.4 convert_element_type.130
  492.7 5.1 all-to-all-done.8
  499.2 3.8 all-to-all-start.11
  503.0 4.2 fusion.9
  508.5 17.4 %collective-permute-done.11 = bf16[416,768]{1,0:T(8,128)(2,1)} collective-permute-done((bf16[416,768]{1,0:T(8,128)(2,1)S(1)}, bf16[416,768]{1,0:T(8,128)(2,1)}, u32[]{:S(2)}, u32[]{:S(2)}) %collective-permute-start.11) | collective-permute-done | bytes 639008 | tf_op jit(solution)/shard_map/ppermute | solution.py:315
  528.4 5.2 fusion.4
  535.0 2.2 convert_element_type.126
  537.2 1.9 fusion.8
  540.2 10.9 %collective-permute-done.23 = bf16[384,1536]{1,0:T(8,128)(2,1)} collective-permute-done((bf16[384,1536]{1,0:T(8,128)(2,1)}, bf16[384,1536]{1,0:T(8,128)(2,1)}, u32[]{:S(2)}, u32[]{:S(2)}) %collective-permute-start.23) | collective-permute-done | bytes 1179680 | tf_op jit(solution)/shard_map/ppermute | solution.py:315
  551.2 3.7 fusion.6
  554.9 2.1 convert_element_type.134
  557.6 2.1 fusion.10
  561.8 2.9 collective-permute-done.15.refs_1_
  568.5 5.9 all-to-all-start.9
  575.7 74.1 %psum.7 = f32[2,10,768]{2,1,0:T(8,128)S(1)} all-reduce(f32[2,10,768]{2,1,0:T(8,128)S(1)} %pad_maximum_fusion.4), channel_id=1, replica_groups=mesh['tensor'=2,'expert'=8,'replica'=2] {'tensor','expert','replica'}, use_global_device_ids=true, to_apply=%region_0.1 | all-reduce | flops 15360 | bytes 122880 | tf_op jit(solution)/shard_map/psum | solution.py:550
  651.1 3.4 fusion.7
  654.6 2.7 maximum_bitcast_fusion
  658.6 2.3 fusion.5
  660.9 2.5 maximum_bitcast_fusion.1
  664.6 1.9 collective-permute-done.17
  668.5 3.4 pad_maximum_fusion
  (235 shorter events, 71.4 us)
Async XLA Ops:
  4.0 78.7 %collective-permute-start.1 = (bf16[768,768]{1,0:T(8,128)(2,1)}, bf16[768,768]{1,0:T(8,128)(2,1)}, u32[]{:S(2)}, u32[]{:S(2)}) collective-permute-start(bf16[768,768]{1,0:T(8,128)(2,1)} %get-tuple-element.113), channel_id=1, source_target_pairs={{0,16},{16,0},{1,17},{17,1},{2,18},{18,2},{3,19},{19,3},{4,20},{20... | collective-permute-start | bytes 3538952 | tf_op jit(solution)/shard_map/ppermute | solution.py:315
  8.5 74.3 %collective-permute-start.3 = (bf16[768,768]{1,0:T(8,128)(2,1)}, bf16[768,768]{1,0:T(8,128)(2,1)}, u32[]{:S(2)}, u32[]{:S(2)}) collective-permute-start(bf16[768,768]{1,0:T(8,128)(2,1)} %get-tuple-element.111), channel_id=1, source_target_pairs={{0,16},{16,0},{1,17},{17,1},{2,18},{18,2},{3,19},{19,3},{4,20},{20... | collective-permute-start | bytes 3538952 | tf_op jit(solution)/shard_map/ppermute | solution.py:315
  22.1 50.0 %collective-permute-start = (bf16[416,768]{1,0:T(8,128)(2,1)}, bf16[416,768]{1,0:T(8,128)(2,1)S(1)}, u32[]{:S(2)}, u32[]{:S(2)}) collective-permute-start(bf16[416,768]{1,0:T(8,128)(2,1)} %get-tuple-element.52.own_ref), channel_id=1, source_target_pairs={{0,16},{16,0},{1,17},{17,1},{2,18},{18,2},{3,19},{19,3},{4,20},{20... | collective-permute-start | bytes 1916936 | tf_op jit(solution)/shard_map/ppermute | solution.py:315
  24.7 51.7 %copy-start.38 = (s32[3]{0:T(128)}, s32[3]{0:T(128)S(1)}, u32[]{:S(2)}) copy-start(s32[3]{0:T(128)S(1)} %pad_add_fusion.where_ref) | copy-start | bytes 40
  73.4 9.9 %copy-start.64 = (bf16[2,768,8]{1,2,0:T(8,128)(2,1)S(1)}, bf16[2,768,8]{1,2,0:T(8,128)(2,1)}, u32[]{:S(2)}) copy-start(bf16[2,768,8]{1,2,0:T(8,128)(2,1)} %param.13) | copy-start | bytes 73732
  76.4 79.9 %copy-start.13 = (f32[416,768]{1,0:T(8,128)}, f32[416,768]{1,0:T(8,128)S(1)}, u32[]{:S(2)}) copy-start(f32[416,768]{1,0:T(8,128)S(1)} %get-tuple-element.53.refs_0_.mid_ref) | copy-start | bytes 3833860
  76.4 25.6 %all-to-all-start = ((bf16[8,64,768]{2,1,0:T(8,128)(2,1)}), bf16[8,64,768]{2,1,0:T(8,128)(2,1)S(1)}, u32[]{:S(2)}, u32[]{:S(2)}) async-start(bf16[8,64,768]{2,1,0:T(8,128)(2,1)} %bitcast.5), calls=%async_computation | async-start | bytes 1572864 | tf_op jit(solution)/shard_map/all_to_all | solution.py:343
  82.7 19.3 %collective-permute-start.2 = (bf16[768,768]{1,0:T(8,128)(2,1)}, bf16[768,768]{1,0:T(8,128)(2,1)}, u32[]{:S(2)}, u32[]{:S(2)}) collective-permute-start(bf16[768,768]{1,0:T(8,128)(2,1)} %collective-permute-done.1.win_a), channel_id=1, source_target_pairs={{0,1},{1,0},{2,3},{3,2},{4,5},{5,4},{6,7},{7,6},{8,9},{9,8},{10,11... | collective-permute-start | bytes 3538952 | tf_op jit(solution)/shard_map/ppermute | solution.py:315
  82.8 19.2 %collective-permute-start.4 = (bf16[768,768]{1,0:T(8,128)(2,1)}, bf16[768,768]{1,0:T(8,128)(2,1)}, u32[]{:S(2)}, u32[]{:S(2)}) collective-permute-start(bf16[768,768]{1,0:T(8,128)(2,1)} %collective-permute-done.3.wout_a), channel_id=1, source_target_pairs={{0,1},{1,0},{2,3},{3,2},{4,5},{5,4},{6,7},{7,6},{8,9},{9,8},{10,11... | collective-permute-start | bytes 3538952 | tf_op jit(solution)/shard_map/ppermute | solution.py:315
  102.9 53.4 %copy-start.4 = (bf16[2,384,768]{2,1,0:T(8,128)(2,1)S(1)}, bf16[2,384,768]{2,1,0:T(8,128)(2,1)}, u32[]{:S(2)}) copy-start(bf16[2,384,768]{2,1,0:T(8,128)(2,1)} %wo_ref.3) | copy-start | bytes 3538948
  116.5 39.8 %copy-start.1 = (bf16[2,3,768,384]{3,2,1,0:T(8,128)(2,1)S(1)}, bf16[2,3,768,384]{3,2,1,0:T(8,128)(2,1)}, u32[]{:S(2)}) copy-start(bf16[2,3,768,384]{3,2,1,0:T(8,128)(2,1)} %qkv_ref.3) | copy-start | bytes 10616836
  141.3 15.0 %collective-permute-start.5 = (bf16[416,768]{1,0:T(8,128)(2,1)S(1)}, bf16[416,768]{1,0:T(8,128)(2,1)S(1)}, u32[]{:S(2)}, u32[]{:S(2)}) collective-permute-start(bf16[416,768]{1,0:T(8,128)(2,1)S(1)} %shard_map.156.refs_1_), channel_id=1, source_target_pairs={{0,16},{16,0},{1,17},{17,1},{2,18},{18,2},{3,19},{19,3},{4,20},{20... | collective-permute-start | bytes 1916936 | tf_op jit(solution)/shard_map/ppermute | solution.py:315
  161.6 19.3 %copy-start.25 = (bf16[3,416,384]{2,1,0:T(8,128)(2,1)}, bf16[3,416,384]{2,1,0:T(8,128)(2,1)S(1)}, u32[]{:S(2)}) copy-start(bf16[3,416,384]{2,1,0:T(8,128)(2,1)S(1)} %get-tuple-element.66.proj_ref) | copy-start | bytes 2875396
  161.6 21.4 %copy-start.36 = (bf16[416,384]{1,0:T(8,128)(2,1)}, bf16[416,384]{1,0:T(8,128)(2,1)S(1)}, u32[]{:S(2)}) copy-start(bf16[416,384]{1,0:T(8,128)(2,1)S(1)} %get-tuple-element.67.mixed_ref) | copy-start | bytes 958468
  161.6 17.3 %collective-permute-start.6 = (bf16[416,768]{1,0:T(8,128)(2,1)S(1)}, bf16[416,768]{1,0:T(8,128)(2,1)S(1)}, u32[]{:S(2)}, u32[]{:S(2)}) collective-permute-start(bf16[416,768]{1,0:T(8,128)(2,1)S(1)} %get-tuple-element.57.own_ref), channel_id=1, source_target_pairs={{0,16},{16,0},{1,17},{17,1},{2,18},{18,2},{3,19},{19,3},{4,20},{20... | collective-permute-start | bytes 1916936 | tf_op jit(solution)/shard_map/ppermute | solution.py:315
  163.1 41.2 %collective-permute-start.7 = (bf16[768,768]{1,0:T(8,128)(2,1)}, bf16[768,768]{1,0:T(8,128)(2,1)}, u32[]{:S(2)}, u32[]{:S(2)}) collective-permute-start(bf16[768,768]{1,0:T(8,128)(2,1)} %get-tuple-element.112), channel_id=1, source_target_pairs={{0,16},{16,0},{1,17},{17,1},{2,18},{18,2},{3,19},{19,3},{4,20},{20... | collective-permute-start | bytes 3538952 | tf_op jit(solution)/shard_map/ppermute | solution.py:315
  163.6 62.6 %collective-permute-start.9 = (bf16[768,768]{1,0:T(8,128)(2,1)}, bf16[768,768]{1,0:T(8,128)(2,1)}, u32[]{:S(2)}, u32[]{:S(2)}) collective-permute-start(bf16[768,768]{1,0:T(8,128)(2,1)} %get-tuple-element.110), channel_id=1, source_target_pairs={{0,16},{16,0},{1,17},{17,1},{2,18},{18,2},{3,19},{19,3},{4,20},{20... | collective-permute-start | bytes 3538952 | tf_op jit(solution)/shard_map/ppermute | solution.py:315
  178.9 47.3 %copy-start.57 = (bf16[394,768]{1,0:T(8,128)(2,1)S(1)}, bf16[394,768]{1,0:T(8,128)(2,1)}, u32[]{:S(2)}) copy-start(bf16[394,768]{1,0:T(8,128)(2,1)} %param.17) | copy-start | bytes 1815556
  183.0 44.8 %all-to-all-start.2 = ((bf16[8,64,768]{2,1,0:T(8,128)(2,1)}), bf16[8,64,768]{2,1,0:T(8,128)(2,1)}, u32[]{:S(2)}, u32[]{:S(2)}) async-start(bf16[8,64,768]{2,1,0:T(8,128)(2,1)} %bitcast.13), calls=%async_computation.2 | async-start | bytes 1572864 | tf_op jit(solution)/shard_map/all_to_all | solution.py:343
  204.3 29.3 %collective-permute-start.8 = (bf16[768,768]{1,0:T(8,128)(2,1)}, bf16[768,768]{1,0:T(8,128)(2,1)}, u32[]{:S(2)}, u32[]{:S(2)}) collective-permute-start(bf16[768,768]{1,0:T(8,128)(2,1)} %collective-permute-done.7.win_a), channel_id=1, source_target_pairs={{0,1},{1,0},{2,3},{3,2},{4,5},{5,4},{6,7},{7,6},{8,9},{9,8},{10,11... | collective-permute-start | bytes 3538952 | tf_op jit(solution)/shard_map/ppermute | solution.py:315
  226.2 7.4 %collective-permute-start.10 = (bf16[768,768]{1,0:T(8,128)(2,1)}, bf16[768,768]{1,0:T(8,128)(2,1)}, u32[]{:S(2)}, u32[]{:S(2)}) collective-permute-start(bf16[768,768]{1,0:T(8,128)(2,1)} %collective-permute-done.9.wout_a), channel_id=1, source_target_pairs={{0,1},{1,0},{2,3},{3,2},{4,5},{5,4},{6,7},{7,6},{8,9},{9,8},{10,11... | collective-permute-start | bytes 3538952 | tf_op jit(solution)/shard_map/ppermute | solution.py:315
  227.8 26.3 %all-to-all-start.4 = ((bf16[8,64,768]{2,1,0:T(8,128)(2,1)}), bf16[8,64,768]{2,1,0:T(8,128)(2,1)}, u32[]{:S(2)}, u32[]{:S(2)}) async-start(bf16[8,64,768]{2,1,0:T(8,128)(2,1)} %bitcast.92), calls=%async_computation.4 | async-start | bytes 1572864 | tf_op jit(solution)/shard_map/all_to_all | solution.py:343
  254.1 53.6 %copy-start.11 = (f32[416,768]{1,0:T(8,128)S(1)}, f32[416,768]{1,0:T(8,128)}, u32[]{:S(2)}) copy-start(f32[416,768]{1,0:T(8,128)} %copy-done.10) | copy-start | bytes 3833860
  254.1 53.6 %copy-start.26 = (bf16[3,416,384]{2,1,0:T(8,128)(2,1)S(1)}, bf16[3,416,384]{2,1,0:T(8,128)(2,1)}, u32[]{:S(2)}) copy-start(bf16[3,416,384]{2,1,0:T(8,128)(2,1)} %copy-done.25) | copy-start | bytes 2875396
  254.1 53.6 %copy-start.33 = (bf16[416,768]{1,0:T(8,128)(2,1)S(1)}, bf16[416,768]{1,0:T(8,128)(2,1)}, u32[]{:S(2)}) copy-start(bf16[416,768]{1,0:T(8,128)(2,1)} %copy-done.32) | copy-start | bytes 1916932
  268.0 39.7 %copy-start.2 = (bf16[2,3,768,384]{3,2,1,0:T(8,128)(2,1)S(1)}, bf16[2,3,768,384]{3,2,1,0:T(8,128)(2,1)}, u32[]{:S(2)}) copy-start(bf16[2,3,768,384]{3,2,1,0:T(8,128)(2,1)} %qkv_ref.3) | copy-start | bytes 10616836
  268.1 39.7 %copy-start.37 = (bf16[416,384]{1,0:T(8,128)(2,1)S(1)}, bf16[416,384]{1,0:T(8,128)(2,1)}, u32[]{:S(2)}) copy-start(bf16[416,384]{1,0:T(8,128)(2,1)} %copy-done.36) | copy-start | bytes 958468
  292.8 14.9 %collective-permute-start.12 = (bf16[416,768]{1,0:T(8,128)(2,1)S(1)}, bf16[416,768]{1,0:T(8,128)(2,1)S(1)}, u32[]{:S(2)}, u32[]{:S(2)}) collective-permute-start(bf16[416,768]{1,0:T(8,128)(2,1)S(1)} %shard_map.163.own_ref), channel_id=1, source_target_pairs={{0,16},{16,0},{1,17},{17,1},{2,18},{18,2},{3,19},{19,3},{4,20},{20... | collective-permute-start | bytes 1916936 | tf_op jit(solution)/shard_map/ppermute | solution.py:315
  307.8 24.5 %copy-start.6 = (f32[416,768]{1,0:T(8,128)S(1)}, f32[416,768]{1,0:T(8,128)}, u32[]{:S(2)}) copy-start(f32[416,768]{1,0:T(8,128)} %copy-done.5) | copy-start | bytes 3833860
  318.2 15.5 %copy-start.16 = (bf16[3072,384]{1,0:T(8,128)(2,1)}, bf16[3072,384]{1,0:T(8,128)(2,1)S(1)}, u32[]{:S(2)}) copy-start(bf16[3072,384]{1,0:T(8,128)(2,1)S(1)} %get-tuple-element.89) | copy-start | bytes 7077892
  318.3 14.0 %collective-permute-start.13 = (bf16[416,768]{1,0:T(8,128)(2,1)S(1)}, bf16[416,768]{1,0:T(8,128)(2,1)S(1)}, u32[]{:S(2)}, u32[]{:S(2)}) collective-permute-start(bf16[416,768]{1,0:T(8,128)(2,1)S(1)} %get-tuple-element.68.refs_0_), channel_id=1, source_target_pairs={{0,16},{16,0},{1,17},{17,1},{2,18},{18,2},{3,19},{19,3},{4,20},{20... | collective-permute-start | bytes 1916936 | tf_op jit(solution)/shard_map/ppermute | solution.py:315
  372.3 22.6 %all-to-all-start.7 = ((bf16[8,64,768]{2,1,0:T(8,128)(2,1)}), bf16[8,64,768]{2,1,0:T(8,128)(2,1)S(1)}, u32[]{:S(2)}, u32[]{:S(2)}) async-start(bf16[8,64,768]{2,1,0:T(8,128)(2,1)} %bitcast.119), calls=%async_computation.7 | async-start | bytes 1572864 | tf_op jit(solution)/shard_map/all_to_all | solution.py:343
  378.3 23.6 %collective-permute-start.18 = (bf16[1536,384]{1,0:T(8,128)(2,1)}, bf16[1536,384]{1,0:T(8,128)(2,1)}, u32[]{:S(2)}, u32[]{:S(2)}) collective-permute-start(bf16[1536,384]{1,0:T(8,128)(2,1)} %dynamic-slice_bitcast_fusion), channel_id=1, source_target_pairs={{0,1},{1,0},{2,3},{3,2},{4,5},{5,4},{6,7},{7,6},{8,9},{9,8},{10,11... | collective-permute-start | bytes 3538952 | tf_op jit(solution)/shard_map/ppermute | solution.py:315
  394.9 38.5 %all-to-all-start.3 = ((bf16[8,64,768]{2,1,0:T(8,128)(2,1)}), bf16[8,64,768]{2,1,0:T(8,128)(2,1)}, u32[]{:S(2)}, u32[]{:S(2)}) async-start(bf16[8,64,768]{2,1,0:T(8,128)(2,1)} %bitcast.118), calls=%async_computation.3 | async-start | bytes 1572864 | tf_op jit(solution)/shard_map/all_to_all | solution.py:343
  400.5 15.2 %copy-start.14 = (f32[416,768]{1,0:T(8,128)S(1)}, f32[416,768]{1,0:T(8,128)}, u32[]{:S(2)}) copy-start(f32[416,768]{1,0:T(8,128)} %copy-done.13) | copy-start | bytes 3833860
  400.5 15.2 %collective-permute-start.14 = (bf16[416,768]{1,0:T(8,128)(2,1)}, bf16[416,768]{1,0:T(8,128)(2,1)}, u32[]{:S(2)}, u32[]{:S(2)}) collective-permute-start(bf16[416,768]{1,0:T(8,128)(2,1)} %shard_map.167.own_ref), channel_id=1, source_target_pairs={{0,16},{16,0},{1,17},{17,1},{2,18},{18,2},{3,19},{19,3},{4,20},{20... | collective-permute-start | bytes 1916936 | tf_op jit(solution)/shard_map/ppermute | solution.py:315
  402.0 13.8 %copy-start.22 = (f32[416,768]{1,0:T(8,128)S(1)}, f32[416,768]{1,0:T(8,128)}, u32[]{:S(2)}) copy-start(f32[416,768]{1,0:T(8,128)} %copy-done.21) | copy-start | bytes 3833860
  402.0 13.8 %copy-start.24 = (bf16[3,416,384]{2,1,0:T(8,128)(2,1)S(1)}, bf16[3,416,384]{2,1,0:T(8,128)(2,1)}, u32[]{:S(2)}) copy-start(bf16[3,416,384]{2,1,0:T(8,128)(2,1)} %copy-done.23) | copy-start | bytes 2875396
  433.4 32.6 %all-to-all-start.10 = ((bf16[8,192,384]{2,1,0:T(8,128)(2,1)}), bf16[8,192,384]{2,1,0:T(8,128)(2,1)}, u32[]{:S(2)}, u32[]{:S(2)}) async-start(bf16[8,192,384]{2,1,0:T(8,128)(2,1)} %bitcast.115), calls=%async_computation.10 | async-start | bytes 2359296 | tf_op jit(solution)/shard_map/all_to_all | solution.py:516
  439.7 10.7 %collective-permute-start.16 = (bf16[1536,384]{1,0:T(8,128)(2,1)S(1)}, bf16[1536,384]{1,0:T(8,128)(2,1)S(1)}, u32[]{:S(2)}, u32[]{:S(2)}) collective-permute-start(bf16[1536,384]{1,0:T(8,128)(2,1)S(1)} %dynamic-slice_bitcast_fusion.1), channel_id=1, source_target_pairs={{0,1},{1,0},{2,3},{3,2},{4,5},{5,4},{6,7},{7,6},{8,9},{9,8},{10,11... | collective-permute-start | bytes 3538952 | tf_op jit(solution)/shard_map/ppermute | solution.py:315
  445.9 28.5 %collective-permute-start.26 = (bf16[3072,384]{1,0:T(8,128)(2,1)}, bf16[3072,384]{1,0:T(8,128)(2,1)}, u32[]{:S(2)}, u32[]{:S(2)}) collective-permute-start(bf16[3072,384]{1,0:T(8,128)(2,1)} %convolution_convert_fusion), channel_id=1, source_target_pairs={{0,1},{1,0},{2,3},{3,2},{4,5},{5,4},{6,7},{7,6},{8,9},{9,8},{10,11... | collective-permute-start | bytes 7077896 | tf_op jit(solution)/shard_map/ppermute | solution.py:315
  449.8 37.1 %collective-permute-start.22 = (bf16[384,3072]{1,0:T(8,128)(2,1)}, bf16[384,3072]{1,0:T(8,128)(2,1)}, u32[]{:S(2)}, u32[]{:S(2)}) collective-permute-start(bf16[384,3072]{1,0:T(8,128)(2,1)} %convolution_convert_fusion.2), channel_id=1, source_target_pairs={{0,1},{1,0},{2,3},{3,2},{4,5},{5,4},{6,7},{7,6},{8,9},{9,8},{10,11... | collective-permute-start | bytes 7077896 | tf_op jit(solution)/shard_map/ppermute | solution.py:315
  466.0 31.8 %all-to-all-start.8 = ((bf16[8,192,384]{2,1,0:T(8,128)(2,1)}), bf16[8,192,384]{2,1,0:T(8,128)(2,1)S(1)}, u32[]{:S(2)}, u32[]{:S(2)}) async-start(bf16[8,192,384]{2,1,0:T(8,128)(2,1)} %bitcast.114), calls=%async_computation.8 | async-start | bytes 2359296 | tf_op jit(solution)/shard_map/all_to_all | solution.py:516
  474.4 60.6 %collective-permute-start.20 = (bf16[384,3072]{1,0:T(8,128)(2,1)}, bf16[384,3072]{1,0:T(8,128)(2,1)}, u32[]{:S(2)}, u32[]{:S(2)}) collective-permute-start(bf16[384,3072]{1,0:T(8,128)(2,1)} %convolution_convert_fusion.3), channel_id=1, source_target_pairs={{0,1},{1,0},{2,3},{3,2},{4,5},{5,4},{6,7},{7,6},{8,9},{9,8},{10,11... | collective-permute-start | bytes 7077896 | tf_op jit(solution)/shard_map/ppermute | solution.py:315
  480.4 74.4 %collective-permute-start.24 = (bf16[3072,384]{1,0:T(8,128)(2,1)}, bf16[3072,384]{1,0:T(8,128)(2,1)}, u32[]{:S(2)}, u32[]{:S(2)}) collective-permute-start(bf16[3072,384]{1,0:T(8,128)(2,1)} %convolution_convert_fusion.1), channel_id=1, source_target_pairs={{0,1},{1,0},{2,3},{3,2},{4,5},{5,4},{6,7},{7,6},{8,9},{9,8},{10,11... | collective-permute-start | bytes 7077896 | tf_op jit(solution)/shard_map/ppermute | solution.py:315
  483.1 45.1 %collective-permute-start.27 = (bf16[1536,384]{1,0:T(8,128)(2,1)}, bf16[1536,384]{1,0:T(8,128)(2,1)}, u32[]{:S(2)}, u32[]{:S(2)}) collective-permute-start(bf16[1536,384]{1,0:T(8,128)(2,1)} %fusion.11), channel_id=1, source_target_pairs={{0,16},{16,0},{1,17},{17,1},{2,18},{18,2},{3,19},{19,3},{4,20},{20... | collective-permute-start | bytes 3538952 | tf_op jit(solution)/shard_map/ppermute | solution.py:315
  486.1 39.8 %collective-permute-start.11 = (bf16[416,768]{1,0:T(8,128)(2,1)S(1)}, bf16[416,768]{1,0:T(8,128)(2,1)}, u32[]{:S(2)}, u32[]{:S(2)}) collective-permute-start(bf16[416,768]{1,0:T(8,128)(2,1)S(1)} %shard_map.160), channel_id=1, source_target_pairs={{0,16},{16,0},{1,17},{17,1},{2,18},{18,2},{3,19},{19,3},{4,20},{20... | collective-permute-start | bytes 1916936 | tf_op jit(solution)/shard_map/ppermute | solution.py:315
  499.2 68.1 %all-to-all-start.11 = ((bf16[8,192,384]{2,1,0:T(8,128)(2,1)}), bf16[8,192,384]{2,1,0:T(8,128)(2,1)S(1)}, u32[]{:S(2)}, u32[]{:S(2)}) async-start(bf16[8,192,384]{2,1,0:T(8,128)(2,1)} %broadcast_in_dim.25), calls=%async_computation.11 | async-start | bytes 2359296 | tf_op jit(solution)/shard_map/all_to_all | solution.py:519
  503.0 22.9 %copy-start.12 = (f32[416,768]{1,0:T(8,128)S(1)}, f32[416,768]{1,0:T(8,128)}, u32[]{:S(2)}) copy-start(f32[416,768]{1,0:T(8,128)} %copy-done.10) | copy-start | bytes 3833860
  507.2 44.0 %collective-permute-start.23 = (bf16[384,1536]{1,0:T(8,128)(2,1)}, bf16[384,1536]{1,0:T(8,128)(2,1)}, u32[]{:S(2)}, u32[]{:S(2)}) collective-permute-start(bf16[384,1536]{1,0:T(8,128)(2,1)} %fusion.9), channel_id=1, source_target_pairs={{0,16},{16,0},{1,17},{17,1},{2,18},{18,2},{3,19},{19,3},{4,20},{20... | collective-permute-start | bytes 3538952 | tf_op jit(solution)/shard_map/ppermute | solution.py:315
  528.4 22.8 %slice-start = ((s8[4718592]{0:T(1024)(128)(4,1)}), s8[4194304]{0:T(1024)(128)(4,1)S(1)}, s32[]{:S(2)}) async-start(s8[4718592]{0:T(1024)(128)(4,1)} %bitcast.102), calls=%async_computation.12 | async-start | bytes 8388608
  533.5 17.6 %slice-start.1 = ((s8[4718592]{0:T(1024)(128)(4,1)}), s8[524288]{0:T(1024)(128)(4,1)S(1)}, s32[]{:S(2)}) async-start(s8[4718592]{0:T(1024)(128)(4,1)} %bitcast.102), calls=%async_computation.13 | async-start | bytes 1048576
  533.5 31.2 %collective-permute-start.15 = (bf16[416,768]{1,0:T(8,128)(2,1)S(1)}, bf16[416,768]{1,0:T(8,128)(2,1)S(1)}, u32[]{:S(2)}, u32[]{:S(2)}) collective-permute-start(bf16[416,768]{1,0:T(8,128)(2,1)S(1)} %copy-done.31), channel_id=1, source_target_pairs={{0,16},{16,0},{1,17},{17,1},{2,18},{18,2},{3,19},{19,3},{4,20},{20... | collective-permute-start | bytes 1916936 | tf_op jit(solution)/shard_map/ppermute | solution.py:315
  537.2 19.8 %copy-start.40 = (f32[384,3072]{1,0:T(8,128)}, f32[384,3072]{1,0:T(8,128)S(1)}, u32[]{:S(2)}) copy-start(f32[384,3072]{1,0:T(8,128)S(1)} %convert_element_type.126) | copy-start | bytes 14155780
  537.2 13.9 %copy-start.43 = (bf16[512,3072]{1,0:T(8,128)(2,1)S(1)}, bf16[512,3072]{1,0:T(8,128)(2,1)}, u32[]{:S(2)}) copy-start(bf16[512,3072]{1,0:T(8,128)(2,1)} %get-tuple-element.91) | copy-start | bytes 9437188
  539.2 111.9 %collective-permute-start.21 = (bf16[384,1536]{1,0:T(8,128)(2,1)}, bf16[384,1536]{1,0:T(8,128)(2,1)}, u32[]{:S(2)}, u32[]{:S(2)}) collective-permute-start(bf16[384,1536]{1,0:T(8,128)(2,1)} %fusion.8), channel_id=1, source_target_pairs={{0,16},{16,0},{1,17},{17,1},{2,18},{18,2},{3,19},{19,3},{4,20},{20... | collective-permute-start | bytes 3538952 | tf_op jit(solution)/shard_map/ppermute | solution.py:315
  560.5 96.8 %collective-permute-start.25 = (bf16[1536,384]{1,0:T(8,128)(2,1)}, bf16[1536,384]{1,0:T(8,128)(2,1)}, u32[]{:S(2)}, u32[]{:S(2)}) collective-permute-start(bf16[1536,384]{1,0:T(8,128)(2,1)} %fusion.10), channel_id=1, source_target_pairs={{0,16},{16,0},{1,17},{17,1},{2,18},{18,2},{3,19},{19,3},{4,20},{20... | collective-permute-start | bytes 3538952 | tf_op jit(solution)/shard_map/ppermute | solution.py:315
  565.8 8.6 %copy-start.65 = (f32[8,768]{1,0:T(8,128)S(1)}, f32[8,768]{1,0:T(8,128)}, u32[]{:S(2)}) copy-start(f32[8,768]{1,0:T(8,128)} %get-tuple-element.85) | copy-start | bytes 73732
  565.8 8.6 %copy-start.66 = (f32[8,768]{1,0:T(8,128)S(1)}, f32[8,768]{1,0:T(8,128)}, u32[]{:S(2)}) copy-start(f32[8,768]{1,0:T(8,128)} %get-tuple-element.82) | copy-start | bytes 73732
  567.3 7.2 %copy-start.54 = (bf16[8,192,384]{2,1,0:T(8,128)(2,1)}, bf16[8,192,384]{2,1,0:T(8,128)(2,1)S(1)}, u32[]{:S(2)}) copy-start(bf16[8,192,384]{2,1,0:T(8,128)(2,1)S(1)} %all-to-all-done.11) | copy-start | bytes 3538948
  568.5 95.0 %all-to-all-start.9 = ((bf16[8,192,384]{2,1,0:T(8,128)(2,1)}), bf16[8,192,384]{2,1,0:T(8,128)(2,1)}, u32[]{:S(2)}, u32[]{:S(2)}) async-start(bf16[8,192,384]{2,1,0:T(8,128)(2,1)} %broadcast_in_dim.24), calls=%async_computation.9 | async-start | bytes 2359296 | tf_op jit(solution)/shard_map/all_to_all | solution.py:519
  574.5 76.5 %copy-start.55 = (bf16[8,192,384]{2,1,0:T(8,128)(2,1)S(1)}, bf16[8,192,384]{2,1,0:T(8,128)(2,1)}, u32[]{:S(2)}) copy-start(bf16[8,192,384]{2,1,0:T(8,128)(2,1)} %copy-done.54) | copy-start | bytes 3538948
  651.1 12.7 %collective-permute-start.19 = (bf16[1536,384]{1,0:T(8,128)(2,1)S(1)}, bf16[1536,384]{1,0:T(8,128)(2,1)S(1)}, u32[]{:S(2)}, u32[]{:S(2)}) collective-permute-start(bf16[1536,384]{1,0:T(8,128)(2,1)S(1)} %bitcast.113), channel_id=1, source_target_pairs={{0,1},{1,0},{2,3},{3,2},{4,5},{5,4},{6,7},{7,6},{8,9},{9,8},{10,11... | collective-permute-start | bytes 3538952 | tf_op jit(solution)/shard_map/ppermute | solution.py:315
  663.4 3.1 collective-permute-start.17
  (44 other events, 124.2 us)

commit v2 on v1

v2 whole, which is shorter than its diff:
```python
import functools

import jax
import jax.numpy as jnp
from jax import lax
from jax.experimental import pallas as pl
from jax.experimental.pallas import tpu as pltpu
from jax.sharding import PartitionSpec as P

HEAD_DIM = 64
SEQ = 197
PAD = 208
PAIR = 2 * HEAD_DIM
EPSILON = 1e-06
GELU_A = 0.7978845608028654
GELU_B = 0.044715
F32 = jnp.float32
BF16 = jnp.bfloat16
NT = (((1,), (1,)), ((), ()))
TN = (((0,), (0,)), ((), ()))


def mm(a, b):
    return jnp.dot(a, b, preferred_element_type=F32)


def mm_nt(a, b):
    return lax.dot_general(a, b, NT, preferred_element_type=F32)


def mm_tn(a, b):
    return lax.dot_general(a, b, TN, preferred_element_type=F32)


def normalize(stream):
    shifted = stream - jnp.mean(stream, axis=-1, keepdims=True)
    scale = lax.rsqrt(jnp.mean(shifted * shifted, axis=-1, keepdims=True) + EPSILON)
    return shifted * scale, scale


def norm_back(stream, gain, out_grad):
    xhat, scale = normalize(stream)
    u = out_grad * gain
    mean_u = jnp.mean(u, axis=-1, keepdims=True)
    mean_ux = jnp.mean(u * xhat, axis=-1, keepdims=True)
    return scale * (u - mean_u - xhat * mean_ux), jnp.sum(out_grad * xhat, axis=0, keepdims=True)


def both(own_ref, got_ref):
    return own_ref[...].astype(F32) + got_ref[...].astype(F32)


VMEM_SPEC = pl.BlockSpec(memory_space=pltpu.VMEM)
SMEM_SPEC = pl.BlockSpec(memory_space=pltpu.SMEM)
ANY_SPEC = pl.BlockSpec(memory_space=pl.ANY)


def call(body, outs, args, specs, scratch=(), flops=0, limit=40, deps=(), grid=(1,), alias=None):
    out_specs = [o[2] if len(o) > 2 else VMEM_SPEC for o in outs]
    outs = [jax.ShapeDtypeStruct(o[0], o[1]) for o in outs]
    size = sum(o.size * o.dtype.itemsize for o in outs)
    size += sum(a.size * a.dtype.itemsize for a in args)
    taken, last = len(args), len(args) + len(deps)

    def kernel(*refs):
        body(*refs[:taken], *refs[last:])

    return pl.pallas_call(
        kernel,
        grid=grid,
        out_shape=outs,
        in_specs=[*specs, *([ANY_SPEC] * len(deps))],
        out_specs=out_specs,
        scratch_shapes=list(scratch),
        input_output_aliases=alias or {},
        compiler_params=pltpu.CompilerParams(vmem_limit_bytes=limit << 20),
        cost_estimate=pl.CostEstimate(flops=flops, bytes_accessed=size, transcendentals=0),
    )(*args, *deps)


def layer_spec(shape, layer):
    return pl.BlockSpec(shape, lambda step: (layer,) + (0,) * (len(shape) - 1))


def place_kernel(slot_half, where_ref, routes_ref, rows_ref, place_ref, send_ref):
    layers, _, rows = routes_ref.shape
    experts = place_ref.shape[1] // slot_half
    first = where_ref[0] * slot_half
    before_of = lax.broadcasted_iota(jnp.int32, (rows, rows), 0) < lax.broadcasted_iota(
        jnp.int32, (rows, rows), 1
    )
    earlier = jnp.where(before_of, 1.0, 0.0).astype(BF16)
    labels = lax.broadcasted_iota(jnp.int32, (experts, rows), 0)
    slots = lax.broadcasted_iota(jnp.int32, (slot_half, rows), 0)
    for layer in range(layers):
        named = (labels == routes_ref[layer, 0:1, :]) | (labels == routes_ref[layer, 1:2, :])
        count = mm(jnp.where(named, 1.0, 0.0).astype(BF16), earlier)
        slot = jnp.where(named, count.astype(jnp.int32) - first, -1)
        for e in range(experts):
            hit = slots == slot[e : e + 1, :]
            place_ref[layer, e * slot_half : (e + 1) * slot_half, :] = jnp.where(
                hit, 1.0, 0.0
            ).astype(BF16)
    send_ref[...] = mm(place_ref[layers - 1], rows_ref[...]).astype(BF16)


def piece_of(matrix_in, matrix_out, layer, core):
    if matrix_in is not None:
        part = matrix_in.shape[3] // 2
        return matrix_in.at[layer, 0, :, pl.ds(pl.multiple_of(core * part, part), part)]
    part = matrix_out.shape[2] // 2
    return matrix_out.at[layer, 0, pl.ds(pl.multiple_of(core * part, part), part), :]


def fetch_kernel(layer, where_ref, source_ref, piece_ref, sem):
    copy = pltpu.make_async_copy(
        piece_of(source_ref, None, layer, where_ref[2]), piece_ref, sem.at[0]
    )
    copy.start()
    copy.wait()


def unpack_kernel(place_ref, got_ref, out_ref):
    out_ref[...] = mm_tn(place_ref[0], got_ref[...]).astype(BF16)


def unpack_pass_kernel(place_ref, got_ref, reply_ref, out_ref, passed_ref, sem):
    copy = pltpu.make_async_copy(reply_ref, passed_ref, sem.at[0])
    copy.start()
    out_ref[...] = mm_tn(place_ref[0], got_ref[...]).astype(BF16)
    copy.wait()


def pair_masks():
    lane = lax.broadcasted_iota(jnp.int32, (PAD, PAIR), 1)
    return lane < HEAD_DIM


def softmax_rows(q, k):
    scores = mm_nt(q, k) * HEAD_DIM ** (-0.5)
    column = lax.broadcasted_iota(jnp.int32, scores.shape, 1)
    scores = jnp.where(column < SEQ, scores, -1e30)
    top = jnp.max(scores, axis=-1, keepdims=True)
    weights = jnp.exp(scores - top)
    return weights / jnp.sum(weights, axis=-1, keepdims=True)


def attend_kernel(first, *refs):
    if first:
        tokens_ref, gain_ref, qkv_ref, wo_ref, h_ref, a_ref, proj_ref, mixed_ref, out_ref = refs
        h = tokens_ref[...].astype(F32)
    else:
        mid_ref, own_ref, got_ref, gain_ref, qkv_ref, wo_ref = refs[:6]
        h_ref, a_ref, proj_ref, mixed_ref, out_ref = refs[6:]
        h = mid_ref[...] + both(own_ref, got_ref)
    h_ref[...] = h
    a = (normalize(h)[0] * gain_ref[0, 0:1, :]).astype(BF16)
    a_ref[...] = a
    for c in range(3):
        proj_ref[c] = mm(a, qkv_ref[0, c]).astype(BF16)
    low = pair_masks()
    zero = jnp.zeros((PAD, PAIR), BF16)
    for image in range(a.shape[0] // PAD):
        rows = slice(image * PAD, (image + 1) * PAD)
        for pair in range(proj_ref.shape[2] // PAIR):
            lanes = slice(pair * PAIR, (pair + 1) * PAIR)
            q, k, v = (proj_ref[c, rows, lanes] for c in range(3))
            p0 = softmax_rows(jnp.where(low, q, zero), k).astype(BF16)
            p1 = softmax_rows(jnp.where(low, zero, q), k).astype(BF16)
            mixed_ref[rows, lanes] = jnp.where(low, mm(p0, v), mm(p1, v)).astype(BF16)
    out_ref[...] = mm(mixed_ref[...], wo_ref[0]).astype(BF16)


def route_kernel(
    layer, where_ref, h_ref, own_ref, got_ref, gain_ref, place_ref, source_ref, mid_ref, send_ref, piece_ref, sem
):
    copy = pltpu.make_async_copy(
        piece_of(None, source_ref, layer, where_ref[2]), piece_ref, sem.at[0]
    )
    copy.start()
    mid = h_ref[...] + both(own_ref, got_ref)
    mid_ref[...] = mid
    z = (normalize(mid)[0] * gain_ref[0, 1:2, :]).astype(BF16)
    send_ref[...] = mm(place_ref[0], z).astype(BF16)
    copy.wait()


def load_weights(layer, core, sources, win, wout, sems, in_first):
    win_own, win_a, win_b, wout_own, wout_a, wout_b = sources
    part = win.shape[2]
    groups = []
    for c in range(2):
        groups.append(
            [
                (win_own.at[layer, 0, :, pl.ds(c * part, part)], win.at[c], 2 * c),
                (wout_own.at[layer, 0, pl.ds(c * part, part), :], wout.at[c], 2 * c + 1),
            ]
        )
    groups.append(
        [
            (win_a, win.at[2 + core], 4),
            (wout_a, wout.at[2 + core], 5),
            (win_b, win.at[3 - core], 6),
            (wout_b, wout.at[3 - core], 7),
        ]
    )
    groups = [[pltpu.make_async_copy(s, d, sems.at[i]) for s, d, i in group] for group in groups]

    @pl.when(pl.program_id(0) == 0)
    def _():
        for group in groups:
            for copy in group:
                copy.start()

    for step, group in enumerate(groups):

        @pl.when(pl.program_id(0) == step)
        def _(group=group):
            for copy in group:
                copy.wait()


def gate_of(x, router, expert):
    logits = mm_nt(x, router)
    gate = jnp.exp(logits - jnp.max(logits, axis=-1, keepdims=True))
    gate = gate / jnp.sum(gate, axis=-1, keepdims=True)
    mine = lax.broadcasted_iota(jnp.int32, gate.shape, 1) == expert
    return gate, mine, jnp.sum(jnp.where(mine, gate, 0.0), axis=-1, keepdims=True)


def bend(pre):
    square = pre * pre
    bent = jnp.tanh(pre * (GELU_A + (GELU_A * GELU_B) * square))
    half = 0.5 + 0.5 * bent
    slope = half + pre * (1.0 - bent * bent) * (0.5 * GELU_A + (1.5 * GELU_A * GELU_B) * square)
    return pre * half, slope


def add_step(total, term):
    @pl.when(pl.program_id(0) == 0)
    def _():
        total[...] = term

    @pl.when(pl.program_id(0) > 0)
    def _():
        total[...] += term


def expert_kernel(
    layer, where_ref, x_ref, router_ref, win_own, win_a, win_b, wout_own, wout_a, wout_b,
    out_ref, act_ref, slope_ref, win, wout, total, sems,
):
    step = pl.program_id(0)
    sources = (win_own, win_a, win_b, wout_own, wout_a, wout_b)
    load_weights(layer, where_ref[2], sources, win, wout, sems, True)
    act, slope = bend(mm(x_ref[...], win[step]))
    act = act.astype(BF16)
    act_ref[...] = act
    slope_ref[...] = slope.astype(BF16)
    add_step(total, mm(act, wout[step]))

    @pl.when(step == pl.num_programs(0) - 1)
    def _():
        _, _, share = gate_of(x_ref[...], router_ref[...], where_ref[1])
        out_ref[...] = (share * total[...]).astype(BF16)


def finish_back(x_ref, router_ref, gate, mine, share, dot, total, out_ref, router_grad_ref):
    logit_grad = (dot * share * (jnp.where(mine, 1.0, 0.0) - gate)).astype(BF16)
    router_grad_ref[...] = mm_tn(logit_grad, x_ref[...])
    out_ref[...] = (total + mm(logit_grad, router_ref[...])).astype(BF16)


def expert_back_kernel(
    layer, where_ref, g_ref, x_ref, act_ref, slope_ref, router_ref,
    win_own, win_a, win_b, wout_own, wout_a, wout_b,
    out_ref, pre_grad_ref, scaled_ref, router_grad_ref, win, wout, total, dot_ref, sems,
):
    step = pl.program_id(0)
    sources = (win_own, win_a, win_b, wout_own, wout_a, wout_b)
    load_weights(layer, where_ref[2], sources, win, wout, sems, False)
    g = g_ref[...]
    gate, mine, share = gate_of(x_ref[...], router_ref[...], where_ref[1])
    u = mm_nt(g, wout[step])
    pre_grad = (share * u * slope_ref[...].astype(F32)).astype(BF16)
    pre_grad_ref[...] = pre_grad
    add_step(total, mm_nt(pre_grad, win[step]))
    add_step(dot_ref, jnp.sum(u * act_ref[...].astype(F32), axis=-1, keepdims=True))

    @pl.when(step == pl.num_programs(0) - 1)
    def _():
        scaled_ref[...] = (share * g.astype(F32)).astype(BF16)
        finish_back(
            x_ref, router_ref, gate, mine, share, dot_ref[...], total[...], out_ref, router_grad_ref
        )


def expert_both_kernel(
    layer, where_ref, g_ref, x_ref, router_ref,
    win_own, win_a, win_b, wout_own, wout_a, wout_b,
    out_ref, back_ref, act_ref, pre_grad_ref, scaled_ref, router_grad_ref,
    win, wout, total, back_total, dot_ref, sems,
):
    step = pl.program_id(0)
    sources = (win_own, win_a, win_b, wout_own, wout_a, wout_b)
    load_weights(layer, where_ref[2], sources, win, wout, sems, True)
    g = g_ref[...]
    gate, mine, share = gate_of(x_ref[...], router_ref[...], where_ref[1])
    act, slope = bend(mm(x_ref[...], win[step]))
    u = mm_nt(g, wout[step])
    act = act.astype(BF16)
    act_ref[...] = act
    pre_grad = (share * u * slope).astype(BF16)
    pre_grad_ref[...] = pre_grad
    add_step(total, mm(act, wout[step]))
    add_step(back_total, mm_nt(pre_grad, win[step]))
    add_step(dot_ref, jnp.sum(u * act.astype(F32), axis=-1, keepdims=True))

    @pl.when(step == pl.num_programs(0) - 1)
    def _():
        out_ref[...] = (share * total[...]).astype(BF16)
        scaled_ref[...] = (share * g.astype(F32)).astype(BF16)
        finish_back(
            x_ref, router_ref, gate, mine, share, dot_ref[...], back_total[...], back_ref, router_grad_ref
        )


def half_of(ref, which):
    half = ref.shape[1] // 2
    return ref[:, pl.ds(pl.multiple_of(which * half, half), half)]


def grad_other_kernel(where_ref, x_ref, scaled_ref, pre_grad_ref, act_ref, in_ref, out_ref):
    other = 1 - where_ref[2]
    in_ref[...] = mm_tn(half_of(x_ref, other), pre_grad_ref[...]).astype(BF16)
    out_ref[...] = mm_tn(act_ref[...], half_of(scaled_ref, other)).astype(BF16)


def grad_far_kernel(
    where_ref, x_ref, scaled_ref, pre_grad_ref, act_ref, in_got_ref, out_got_ref, in_ref, out_ref
):
    core = where_ref[2]
    term = mm_tn(half_of(x_ref, core), pre_grad_ref[...])
    in_ref[...] = (term + in_got_ref[...].astype(F32)).astype(BF16)
    term = mm_tn(act_ref[...], half_of(scaled_ref, core))
    out_ref[...] = (term + out_got_ref[...].astype(F32)).astype(BF16)


def grad_own_kernel(
    where_ref, x_ref, scaled_ref, pre_grad_ref, act_ref, in_got_ref, out_got_ref, in_far_ref, out_far_ref, *refs
):
    core = where_ref[2]
    in_ref, out_ref = refs[-2:]
    term = mm_tn(half_of(x_ref, core), pre_grad_ref[...])
    in_ref[0] = term + in_got_ref[...].astype(F32) + in_far_ref[...].astype(F32)
    term = mm_tn(act_ref[...], half_of(scaled_ref, core))
    out_ref[0] = term + out_got_ref[...].astype(F32) + out_far_ref[...].astype(F32)


def attend_back_kernel(
    where_ref, own_ref, got_ref, mid_ref, gain_ref, g_ref, a_ref, proj_ref, mixed_ref, qkv_ref, wo_ref,
    g_out_ref, gain_grad_ref, out_ref, *refs,
):
    back_ref, mixed_grad_ref = refs[-2:]
    h_grad, gain_grad_ref[...] = norm_back(
        mid_ref[...], gain_ref[0, 1:2, :], both(own_ref, got_ref)
    )
    g = g_ref[...].astype(F32) + h_grad
    g_out_ref[...] = g
    out_grad = g.astype(BF16)
    width = proj_ref.shape[2]
    depth = a_ref.shape[1]
    mixed_grad_ref[...] = mm_nt(out_grad, wo_ref[0]).astype(BF16)
    low = pair_masks()
    zero = jnp.zeros((PAD, PAIR), BF16)
    for image in range(g.shape[0] // PAD):
        rows = slice(image * PAD, (image + 1) * PAD)
        for pair in range(width // PAIR):
            lanes = slice(pair * PAIR, (pair + 1) * PAIR)
            q, k, v = (proj_ref[c, rows, lanes] for c in range(3))
            dm = mixed_grad_ref[rows, lanes]
            parts = []
            for side in range(2):
                def pick(t, side=side):
                    return jnp.where(low, t, zero) if side == 0 else jnp.where(low, zero, t)

                probs = softmax_rows(pick(q), k)
                prob_grad = mm_nt(pick(dm), v)
                row = jnp.sum(prob_grad * probs, axis=-1, keepdims=True)
                score_grad = (probs * (prob_grad - row)).astype(BF16)
                parts.append(
                    (
                        mm(score_grad, k) * HEAD_DIM ** (-0.5),
                        mm_tn(score_grad, q) * HEAD_DIM ** (-0.5),
                        mm_tn(probs.astype(BF16), dm),
                    )
                )
            for c in range(3):
                back_ref[c, rows, lanes] = jnp.where(low, parts[0][c], parts[1][c]).astype(BF16)
    total = mm_nt(back_ref[0], qkv_ref[0, 0])
    total += mm_nt(back_ref[1], qkv_ref[0, 1])
    total += mm_nt(back_ref[2], qkv_ref[0, 2])
    out_ref[...] = total.astype(BF16)
    core = where_ref[2]

    def put(block, start, value):
        @pl.when(core == block // 2)
        def _():
            refs[0][start : start + value.shape[0], :] = value.astype(BF16)

        @pl.when(core != block // 2)
        def _():
            refs[1][start : start + value.shape[0], :] = value.astype(BF16)

    for c in range(3):
        put(c, c % 2 * depth, mm_tn(a_ref[...], back_ref[c]))
    proj_grad = mm_tn(mixed_ref[...], out_grad)
    for c in range(depth // width):
        put(3, depth + c * width, proj_grad[:, c * width : (c + 1) * width])


def stream_back_kernel(pack, *refs):
    if pack:
        own_ref, got_ref, h_ref, gain_ref, g_ref, place_ref, g_out_ref, gain_grad_ref, send_ref = refs
    else:
        own_ref, got_ref, h_ref, gain_ref, g_ref, g_out_ref, gain_grad_ref = refs
    h_grad, gain_grad_ref[...] = norm_back(h_ref[...], gain_ref[0, 0:1, :], both(own_ref, got_ref))
    g = g_ref[...] + h_grad
    g_out_ref[...] = g
    if pack:
        send_ref[...] = mm(place_ref[0], g.astype(BF16)).astype(BF16)


def swap(value, axis):
    return lax.ppermute(value, axis, [(0, 1), (1, 0)])


def partner(value, axis, bit):
    count = lax.axis_size(axis)
    return lax.ppermute(value, axis, [(i, i ^ (1 << bit)) for i in range(count)])


def split_kernel(sides_ref, keep_a_ref, got_a_ref, keep_b_ref, got_b_ref, *outs):
    for i, (keep_ref, got_ref) in enumerate(((keep_a_ref, got_a_ref), (keep_b_ref, got_b_ref))):
        out_ref, send_ref = outs[2 * i], outs[2 * i + 1]
        half = out_ref.shape[0]
        side = sides_ref[i]
        mine, other = pl.ds(side * half, half), pl.ds((1 - side) * half, half)
        out_ref[...] = keep_ref[mine].astype(F32) + got_ref[mine].astype(F32)
        send_ref[...] = (keep_ref[other].astype(F32) + got_ref[other].astype(F32)).astype(BF16)


def last_sum_kernel(keep_a_ref, got_a_ref, keep_b_ref, got_b_ref, a_ref, b_ref):
    a_ref[...] = both(keep_a_ref, got_a_ref).astype(BF16)
    b_ref[...] = both(keep_b_ref, got_b_ref).astype(BF16)


def join_kernel(sides_ref, own_a_ref, got_a_ref, own_b_ref, got_b_ref, a_ref, b_ref):
    pairs = ((own_a_ref, got_a_ref, a_ref), (own_b_ref, got_b_ref, b_ref))
    for i, (own_ref, got_ref, out_ref) in enumerate(pairs):
        half = own_ref.shape[0]
        side = sides_ref[i]
        out_ref[pl.ds(side * half, half)] = own_ref[...]
        out_ref[pl.ds((1 - side) * half, half)] = got_ref[...]


class ExpertSum:
    def __init__(self, mine, got, experts):
        rows, width = mine.shape
        block = rows // (2 * experts)
        mine, got = (v.reshape(2, experts, block, width) for v in (mine, got))
        bits = list(range(experts.bit_length() - 1))
        self.orders = list(zip(bits, [*bits[1::-1], *bits[2:]]))
        me = lax.axis_index("expert")
        self.sides = [jnp.stack([(me >> a) & 1, (me >> b) & 1]).astype(jnp.int32) for a, b in self.orders]
        self.state = (mine[0], got[0], mine[1], got[1])
        self.count, self.block, self.width = experts, block, width
        self.step = 0

    def shape(self):
        return (self.count, self.block, self.width)

    def split(self, deps=()):
        self.count //= 2
        a, b = self.orders[self.step]
        keep_a, send_a, keep_b, send_b = call(
            split_kernel,
            [(self.shape(), F32), (self.shape(), BF16)] * 2,
            (self.sides[self.step], *self.state),
            [SMEM_SPEC] + [VMEM_SPEC] * 4,
            deps=deps,
        )
        self.step += 1
        self.state = (keep_a, partner(send_a, "expert", a), keep_b, partner(send_b, "expert", b))
        return send_a

    def finish(self, deps=()):
        while self.step < len(self.orders):
            self.split()
        self.state = call(
            last_sum_kernel, [(self.shape(), BF16)] * 2, self.state, [VMEM_SPEC] * 4, deps=deps
        )
        return self.state[0]

    def join(self, deps=()):
        self.step -= 1
        own_a, own_b = self.state
        a, b = self.orders[self.step]
        got_a, got_b = partner(own_a, "expert", a), partner(own_b, "expert", b)
        self.count *= 2
        self.state = call(
            join_kernel,
            [(self.shape(), BF16)] * 2,
            (self.sides[self.step], own_a, got_a, own_b, got_b),
            [SMEM_SPEC] + [VMEM_SPEC] * 4,
            deps=deps,
        )
        return self.state[0]

    def result(self):
        while self.step:
            self.join()
        return jnp.concatenate(self.state).reshape(-1, self.width)


def sum_all(value):
    for bit in range(lax.axis_size("expert").bit_length() - 1):
        value = value + partner(value, "expert", bit)
    value = value + swap(value, "replica")
    return value + swap(value, "tensor")


def on_device(tokens, gains, attn_qkv, attn_out, router, expert_in, expert_out, routes, cotangent):
    row_count, width = tokens.shape
    layers = attn_qkv.shape[0]
    local = attn_qkv.shape[3]
    images = row_count // SEQ
    rows = images * PAD
    experts = router.shape[2]
    hidden = expert_in.shape[3]
    part = hidden // 2
    half = width // 2
    capacity = 8 * (5 * row_count // (16 * experts) + 1)
    slot_half = capacity // 2
    slots = experts * slot_half
    side = lax.axis_index("tensor")
    core = lax.axis_index("replica")
    where = jnp.stack([side, lax.axis_index("expert"), core]).astype(jnp.int32)
    last = layers - 1

    def spread(array):
        array = array.reshape(images, SEQ, width)
        return jnp.pad(array, ((0, 0), (0, PAD - SEQ), (0, 0))).reshape(rows, width)

    def gathered(array):
        return array.reshape(images, PAD, width)[:, :SEQ].reshape(row_count, width)

    def exchange(block):
        block = block.reshape(experts, slot_half, width)
        return lax.all_to_all(block, "expert", 0, 0, tiled=True).reshape(slots, width)

    def fetch(layer, deps=()):
        [piece] = call(
            functools.partial(fetch_kernel, layer),
            [((width, part), BF16, ANY_SPEC)],
            (where, expert_in),
            [SMEM_SPEC, ANY_SPEC],
            [pltpu.SemaphoreType.DMA((1,))],
            deps=deps,
        )
        return piece, pair_of(piece)

    def pair_of(piece):
        got = swap(piece, "tensor")
        return got, swap(got, "replica")

    def place_spec(layer):
        return layer_spec((1, slots, rows), layer)

    def gain_spec(layer):
        return layer_spec((1, 2, width), layer)

    def columns(size, shift=0):
        return pl.BlockSpec(size, lambda step: (0, step + shift))

    def lines(size, shift=0):
        return pl.BlockSpec(size, lambda step: (step + shift, 0))

    pack_flops = 2 * slots * rows * width
    weights = [pltpu.VMEM((4, width, part), BF16), pltpu.VMEM((4, part, width), BF16)]
    total = pltpu.VMEM((slots, width), F32)
    dots = pltpu.VMEM((slots, 1), F32)
    sems = pltpu.SemaphoreType.DMA((8,))
    expert_flops = 8 * slots * width * hidden
    rows_out = ((slots, width), BF16)
    hidden_spec = columns((slots, part))
    hidden_out = ((slots, 2 * hidden), BF16, hidden_spec)

    _, whole_in = fetch(0)
    attend_deps = ()
    router_t = jnp.swapaxes(router, 1, 2)
    routes_t = jnp.swapaxes(routes, 1, 2).reshape(layers, 2, images, SEQ)
    routes_t = jnp.pad(
        routes_t, ((0, 0), (0, 0), (0, 0), (0, PAD - SEQ)), constant_values=-1
    ).reshape(layers, 2, rows)
    upstream = spread(cotangent)
    stream_args = (spread(tokens),)
    place = None
    saved = []
    for layer in range(layers):
        h, a, proj, mixed, term = call(
            functools.partial(attend_kernel, layer == 0),
            [
                ((rows, width), F32),
                ((rows, width), BF16),
                ((3, rows, local), BF16),
                ((rows, local), BF16),
                ((rows, width), BF16),
            ],
            (*stream_args, gains, attn_qkv, attn_out),
            [
                *([VMEM_SPEC] * len(stream_args)),
                gain_spec(layer),
                layer_spec((1, 3, width, local), layer),
                layer_spec((1, local, width), layer),
            ],
            flops=8 * rows * width * local + 4 * rows * PAD * local,
            deps=attend_deps,
        )
        if place is None:
            place, send = call(
                functools.partial(place_kernel, slot_half),
                [((layers, slots, rows), BF16), rows_out],
                (where, routes_t, upstream),
                [SMEM_SPEC, VMEM_SPEC, VMEM_SPEC],
                flops=2 * layers * rows * rows * experts + pack_flops,
                deps=(term,),
            )
            received_grad = exchange(send)
        mid, send, piece = call(
            functools.partial(route_kernel, layer),
            [((rows, width), F32), rows_out, ((part, width), BF16, ANY_SPEC)],
            (where, h, term, swap(term, "tensor"), gains, place, expert_out),
            [SMEM_SPEC] + [VMEM_SPEC] * 3 + [gain_spec(layer), place_spec(layer), ANY_SPEC],
            [pltpu.SemaphoreType.DMA((1,))],
            flops=pack_flops,
        )
        whole = (expert_in, *whole_in, expert_out, *pair_of(piece))
        received = exchange(send)
        if layer < last:
            piece, whole_in = fetch(layer + 1, (received,))
            attend_deps = (whole_in[0],)
            reply, act, slope = call(
                functools.partial(expert_kernel, layer),
                [rows_out, hidden_out, hidden_out],
                (where, received, router_t[layer], *whole),
                [SMEM_SPEC, VMEM_SPEC, VMEM_SPEC] + [ANY_SPEC] * 6,
                [*weights, total, sems],
                flops=expert_flops,
                limit=56,
                deps=(piece,),
                grid=(4,),
            )
            returned = exchange(reply)
            [term] = call(
                unpack_kernel,
                [((rows, width), BF16)],
                (place, returned),
                [place_spec(layer), VMEM_SPEC],
                flops=pack_flops,
            )
            stream_args = (mid, term, swap(term, "tensor"))
            saved.append((h, a, proj, mixed, mid, received, act, slope, whole))
        else:
            saved.append((h, a, proj, mixed, mid, received, None, None, whole))

    small = [None] * layers
    sums = [None] * layers
    grad_in = grad_out = mixed_out = None
    finishers = []
    for layer in reversed(range(layers)):
        h, a, proj, mixed, mid, received, act, slope, whole = saved[layer]
        back_outs = [hidden_out, rows_out, ((experts, width), F32)]
        if layer == last:
            reply, back, act, pre_grad, scaled, router_grad = call(
                functools.partial(expert_both_kernel, layer),
                [rows_out, rows_out, hidden_out, *back_outs],
                (where, received_grad, received, router_t[layer], *whole),
                [SMEM_SPEC] + [VMEM_SPEC] * 3 + [ANY_SPEC] * 6,
                [*weights, total, total, dots, sems],
                flops=2 * expert_flops,
                limit=56,
                grid=(4,),
            )
        else:
            back, pre_grad, scaled, router_grad = call(
                functools.partial(expert_back_kernel, layer),
                [rows_out, *back_outs],
                (where, received_grad, received, act, slope, router_t[layer], *whole),
                [SMEM_SPEC, VMEM_SPEC, VMEM_SPEC, hidden_spec, hidden_spec, VMEM_SPEC] + [ANY_SPEC] * 6,
                [*weights, total, dots, sems],
                flops=expert_flops,
                limit=56,
                deps=(far[0], sums[last].split()),
                grid=(4,),
            )
        returned = exchange(back)
        if layer == last:
            term, reply = call(
                unpack_pass_kernel,
                [((rows, width), BF16), (*rows_out, ANY_SPEC)],
                (place, returned, reply),
                [place_spec(layer), VMEM_SPEC, ANY_SPEC],
                [pltpu.SemaphoreType.DMA((1,))],
                flops=pack_flops,
            )
        else:
            [term] = call(
                unpack_kernel,
                [((rows, width), BF16)],
                (place, returned),
                [place_spec(layer), VMEM_SPEC],
                flops=pack_flops,
                deps=(far[1], sums[last].split()),
            )
        got = swap(term, "tensor")
        in_other, out_other = call(
            grad_other_kernel,
            [
                ((half, 2 * hidden), BF16, columns((half, part))),
                ((2 * hidden, half), BF16, lines((part, half))),
            ],
            (where, received, scaled, pre_grad, act),
            [SMEM_SPEC, VMEM_SPEC, VMEM_SPEC, hidden_spec, hidden_spec],
            flops=4 * slots * hidden * width,
            deps=(term,),
            grid=(4,),
        )
        in_got, out_got = swap(in_other, "replica"), swap(out_other, "replica")
        upstream, gain_two, term, *weight_grads = call(
            attend_back_kernel,
            [
                ((rows, width), F32),
                ((1, width), F32),
                ((rows, width), BF16),
                *[((2 * width, local), BF16)] * 2,
            ],
            (where, term, got, mid, gains, upstream, a, proj, mixed, attn_qkv, attn_out),
            [SMEM_SPEC]
            + [VMEM_SPEC] * 3
            + [gain_spec(layer)]
            + [VMEM_SPEC] * 4
            + [layer_spec((1, 3, width, local), layer), layer_spec((1, local, width), layer)],
            [pltpu.VMEM((3, rows, local), BF16), pltpu.VMEM((rows, local), BF16)],
            flops=16 * rows * width * local + 10 * rows * PAD * local,
            deps=(in_other, out_other) if layer == last else (in_other, out_other, sums[last].finish()),
        )
        if layer == last:
            [done] = call(
                unpack_kernel,
                [((rows, width), BF16)],
                (place, exchange(reply)),
                [place_spec(layer), VMEM_SPEC],
                flops=pack_flops,
            )
            done = done.astype(F32) + swap(done, "tensor").astype(F32)
            mixed_out = gathered((mid + done).astype(BF16))

        mine, other = weight_grads
        sums[layer] = ExpertSum(mine, swap(other, "replica"), experts)
        got = swap(term, "tensor")
        in_far, out_far = call(
            grad_far_kernel,
            [
                ((half, hidden), BF16, columns((half, part))),
                ((hidden, half), BF16, lines((part, half))),
            ],
            (where, received, scaled, pre_grad, act, in_got, out_got),
            [
                SMEM_SPEC,
                VMEM_SPEC,
                VMEM_SPEC,
                columns((slots, part), 2),
                columns((slots, part), 2),
                columns((half, part), 2),
                lines((part, half), 2),
            ],
            flops=2 * slots * hidden * width,
            deps=(term,),
            grid=(2,),
        )
        if layer > 0:
            upstream, gain_one, send = call(
                functools.partial(stream_back_kernel, True),
                [((rows, width), F32), ((1, width), F32), rows_out],
                (term, got, h, gains, upstream, place),
                [VMEM_SPEC] * 3 + [gain_spec(layer), VMEM_SPEC, place_spec(layer - 1)],
                flops=pack_flops,
                deps=(in_far, out_far, sums[last].split()),
            )
            received_grad = exchange(send)
        else:
            upstream, gain_one = call(
                functools.partial(stream_back_kernel, False),
                [((rows, width), F32), ((1, width), F32)],
                (term, got, h, gains, upstream),
                [VMEM_SPEC] * 3 + [gain_spec(layer), VMEM_SPEC],
                deps=(in_far, out_far, sums[last].join()),
            )
        in_far, out_far = far = swap(in_far, "tensor"), swap(out_far, "tensor")
        gain_pair = jnp.where(side == 0, jnp.concatenate([gain_one, gain_two]), 0.0)
        small[layer] = jnp.concatenate([router_grad, gain_pair])

        def finish_own(deps, layer=layer, args=(where, received, scaled, pre_grad, act, in_got, out_got, in_far, out_far)):
            nonlocal grad_in, grad_out
            stacked = () if grad_in is None else (grad_in, grad_out)
            grad_in, grad_out = call(
                grad_own_kernel,
                [
                    (
                        (layers, half, hidden),
                        F32,
                        pl.BlockSpec((1, half, part), lambda step: (layer, 0, step)),
                    ),
                    (
                        (layers, hidden, half),
                        F32,
                        pl.BlockSpec((1, part, half), lambda step: (layer, step, 0)),
                    ),
                ],
                (*args, *stacked),
                [
                    SMEM_SPEC,
                    VMEM_SPEC,
                    VMEM_SPEC,
                    hidden_spec,
                    hidden_spec,
                    columns((half, part)),
                    lines((part, half)),
                    columns((half, part)),
                    lines((part, half)),
                    *([ANY_SPEC] * len(stacked)),
                ],
                flops=2 * slots * hidden * width,
                deps=deps,
                grid=(2,),
                alias={9: 0, 10: 1} if stacked else None,
            )

        finishers.append(finish_own)

    finishers[0]((term,))
    finishers[1]((upstream,))

    grad_qkv, grad_proj = [], []
    for layer in range(layers):
        if layer < last:
            sums[layer].finish(far[:1])
            sums[layer].join(far[1:])
        mine = sums[layer].result()
        got = swap(mine, "replica")
        lower = jnp.where(core == 0, mine, got).astype(F32)
        upper = jnp.where(core == 0, got, mine).astype(F32)
        grad_qkv.append(jnp.concatenate([lower, upper[:width]]).reshape(3, width, local))
        grad_proj.append(
            jnp.concatenate([upper[width : width + local], upper[width + local :]], axis=1)
        )
    small = sum_all(jnp.stack(small))
    return (
        mixed_out,
        gathered(upstream),
        small[:, experts:],
        jnp.stack(grad_qkv),
        jnp.stack(grad_proj),
        jnp.swapaxes(small[:, :experts], 1, 2),
        grad_in[:, None],
        grad_out[:, None],
    )


def solution(mesh):
    return jax.shard_map(
        on_device,
        mesh=mesh,
        in_specs=(
            P(("expert", "replica"), None),
            P(),
            P(None, None, None, "tensor"),
            P(None, "tensor", None),
            P(),
            P(None, "expert", None, "tensor"),
            P(None, "expert", "tensor", None),
            P(None, ("expert", "replica"), None),
            P(("expert", "replica"), None),
        ),
        out_specs=(
            P(("expert", "replica"), None),
            P(("expert", "replica"), None),
            P(),
            P(None, None, None, "tensor"),
            P(None, "tensor", None),
            P(),
            P(None, "expert", "replica", "tensor"),
            P(None, "expert", "tensor", "replica"),
        ),
        check_vma=False,
    )
```

time: 680 us -> 601 us (0.88)
  blocking collectives: 146 us -> 26.2 us
  Pallas kernels: 100 us -> 145 us
  matrix products: 42 us -> 0 us
  starting transfers between devices: 67.2 us -> 109 us
  local copies, waits for them, and re-layouts: 40.9 us -> 77.4 us
  waiting for transfers between devices: 243 us -> 219 us
  other arithmetic: 32.4 us -> 12.8 us
    psum x1 -> x0, blocking collectives: 74.1 us -> none  [on_device(): small = lax.psum(small, ('tensor', 'expert', 'replica'))]
    ppermute x0 -> x27, waiting for transfers between devices: none -> 65.3 us  [partner(): return lax.ppermute(value, axis, [(i, i ^ 1 << bit) for i in range(count)])]
    ppermute x28 -> x30, waiting for transfers between devices: 182 us -> 134 us  [swap(): return lax.ppermute(value, axis, [(0, 1), (1, 0)])]
    all_to_all x3 -> x1, blocking collectives: 72.2 us -> 26.2 us  [exchange(): lax.all_to_all(block, 'expert', 0, 0, tiled=True).reshape(slots, width)]
    pallas_call x18 -> x38, Pallas kernels: 100 us -> 145 us  [call(): pl.pallas_call(kernel, grid=grid, out_shape=outs, in_specs=[*specs, *[ANY...]
    ppermute x0 -> x27, starting transfers between devices: none -> 44.5 us  [partner(): return lax.ppermute(value, axis, [(i, i ^ 1 << bit) for i in range(count)])]
    dot_general x12 -> x0, matrix products: 42 us -> none  [dot_t(): return lax.dot_general(left, right, TN, preferred_element_type=F32)]
    unnamed x142 -> x226, local copies, waits for them, and re-layouts: 22.3 us -> 59.5 us
  transfers between devices with their start and end apart: 37 -> 64, of which waited for: 17 -> 33; matrix products, arithmetic and copies ran while one was open for 12% -> 3% of each run, Pallas kernels for 6% -> 12%
where the time goes in v2:
time: 601 us; the launch traced here: 592 us
  waiting for transfers between devices  219 us (36%)
  Pallas kernels  145 us (24%)
  starting transfers between devices  109 us (18%)
  local copies, waits for them, and re-layouts  77.4 us (13%)
  blocking collectives  26.2 us (4%)
  other arithmetic  12.8 us (2%)
    pallas_call x38, Pallas kernels, call(): pl.pallas_call(kernel, grid=grid, out_shape=outs, in_specs=[*specs, *[ANY...  145 us
    ppermute x30, waiting for transfers between devices, swap(): return lax.ppermute(value, axis, [(0, 1), (1, 0)])  134 us
    ppermute x27, waiting for transfers between devices, partner(): return lax.ppermute(value, axis, [(i, i ^ 1 << bit) for i in range(count)])  65.3 us
    unnamed x226, local copies, waits for them, and re-layouts  59.5 us
    ppermute x27, starting transfers between devices, partner(): return lax.ppermute(value, axis, [(i, i ^ 1 << bit) for i in range(count)])  44.5 us
    all_to_all x7, starting transfers between devices, exchange(): lax.all_to_all(block, 'expert', 0, 0, tiled=True).reshape(slots, width)  38.9 us
    all_to_all x1, blocking collectives, exchange(): lax.all_to_all(block, 'expert', 0, 0, tiled=True).reshape(slots, width)  26.2 us
    ppermute x30, starting transfers between devices, swap(): return lax.ppermute(value, axis, [(0, 1), (1, 0)])  25.8 us
  transfers between devices with their start and end apart: 64, of which 33 were waited for; matrix products, arithmetic and copies ran while one was open for 3% of the time, Pallas kernels for 12%

profile of v2, /device:TPU:0, one launch (start us, length us, event | category | flops | bytes accessed | tf_op | source)
XLA Modules:
  0.0 592.1 jit_solution(11198632074006096165)
XLA Ops:
  4.1 4.3 shard_map.152
  10.2 2.9 collective-permute-start
  13.2 2.3 copy-done.7
  22.5 5.8 collective-permute-done.refs_3_
  28.4 2.3 copy-done.5
  36.5 5.8 all-to-all-start
  42.4 11.4 %collective-permute-done.1.refs_4_.refs_7_ = bf16[768,768]{1,0:T(8,128)(2,1)} collective-permute-done((bf16[768,768]{1,0:T(8,128)(2,1)}, bf16[768,768]{1,0:T(8,128)(2,1)}, u32[]{:S(2)}, u32[]{:S(2)}) %collective-permute-start.1) | collective-permute-done | bytes 1179680 | tf_op jit(solution)/shard_map/ppermute | solution.py:435
  53.8 24.3 %collective-permute-done.3.refs_7_.refs_10_ = bf16[768,768]{1,0:T(8,128)(2,1)S(1)} collective-permute-done((bf16[768,768]{1,0:T(8,128)(2,1)}, bf16[768,768]{1,0:T(8,128)(2,1)S(1)}, u32[]{:S(2)}, u32[]{:S(2)}) %collective-permute-start.3) | collective-permute-done | bytes 1179680 | tf_op jit(solution)/shard_map/ppermute | solution.py:435
  78.8 2.6 copy-done.8
  84.1 13.1 %shard_map.157 = (bf16[512,768]{1,0:T(8,128)(2,1)}, bf16[512,3072]{1,0:T(8,128)(2,1)}, bf16[512,3072]{1,0:T(8,128)(2,1)}) custom-call(s32[3]{0:T(128)} %copy-done.91, bf16[512,768]{1,0:T(8,128)(2,1)} %bitcast.65, bf16[8,768]{1,0:T(8,128)(2,1)} %get-tuple-element.241.refs_2_.refs_5_, bf16[2,1,768,1536]{3,2,1,0:T(8,128)(2,1)} %refs_6_.7, ...), custom_call_target="tpu_custom_call" | custom-call | flops 4831838208 | bytes 22032396 | tf_op jit(solution)/shard_map/pallas_call | solution.py:68
  97.2 6.6 %all-to-all-start.1 = ((bf16[8,64,768]{2,1,0:T(8,128)(2,1)}), bf16[8,64,768]{2,1,0:T(8,128)(2,1)}, u32[]{:S(2)}, u32[]{:S(2)}) async-start(bf16[8,64,768]{2,1,0:T(8,128)(2,1)} %bitcast.97), calls=%async_computation.1 | async-start | bytes 1572864 | tf_op jit(solution)/shard_map/all_to_all | solution.py:560
  105.4 19.2 %all-to-all-done.1 = bf16[8,64,768]{2,1,0:T(8,128)(2,1)} async-done(((bf16[8,64,768]{2,1,0:T(8,128)(2,1)}), bf16[8,64,768]{2,1,0:T(8,128)(2,1)}, u32[]{:S(2)}, u32[]{:S(2)}) %all-to-all-start.1) | async-done | bytes 786464 | tf_op jit(solution)/shard_map/all_to_all | solution.py:560
  129.1 3.9 collective-permute-done.6.refs_6_.refs_5_
  133.0 12.8 %collective-permute-done.5.refs_2_ = bf16[416,768]{1,0:T(8,128)(2,1)S(1)} collective-permute-done((bf16[416,768]{1,0:T(8,128)(2,1)S(1)}, bf16[416,768]{1,0:T(8,128)(2,1)S(1)}, u32[]{:S(2)}, u32[]{:S(2)}) %collective-permute-start.5) | collective-permute-done | bytes 639008 | tf_op jit(solution)/shard_map/ppermute | solution.py:435
  148.4 5.2 shard_map.159
  158.7 5.7 all-to-all-start.2
  164.4 8.6 %collective-permute-done.7.refs_3_ = bf16[416,768]{1,0:T(8,128)(2,1)S(1)} collective-permute-done((bf16[416,768]{1,0:T(8,128)(2,1)}, bf16[416,768]{1,0:T(8,128)(2,1)S(1)}, u32[]{:S(2)}, u32[]{:S(2)}) %collective-permute-start.7) | collective-permute-done | bytes 639008 | tf_op jit(solution)/shard_map/ppermute | solution.py:435
  173.1 2.3 copy-done.6
  176.7 3.2 shard_map.160
  183.7 4.2 all-to-all-start.3
  187.9 19.6 %collective-permute-done.9.refs_8_ = bf16[768,768]{1,0:T(8,128)(2,1)} collective-permute-done((bf16[768,768]{1,0:T(8,128)(2,1)S(1)}, bf16[768,768]{1,0:T(8,128)(2,1)}, u32[]{:S(2)}, u32[]{:S(2)}) %collective-permute-start.9) | collective-permute-done | bytes 1179680 | tf_op jit(solution)/shard_map/ppermute | solution.py:435
  207.6 3.0 collective-permute-done.10.refs_9_
  211.6 22.2 %shard_map.161 = (bf16[512,768]{1,0:T(8,128)(2,1)}, bf16[512,768]{1,0:T(8,128)(2,1)}, bf16[512,3072]{1,0:T(8,128)(2,1)}, bf16[512,3072]{1,0:T(8,128)(2,1)}, bf16[512,768]{1,0:T(8,128)(2,1)}, /*index=5*/f32[8,768]{1,0:T(8,128)}) custom-call(s32[3]{0:T(128)} %copy-done.91, bf16[512,768]{1,0:T(8,128)(2,1)} %bitcast.13.refs_1_, bf16[512,768]{1,0:T(8,128)(2,1)} %bitcast.70, ...), custom_call_target="tpu_custom_call" | custom-call | flops 9663676416 | bytes 24416268 | tf_op jit(solution)/shard_map/pallas_call | solution.py:68
  233.9 26.2 %all_to_all.40 = bf16[8,64,768]{2,1,0:T(8,128)(2,1)S(1)} all-to-all(bf16[8,64,768]{2,1,0:T(8,128)(2,1)} %bitcast.96), channel_id=1, replica_groups=mesh['tensor'=2,'expert'=8,'replica'=2] {'expert'}, dimensions={0} | all-to-all | bytes 1572864 | tf_op jit(solution)/shard_map/all_to_all | solution.py:560
  265.7 5.5 shard_map.164
  273.2 14.8 %collective-permute-done.12.refs_2_ = bf16[416,768]{1,0:T(8,128)(2,1)S(1)} collective-permute-done((bf16[416,768]{1,0:T(8,128)(2,1)S(1)}, bf16[416,768]{1,0:T(8,128)(2,1)S(1)}, u32[]{:S(2)}, u32[]{:S(2)}) %collective-permute-start.12) | collective-permute-done | bytes 639008 | tf_op jit(solution)/shard_map/ppermute | solution.py:435
  288.1 14.0 %shard_map.165 = (f32[416,768]{1,0:T(8,128)S(1)}, f32[1,768]{1,0:T(1,128)S(1)}, bf16[416,768]{1,0:T(8,128)(2,1)S(1)}, bf16[1536,384]{1,0:T(8,128)(2,1)S(1)}, bf16[1536,384]{1,0:T(8,128)(2,1)}) custom-call(s32[3]{0:T(128)S(1)} %copy-done.93, bf16[416,768]{1,0:T(8,128)(2,1)S(1)} %get-tuple-element.124.refs_5_.refs_1_, ...), custom_call_target="tpu_custom_call" | custom-call | flops 2295201792 | bytes 14121996 | tf_op jit(solution)/shard_map/pallas_call | solution.py:68
  311.5 3.9 shard_map.166
  315.5 6.7 %collective-permute-done.13.refs_1_ = bf16[416,768]{1,0:T(8,128)(2,1)S(1)} collective-permute-done((bf16[416,768]{1,0:T(8,128)(2,1)}, bf16[416,768]{1,0:T(8,128)(2,1)S(1)}, u32[]{:S(2)}, u32[]{:S(2)}) %collective-permute-start.13) | collective-permute-done | bytes 639008 | tf_op jit(solution)/shard_map/ppermute | solution.py:435
  322.2 2.4 shard_map.168
  325.6 4.3 all-to-all-start.6
  334.9 16.5 %collective-permute-done.19.refs_4_ = bf16[4,96,384]{2,1,0:T(8,128)(2,1)S(1)} collective-permute-done((bf16[4,96,384]{2,1,0:T(8,128)(2,1)}, bf16[4,96,384]{2,1,0:T(8,128)(2,1)S(1)}, u32[]{:S(2)}, u32[]{:S(2)}) %collective-permute-start.19) | collective-permute-done | bytes 294944 | tf_op jit(solution)/shard_map/ppermute | solution.py:440
  355.1 2.8 collective-permute-done.17.refs_12_.refs_7_
  357.9 14.5 %shard_map.170 = (bf16[512,768]{1,0:T(8,128)(2,1)}, bf16[512,3072]{1,0:T(8,128)(2,1)}, bf16[512,768]{1,0:T(8,128)(2,1)}, f32[8,768]{1,0:T(8,128)}) custom-call(s32[3]{0:T(128)} %copy-done.91, bf16[512,768]{1,0:T(8,128)(2,1)} %bitcast.29.refs_1_, bf16[512,768]{1,0:T(8,128)(2,1)} %bitcast.66, bf16[512,3072]{1,0:T(8,128)(2,1)} %get-tuple-element.141.refs_3_.refs_4_, ...), custom_call_target="tpu_custom_call" | custom-call | flops 4831838208 | bytes 26775564 | tf_op jit(solution)/shard_map/pallas_call | solution.py:68
  372.4 6.0 %all-to-all-start.7 = ((bf16[8,64,768]{2,1,0:T(8,128)(2,1)}), bf16[8,64,768]{2,1,0:T(8,128)(2,1)}, u32[]{:S(2)}, u32[]{:S(2)}) async-start(bf16[8,64,768]{2,1,0:T(8,128)(2,1)} %bitcast.95), calls=%async_computation.7 | async-start | bytes 1572864 | tf_op jit(solution)/shard_map/all_to_all | solution.py:560
  383.5 6.0 %collective-permute-done.22.refs_4_ = bf16[2,96,384]{2,1,0:T(8,128)(2,1)} collective-permute-done((bf16[2,96,384]{2,1,0:T(8,128)(2,1)}, bf16[2,96,384]{2,1,0:T(8,128)(2,1)}, u32[]{:S(2)}, u32[]{:S(2)}) %collective-permute-start.22) | collective-permute-done | bytes 147488 | tf_op jit(solution)/shard_map/ppermute | solution.py:440
  389.5 4.1 collective-permute-done.21.refs_2_
  397.6 7.4 %collective-permute-done.20.refs_2_.refs_8_ = bf16[1536,384]{1,0:T(8,128)(2,1)} collective-permute-done((bf16[1536,384]{1,0:T(8,128)(2,1)}, bf16[1536,384]{1,0:T(8,128)(2,1)}, u32[]{:S(2)}, u32[]{:S(2)}) %collective-permute-start.20) | collective-permute-done | bytes 1179680 | tf_op jit(solution)/shard_map/ppermute | solution.py:435
  411.0 5.5 shard_map.173
  418.5 2.6 collective-permute-start.25
  421.4 5.0 collective-permute-done.25.refs_3_
  429.1 4.2 collective-permute-done.23.refs_2_
  433.4 13.9 %shard_map.175 = (f32[416,768]{1,0:T(8,128)S(1)}, f32[1,768]{1,0:T(1,128)S(1)}, bf16[416,768]{1,0:T(8,128)(2,1)S(1)}, bf16[1536,384]{1,0:T(8,128)(2,1)S(1)}, bf16[1536,384]{1,0:T(8,128)(2,1)}) custom-call(s32[3]{0:T(128)S(1)} %copy-done.94, bf16[416,768]{1,0:T(8,128)(2,1)S(1)} %shard_map.172.refs_5_.refs_1_, ...), custom_call_target="tpu_custom_call" | custom-call | flops 2295201792 | bytes 14760972 | tf_op jit(solution)/shard_map/pallas_call | solution.py:68
  450.2 6.2 %all-to-all-start.5 = ((bf16[8,64,768]{2,1,0:T(8,128)(2,1)}), bf16[8,64,768]{2,1,0:T(8,128)(2,1)}, u32[]{:S(2)}, u32[]{:S(2)}) async-start(bf16[8,64,768]{2,1,0:T(8,128)(2,1)} %bitcast.87), calls=%async_computation.5 | async-start | bytes 1572864 | tf_op jit(solution)/shard_map/all_to_all | solution.py:560
  458.3 4.3 shard_map.176
  470.5 2.4 collective-permute-start.30
  472.9 4.7 collective-permute-done.37.refs_2_
  477.7 4.2 collective-permute-done.38.refs_4_
  483.5 3.7 collective-permute-start.29
  487.1 3.0 collective-permute-done.29.refs_2_
  495.9 2.3 collective-permute-start.41
  498.7 2.4 collective-permute-start.42
  509.5 7.6 %collective-permute-done.46.refs_5_.refs_8_ = bf16[1536,384]{1,0:T(8,128)(2,1)} collective-permute-done((bf16[1536,384]{1,0:T(8,128)(2,1)}, bf16[1536,384]{1,0:T(8,128)(2,1)}, u32[]{:S(2)}, u32[]{:S(2)}) %collective-permute-start.46) | collective-permute-done | bytes 1179680 | tf_op jit(solution)/shard_map/ppermute | solution.py:435
  517.1 3.0 collective-permute-start.45
  520.0 2.3 collective-permute-done.45.refs_4_
  537.7 6.2 %collective-permute-done.49.refs_2_ = bf16[4,96,384]{2,1,0:T(8,128)(2,1)S(1)} collective-permute-done((bf16[4,96,384]{2,1,0:T(8,128)(2,1)S(1)}, bf16[4,96,384]{2,1,0:T(8,128)(2,1)S(1)}, u32[]{:S(2)}, u32[]{:S(2)}) %collective-permute-start.49) | collective-permute-done | bytes 294944 | tf_op jit(solution)/shard_map/ppermute | solution.py:440
  546.4 4.6 collective-permute-done.32
  551.0 3.2 collective-permute-start.33
  554.3 4.6 collective-permute-done.33
  566.0 4.9 shard_map.188
  572.1 2.6 reshape.145
  577.8 4.9 shard_map.189
  582.7 3.0 select_convert_fusion.1
  588.2 3.4 pad_maximum_fusion
  (375 shorter events, 148.1 us)
Async XLA Ops:
  10.2 18.1 %collective-permute-start = (bf16[416,768]{1,0:T(8,128)(2,1)S(1)}, bf16[416,768]{1,0:T(8,128)(2,1)S(1)}, u32[]{:S(2)}, u32[]{:S(2)}) collective-permute-start(bf16[416,768]{1,0:T(8,128)(2,1)S(1)} %get-tuple-element.109.refs_3_.refs_2_), channel_id=1, source_target_pairs={{0,16},{16,0},{1,17},{17,1},{2,18},{18,2},{3,19},{19,3},{4,20},{20... | collective-permute-start | bytes 1916936 | tf_op jit(solution)/shard_map/ppermute | solution.py:435
  17.2 36.6 %collective-permute-start.1 = (bf16[768,768]{1,0:T(8,128)(2,1)}, bf16[768,768]{1,0:T(8,128)(2,1)}, u32[]{:S(2)}, u32[]{:S(2)}) collective-permute-start(bf16[768,768]{1,0:T(8,128)(2,1)} %shard_map.155), channel_id=1, source_target_pairs={{0,16},{16,0},{1,17},{17,1},{2,18},{18,2},{3,19},{19,3},{4,20},{20... | collective-permute-start | bytes 3538952 | tf_op jit(solution)/shard_map/ppermute | solution.py:435
  34.5 43.6 %collective-permute-start.3 = (bf16[768,768]{1,0:T(8,128)(2,1)}, bf16[768,768]{1,0:T(8,128)(2,1)S(1)}, u32[]{:S(2)}, u32[]{:S(2)}) collective-permute-start(bf16[768,768]{1,0:T(8,128)(2,1)} %get-tuple-element.113), channel_id=1, source_target_pairs={{0,16},{16,0},{1,17},{17,1},{2,18},{18,2},{3,19},{19,3},{4,20},{20... | collective-permute-start | bytes 3538952 | tf_op jit(solution)/shard_map/ppermute | solution.py:435
  36.5 42.2 %all-to-all-start = ((bf16[8,64,768]{2,1,0:T(8,128)(2,1)}), bf16[8,64,768]{2,1,0:T(8,128)(2,1)S(1)}, u32[]{:S(2)}, u32[]{:S(2)}) async-start(bf16[8,64,768]{2,1,0:T(8,128)(2,1)} %bitcast.89), calls=%async_computation | async-start | bytes 1572864 | tf_op jit(solution)/shard_map/all_to_all | solution.py:560
  53.8 29.3 %collective-permute-start.2 = (bf16[768,768]{1,0:T(8,128)(2,1)}, bf16[768,768]{1,0:T(8,128)(2,1)S(1)}, u32[]{:S(2)}, u32[]{:S(2)}) collective-permute-start(bf16[768,768]{1,0:T(8,128)(2,1)} %collective-permute-done.1.refs_4_.refs_7_), channel_id=1, source_target_pairs={{0,1},{1,0},{2,3},{3,2},{4,5},{5,4},{6,7},{7,6},{8,9},{9,8},{10,11... | collective-permute-start | bytes 3538952 | tf_op jit(solution)/shard_map/ppermute | solution.py:435
  78.1 5.0 collective-permute-start.4
  97.2 27.4 %all-to-all-start.1 = ((bf16[8,64,768]{2,1,0:T(8,128)(2,1)}), bf16[8,64,768]{2,1,0:T(8,128)(2,1)}, u32[]{:S(2)}, u32[]{:S(2)}) async-start(bf16[8,64,768]{2,1,0:T(8,128)(2,1)} %bitcast.97), calls=%async_computation.1 | async-start | bytes 1572864 | tf_op jit(solution)/shard_map/all_to_all | solution.py:560
  103.8 29.2 %collective-permute-start.6 = (bf16[768,768]{1,0:T(8,128)(2,1)}, bf16[768,768]{1,0:T(8,128)(2,1)}, u32[]{:S(2)}, u32[]{:S(2)}) collective-permute-start(bf16[768,768]{1,0:T(8,128)(2,1)} %copy-done.61), channel_id=1, source_target_pairs={{0,16},{16,0},{1,17},{17,1},{2,18},{18,2},{3,19},{19,3},{4,20},{20... | collective-permute-start | bytes 3538952 | tf_op jit(solution)/shard_map/ppermute | solution.py:435
  127.5 18.3 %collective-permute-start.5 = (bf16[416,768]{1,0:T(8,128)(2,1)S(1)}, bf16[416,768]{1,0:T(8,128)(2,1)S(1)}, u32[]{:S(2)}, u32[]{:S(2)}) collective-permute-start(bf16[416,768]{1,0:T(8,128)(2,1)S(1)} %shard_map.158.refs_1_), channel_id=1, source_target_pairs={{0,16},{16,0},{1,17},{17,1},{2,18},{18,2},{3,19},{19,3},{4,20},{20... | collective-permute-start | bytes 1916936 | tf_op jit(solution)/shard_map/ppermute | solution.py:435
  157.2 15.8 %collective-permute-start.7 = (bf16[416,768]{1,0:T(8,128)(2,1)}, bf16[416,768]{1,0:T(8,128)(2,1)S(1)}, u32[]{:S(2)}, u32[]{:S(2)}) collective-permute-start(bf16[416,768]{1,0:T(8,128)(2,1)} %get-tuple-element.116.refs_2_), channel_id=1, source_target_pairs={{0,16},{16,0},{1,17},{17,1},{2,18},{18,2},{3,19},{19,3},{4,20},{20... | collective-permute-start | bytes 1916936 | tf_op jit(solution)/shard_map/ppermute | solution.py:435
  158.7 25.0 %all-to-all-start.2 = ((bf16[8,64,768]{2,1,0:T(8,128)(2,1)}), bf16[8,64,768]{2,1,0:T(8,128)(2,1)}, u32[]{:S(2)}, u32[]{:S(2)}) async-start(bf16[8,64,768]{2,1,0:T(8,128)(2,1)} %bitcast.88), calls=%async_computation.2 | async-start | bytes 1572864 | tf_op jit(solution)/shard_map/all_to_all | solution.py:560
  181.0 26.5 %collective-permute-start.9 = (bf16[768,768]{1,0:T(8,128)(2,1)S(1)}, bf16[768,768]{1,0:T(8,128)(2,1)}, u32[]{:S(2)}, u32[]{:S(2)}) collective-permute-start(bf16[768,768]{1,0:T(8,128)(2,1)S(1)} %get-tuple-element.120), channel_id=1, source_target_pairs={{0,16},{16,0},{1,17},{17,1},{2,18},{18,2},{3,19},{19,3},{4,20},{20... | collective-permute-start | bytes 3538952 | tf_op jit(solution)/shard_map/ppermute | solution.py:435
  183.7 23.9 %all-to-all-start.3 = ((bf16[8,64,768]{2,1,0:T(8,128)(2,1)}), bf16[8,64,768]{2,1,0:T(8,128)(2,1)S(1)}, u32[]{:S(2)}, u32[]{:S(2)}) async-start(bf16[8,64,768]{2,1,0:T(8,128)(2,1)} %bitcast.14), calls=%async_computation.3 | async-start | bytes 1572864 | tf_op jit(solution)/shard_map/all_to_all | solution.py:560
  187.9 19.6 %collective-permute-start.8 = (bf16[768,768]{1,0:T(8,128)(2,1)}, bf16[768,768]{1,0:T(8,128)(2,1)}, u32[]{:S(2)}, u32[]{:S(2)}) collective-permute-start(bf16[768,768]{1,0:T(8,128)(2,1)} %collective-permute-done.6.refs_6_.refs_5_), channel_id=1, source_target_pairs={{0,1},{1,0},{2,3},{3,2},{4,5},{5,4},{6,7},{7,6},{8,9},{9,8},{10,11... | collective-permute-start | bytes 3538952 | tf_op jit(solution)/shard_map/ppermute | solution.py:435
  207.5 3.1 collective-permute-start.10
  271.3 40.2 %collective-permute-start.14 = (bf16[384,3072]{1,0:T(8,128)(2,1)}, bf16[384,3072]{1,0:T(8,128)(2,1)}, u32[]{:S(2)}, u32[]{:S(2)}) collective-permute-start(bf16[384,3072]{1,0:T(8,128)(2,1)} %get-tuple-element.131.refs_11_), channel_id=1, source_target_pairs={{0,1},{1,0},{2,3},{3,2},{4,5},{5,4},{6,7},{7,6},{8,9},{9,8},{10,11... | collective-permute-start | bytes 7077896 | tf_op jit(solution)/shard_map/ppermute | solution.py:435
  271.3 40.2 %collective-permute-start.15 = (bf16[3072,384]{1,0:T(8,128)(2,1)}, bf16[3072,384]{1,0:T(8,128)(2,1)}, u32[]{:S(2)}, u32[]{:S(2)}) collective-permute-start(bf16[3072,384]{1,0:T(8,128)(2,1)} %get-tuple-element.132.refs_12_), channel_id=1, source_target_pairs={{0,1},{1,0},{2,3},{3,2},{4,5},{5,4},{6,7},{7,6},{8,9},{9,8},{10,11... | collective-permute-start | bytes 7077896 | tf_op jit(solution)/shard_map/ppermute | solution.py:435
  271.8 16.3 %collective-permute-start.12 = (bf16[416,768]{1,0:T(8,128)(2,1)S(1)}, bf16[416,768]{1,0:T(8,128)(2,1)S(1)}, u32[]{:S(2)}, u32[]{:S(2)}) collective-permute-start(bf16[416,768]{1,0:T(8,128)(2,1)S(1)} %get-tuple-element.124.refs_5_.refs_1_), channel_id=1, source_target_pairs={{0,16},{16,0},{1,17},{17,1},{2,18},{18,2},{3,19},{19,3},{4,20},{20... | collective-permute-start | bytes 1916936 | tf_op jit(solution)/shard_map/ppermute | solution.py:435
  305.1 3.2 collective-permute-start.16
  305.2 17.0 %collective-permute-start.13 = (bf16[416,768]{1,0:T(8,128)(2,1)}, bf16[416,768]{1,0:T(8,128)(2,1)S(1)}, u32[]{:S(2)}, u32[]{:S(2)}) collective-permute-start(bf16[416,768]{1,0:T(8,128)(2,1)} %copy-done.48), channel_id=1, source_target_pairs={{0,16},{16,0},{1,17},{17,1},{2,18},{18,2},{3,19},{19,3},{4,20},{20... | collective-permute-start | bytes 1916936 | tf_op jit(solution)/shard_map/ppermute | solution.py:435
  325.6 32.3 %all-to-all-start.6 = ((bf16[8,64,768]{2,1,0:T(8,128)(2,1)}), bf16[8,64,768]{2,1,0:T(8,128)(2,1)}, u32[]{:S(2)}, u32[]{:S(2)}) async-start(bf16[8,64,768]{2,1,0:T(8,128)(2,1)} %bitcast.28), calls=%async_computation.6 | async-start | bytes 1572864 | tf_op jit(solution)/shard_map/all_to_all | solution.py:560
  330.0 28.0 %collective-permute-start.17 = (bf16[384,1536]{1,0:T(8,128)(2,1)}, bf16[384,1536]{1,0:T(8,128)(2,1)}, u32[]{:S(2)}, u32[]{:S(2)}) collective-permute-start(bf16[384,1536]{1,0:T(8,128)(2,1)} %copy-done.60), channel_id=1, source_target_pairs={{0,16},{16,0},{1,17},{17,1},{2,18},{18,2},{3,19},{19,3},{4,20},{20... | collective-permute-start | bytes 3538952 | tf_op jit(solution)/shard_map/ppermute | solution.py:435
  331.5 19.9 %collective-permute-start.19 = (bf16[4,96,384]{2,1,0:T(8,128)(2,1)}, bf16[4,96,384]{2,1,0:T(8,128)(2,1)S(1)}, u32[]{:S(2)}, u32[]{:S(2)}) collective-permute-start(bf16[4,96,384]{2,1,0:T(8,128)(2,1)} %copy-done.102), channel_id=1, source_target_pairs={{0,4},{2,6},{4,0},{6,2},{8,12},{10,14},{12,8},{14,10},{1,5},{3,7},... | collective-permute-start | bytes 884744 | tf_op jit(solution)/shard_map/ppermute | solution.py:440
  333.3 18.1 %collective-permute-start.18 = (bf16[4,96,384]{2,1,0:T(8,128)(2,1)S(1)}, bf16[4,96,384]{2,1,0:T(8,128)(2,1)S(1)}, u32[]{:S(2)}, u32[]{:S(2)}) collective-permute-start(bf16[4,96,384]{2,1,0:T(8,128)(2,1)S(1)} %get-tuple-element.139.refs_8_), channel_id=1, source_target_pairs={{0,2},{2,0},{4,6},{6,4},{8,10},{10,8},{12,14},{14,12},{1,3},{3,1},... | collective-permute-start | bytes 884744 | tf_op jit(solution)/shard_map/ppermute | solution.py:440
  372.4 32.5 %all-to-all-start.7 = ((bf16[8,64,768]{2,1,0:T(8,128)(2,1)}), bf16[8,64,768]{2,1,0:T(8,128)(2,1)}, u32[]{:S(2)}, u32[]{:S(2)}) async-start(bf16[8,64,768]{2,1,0:T(8,128)(2,1)} %bitcast.95), calls=%async_computation.7 | async-start | bytes 1572864 | tf_op jit(solution)/shard_map/all_to_all | solution.py:560
  378.4 26.5 %collective-permute-start.20 = (bf16[1536,384]{1,0:T(8,128)(2,1)}, bf16[1536,384]{1,0:T(8,128)(2,1)}, u32[]{:S(2)}, u32[]{:S(2)}) collective-permute-start(bf16[1536,384]{1,0:T(8,128)(2,1)} %copy-done.59), channel_id=1, source_target_pairs={{0,16},{16,0},{1,17},{17,1},{2,18},{18,2},{3,19},{19,3},{4,20},{20... | collective-permute-start | bytes 3538952 | tf_op jit(solution)/shard_map/ppermute | solution.py:435
  379.9 9.6 %collective-permute-start.22 = (bf16[2,96,384]{2,1,0:T(8,128)(2,1)}, bf16[2,96,384]{2,1,0:T(8,128)(2,1)}, u32[]{:S(2)}, u32[]{:S(2)}) collective-permute-start(bf16[2,96,384]{2,1,0:T(8,128)(2,1)} %copy-done.103), channel_id=1, source_target_pairs={{0,2},{2,0},{4,6},{6,4},{8,10},{10,8},{12,14},{14,12},{1,3},{3,1},... | collective-permute-start | bytes 442376 | tf_op jit(solution)/shard_map/ppermute | solution.py:440
  381.9 11.7 %collective-permute-start.21 = (bf16[2,96,384]{2,1,0:T(8,128)(2,1)S(1)}, bf16[2,96,384]{2,1,0:T(8,128)(2,1)}, u32[]{:S(2)}, u32[]{:S(2)}) collective-permute-start(bf16[2,96,384]{2,1,0:T(8,128)(2,1)S(1)} %copy-done.86), channel_id=1, source_target_pairs={{0,4},{2,6},{4,0},{6,2},{8,12},{10,14},{12,8},{14,10},{1,5},{3,7},... | collective-permute-start | bytes 442376 | tf_op jit(solution)/shard_map/ppermute | solution.py:440
  416.5 39.8 %collective-permute-start.27 = (bf16[384,3072]{1,0:T(8,128)(2,1)}, bf16[384,3072]{1,0:T(8,128)(2,1)}, u32[]{:S(2)}, u32[]{:S(2)}) collective-permute-start(bf16[384,3072]{1,0:T(8,128)(2,1)} %get-tuple-element.158.refs_11_), channel_id=1, source_target_pairs={{0,1},{1,0},{2,3},{3,2},{4,5},{5,4},{6,7},{7,6},{8,9},{9,8},{10,11... | collective-permute-start | bytes 7077896 | tf_op jit(solution)/shard_map/ppermute | solution.py:435
  416.5 39.8 %collective-permute-start.28 = (bf16[3072,384]{1,0:T(8,128)(2,1)}, bf16[3072,384]{1,0:T(8,128)(2,1)}, u32[]{:S(2)}, u32[]{:S(2)}) collective-permute-start(bf16[3072,384]{1,0:T(8,128)(2,1)} %get-tuple-element.159.refs_12_), channel_id=1, source_target_pairs={{0,1},{1,0},{2,3},{3,2},{4,5},{5,4},{6,7},{7,6},{8,9},{9,8},{10,11... | collective-permute-start | bytes 7077896 | tf_op jit(solution)/shard_map/ppermute | solution.py:435
  417.0 16.3 %collective-permute-start.23 = (bf16[416,768]{1,0:T(8,128)(2,1)S(1)}, bf16[416,768]{1,0:T(8,128)(2,1)S(1)}, u32[]{:S(2)}, u32[]{:S(2)}) collective-permute-start(bf16[416,768]{1,0:T(8,128)(2,1)S(1)} %shard_map.172.refs_5_.refs_1_), channel_id=1, source_target_pairs={{0,16},{16,0},{1,17},{17,1},{2,18},{18,2},{3,19},{19,3},{4,20},{20... | collective-permute-start | bytes 1916936 | tf_op jit(solution)/shard_map/ppermute | solution.py:435
  418.5 7.9 %collective-permute-start.25 = (bf16[1,96,384]{2,1,0:T(8,128)(2,1)S(1)}, bf16[1,96,384]{2,1,0:T(8,128)(2,1)S(1)}, u32[]{:S(2)}, u32[]{:S(2)}) collective-permute-start(bf16[1,96,384]{2,1,0:T(8,128)(2,1)S(1)} %copy-done.105), channel_id=1, source_target_pairs={{0,8},{2,10},{4,12},{6,14},{8,0},{10,2},{12,4},{14,6},{1,9},{3,11}... | collective-permute-start | bytes 221192 | tf_op jit(solution)/shard_map/ppermute | solution.py:440
  421.1 7.3 %collective-permute-start.24 = (bf16[1,96,384]{2,1,0:T(8,128)(2,1)S(1)}, bf16[1,96,384]{2,1,0:T(8,128)(2,1)S(1)}, u32[]{:S(2)}, u32[]{:S(2)}) collective-permute-start(bf16[1,96,384]{2,1,0:T(8,128)(2,1)S(1)} %copy-done.101), channel_id=1, source_target_pairs={{0,8},{2,10},{4,12},{6,14},{8,0},{10,2},{12,4},{14,6},{1,9},{3,11}... | collective-permute-start | bytes 221192 | tf_op jit(solution)/shard_map/ppermute | solution.py:440
  450.2 14.6 %collective-permute-start.36 = (bf16[1536,384]{1,0:T(8,128)(2,1)}, bf16[1536,384]{1,0:T(8,128)(2,1)}, u32[]{:S(2)}, u32[]{:S(2)}) collective-permute-start(bf16[1536,384]{1,0:T(8,128)(2,1)} %get-tuple-element.178), channel_id=1, source_target_pairs={{0,1},{1,0},{2,3},{3,2},{4,5},{5,4},{6,7},{7,6},{8,9},{9,8},{10,11... | collective-permute-start | bytes 3538952 | tf_op jit(solution)/shard_map/ppermute | solution.py:435
  450.2 55.6 %all-to-all-start.5 = ((bf16[8,64,768]{2,1,0:T(8,128)(2,1)}), bf16[8,64,768]{2,1,0:T(8,128)(2,1)}, u32[]{:S(2)}, u32[]{:S(2)}) async-start(bf16[8,64,768]{2,1,0:T(8,128)(2,1)} %bitcast.87), calls=%async_computation.5 | async-start | bytes 1572864 | tf_op jit(solution)/shard_map/all_to_all | solution.py:560
  462.6 44.9 %collective-permute-start.43 = (bf16[384,1536]{1,0:T(8,128)(2,1)}, bf16[384,1536]{1,0:T(8,128)(2,1)}, u32[]{:S(2)}, u32[]{:S(2)}) collective-permute-start(bf16[384,1536]{1,0:T(8,128)(2,1)} %get-tuple-element.166.refs_5_), channel_id=1, source_target_pairs={{0,16},{16,0},{1,17},{17,1},{2,18},{18,2},{3,19},{19,3},{4,20},{20... | collective-permute-start | bytes 3538952 | tf_op jit(solution)/shard_map/ppermute | solution.py:435
  464.1 53.0 %collective-permute-start.46 = (bf16[1536,384]{1,0:T(8,128)(2,1)}, bf16[1536,384]{1,0:T(8,128)(2,1)}, u32[]{:S(2)}, u32[]{:S(2)}) collective-permute-start(bf16[1536,384]{1,0:T(8,128)(2,1)} %get-tuple-element.167.refs_6_), channel_id=1, source_target_pairs={{0,16},{16,0},{1,17},{17,1},{2,18},{18,2},{3,19},{19,3},{4,20},{20... | collective-permute-start | bytes 3538952 | tf_op jit(solution)/shard_map/ppermute | solution.py:435
  467.0 10.7 %collective-permute-start.37 = (bf16[4,96,384]{2,1,0:T(8,128)(2,1)S(1)}, bf16[4,96,384]{2,1,0:T(8,128)(2,1)S(1)}, u32[]{:S(2)}, u32[]{:S(2)}) collective-permute-start(bf16[4,96,384]{2,1,0:T(8,128)(2,1)S(1)} %get-tuple-element.180), channel_id=1, source_target_pairs={{0,2},{2,0},{4,6},{6,4},{8,10},{10,8},{12,14},{14,12},{1,3},{3,1},... | collective-permute-start | bytes 884744 | tf_op jit(solution)/shard_map/ppermute | solution.py:440
  469.1 12.8 %collective-permute-start.38 = (bf16[4,96,384]{2,1,0:T(8,128)(2,1)S(1)}, bf16[4,96,384]{2,1,0:T(8,128)(2,1)S(1)}, u32[]{:S(2)}, u32[]{:S(2)}) collective-permute-start(bf16[4,96,384]{2,1,0:T(8,128)(2,1)S(1)} %get-tuple-element.182), channel_id=1, source_target_pairs={{0,4},{2,6},{4,0},{6,2},{8,12},{10,14},{12,8},{14,10},{1,5},{3,7},... | collective-permute-start | bytes 884744 | tf_op jit(solution)/shard_map/ppermute | solution.py:440
  470.5 12.9 %collective-permute-start.30 = (bf16[1,96,384]{2,1,0:T(8,128)(2,1)S(1)}, bf16[1,96,384]{2,1,0:T(8,128)(2,1)S(1)}, u32[]{:S(2)}, u32[]{:S(2)}) collective-permute-start(bf16[1,96,384]{2,1,0:T(8,128)(2,1)S(1)} %copy-done.98), channel_id=1, source_target_pairs={{0,8},{2,10},{4,12},{6,14},{8,0},{10,2},{12,4},{14,6},{1,9},{3,11}... | collective-permute-start | bytes 221192 | tf_op jit(solution)/shard_map/ppermute | solution.py:440
  482.5 10.2 %collective-permute-start.39 = (bf16[2,96,384]{2,1,0:T(8,128)(2,1)S(1)}, bf16[2,96,384]{2,1,0:T(8,128)(2,1)S(1)}, u32[]{:S(2)}, u32[]{:S(2)}) collective-permute-start(bf16[2,96,384]{2,1,0:T(8,128)(2,1)S(1)} %get-tuple-element.184), channel_id=1, source_target_pairs={{0,4},{2,6},{4,0},{6,2},{8,12},{10,14},{12,8},{14,10},{1,5},{3,7},... | collective-permute-start | bytes 442376 | tf_op jit(solution)/shard_map/ppermute | solution.py:440
  482.6 10.3 %collective-permute-start.40 = (bf16[2,96,384]{2,1,0:T(8,128)(2,1)S(1)}, bf16[2,96,384]{2,1,0:T(8,128)(2,1)S(1)}, u32[]{:S(2)}, u32[]{:S(2)}) collective-permute-start(bf16[2,96,384]{2,1,0:T(8,128)(2,1)S(1)} %get-tuple-element.186), channel_id=1, source_target_pairs={{0,2},{2,0},{4,6},{6,4},{8,10},{10,8},{12,14},{14,12},{1,3},{3,1},... | collective-permute-start | bytes 442376 | tf_op jit(solution)/shard_map/ppermute | solution.py:440
  483.5 6.7 %collective-permute-start.29 = (bf16[1,96,384]{2,1,0:T(8,128)(2,1)S(1)}, bf16[1,96,384]{2,1,0:T(8,128)(2,1)S(1)}, u32[]{:S(2)}, u32[]{:S(2)}) collective-permute-start(bf16[1,96,384]{2,1,0:T(8,128)(2,1)S(1)} %get-tuple-element.163.refs_13_.refs_1_), channel_id=1, source_target_pairs={{0,8},{2,10},{4,12},{6,14},{8,0},{10,2},{12,4},{14,6},{1,9},{3,11}... | collective-permute-start | bytes 221192 | tf_op jit(solution)/shard_map/ppermute | solution.py:440
  490.7 5.2 collective-permute-start.53
  492.8 5.9 %collective-permute-start.52 = (bf16[2,96,384]{2,1,0:T(8,128)(2,1)S(1)}, bf16[2,96,384]{2,1,0:T(8,128)(2,1)S(1)}, u32[]{:S(2)}, u32[]{:S(2)}) collective-permute-start(bf16[2,96,384]{2,1,0:T(8,128)(2,1)S(1)} %get-tuple-element.169.refs_7_.refs_1_), channel_id=1, source_target_pairs={{0,4},{2,6},{4,0},{6,2},{8,12},{10,14},{12,8},{14,10},{1,5},{3,7},... | collective-permute-start | bytes 442376 | tf_op jit(solution)/shard_map/ppermute | solution.py:440
  492.9 37.8 %collective-permute-start.26 = (bf16[416,768]{1,0:T(8,128)(2,1)S(1)}, bf16[416,768]{1,0:T(8,128)(2,1)}, u32[]{:S(2)}, u32[]{:S(2)}) collective-permute-start(bf16[416,768]{1,0:T(8,128)(2,1)S(1)} %copy-done.28), channel_id=1, source_target_pairs={{0,16},{16,0},{1,17},{17,1},{2,18},{18,2},{3,19},{19,3},{4,20},{20... | collective-permute-start | bytes 1916936 | tf_op jit(solution)/shard_map/ppermute | solution.py:435
  495.9 6.6 %collective-permute-start.41 = (bf16[1,96,384]{2,1,0:T(8,128)(2,1)S(1)}, bf16[1,96,384]{2,1,0:T(8,128)(2,1)S(1)}, u32[]{:S(2)}, u32[]{:S(2)}) collective-permute-start(bf16[1,96,384]{2,1,0:T(8,128)(2,1)S(1)} %get-tuple-element.188), channel_id=1, source_target_pairs={{0,8},{2,10},{4,12},{6,14},{8,0},{10,2},{12,4},{14,6},{1,9},{3,11}... | collective-permute-start | bytes 221192 | tf_op jit(solution)/shard_map/ppermute | solution.py:440
  498.7 6.1 %collective-permute-start.42 = (bf16[1,96,384]{2,1,0:T(8,128)(2,1)S(1)}, bf16[1,96,384]{2,1,0:T(8,128)(2,1)S(1)}, u32[]{:S(2)}, u32[]{:S(2)}) collective-permute-start(bf16[1,96,384]{2,1,0:T(8,128)(2,1)S(1)} %get-tuple-element.190), channel_id=1, source_target_pairs={{0,8},{2,10},{4,12},{6,14},{8,0},{10,2},{12,4},{14,6},{1,9},{3,11}... | collective-permute-start | bytes 221192 | tf_op jit(solution)/shard_map/ppermute | solution.py:440
  502.6 23.9 %collective-permute-start.54 = (bf16[4,96,384]{2,1,0:T(8,128)(2,1)}, bf16[4,96,384]{2,1,0:T(8,128)(2,1)}, u32[]{:S(2)}, u32[]{:S(2)}) collective-permute-start(bf16[4,96,384]{2,1,0:T(8,128)(2,1)} %get-tuple-element.200.refs_1_), channel_id=1, source_target_pairs={{0,2},{2,0},{4,6},{6,4},{8,10},{10,8},{12,14},{14,12},{1,3},{3,1},... | collective-permute-start | bytes 884744 | tf_op jit(solution)/shard_map/ppermute | solution.py:440
  505.5 22.5 %collective-permute-start.55 = (bf16[4,96,384]{2,1,0:T(8,128)(2,1)}, bf16[4,96,384]{2,1,0:T(8,128)(2,1)}, u32[]{:S(2)}, u32[]{:S(2)}) collective-permute-start(bf16[4,96,384]{2,1,0:T(8,128)(2,1)} %get-tuple-element.201.refs_3_), channel_id=1, source_target_pairs={{0,4},{2,6},{4,0},{6,2},{8,12},{10,14},{12,8},{14,10},{1,5},{3,7},... | collective-permute-start | bytes 884744 | tf_op jit(solution)/shard_map/ppermute | solution.py:440
  507.6 12.4 %collective-permute-start.44 = (bf16[1,96,384]{2,1,0:T(8,128)(2,1)S(1)}, bf16[1,96,384]{2,1,0:T(8,128)(2,1)S(1)}, u32[]{:S(2)}, u32[]{:S(2)}) collective-permute-start(bf16[1,96,384]{2,1,0:T(8,128)(2,1)S(1)} %get-tuple-element.191.refs_1_), channel_id=1, source_target_pairs={{0,8},{2,10},{4,12},{6,14},{8,0},{10,2},{12,4},{14,6},{1,9},{3,11}... | collective-permute-start | bytes 221192 | tf_op jit(solution)/shard_map/ppermute | solution.py:440
  517.1 5.3 collective-permute-start.45
  522.9 10.4 %collective-permute-start.47 = (bf16[2,96,384]{2,1,0:T(8,128)(2,1)S(1)}, bf16[2,96,384]{2,1,0:T(8,128)(2,1)S(1)}, u32[]{:S(2)}, u32[]{:S(2)}) collective-permute-start(bf16[2,96,384]{2,1,0:T(8,128)(2,1)S(1)} %get-tuple-element.193.refs_1_), channel_id=1, source_target_pairs={{0,4},{2,6},{4,0},{6,2},{8,12},{10,14},{12,8},{14,10},{1,5},{3,7},... | collective-permute-start | bytes 442376 | tf_op jit(solution)/shard_map/ppermute | solution.py:440
  525.0 8.3 %collective-permute-start.48 = (bf16[2,96,384]{2,1,0:T(8,128)(2,1)S(1)}, bf16[2,96,384]{2,1,0:T(8,128)(2,1)S(1)}, u32[]{:S(2)}, u32[]{:S(2)}) collective-permute-start(bf16[2,96,384]{2,1,0:T(8,128)(2,1)S(1)} %get-tuple-element.194.refs_3_), channel_id=1, source_target_pairs={{0,2},{2,0},{4,6},{6,4},{8,10},{10,8},{12,14},{14,12},{1,3},{3,1},... | collective-permute-start | bytes 442376 | tf_op jit(solution)/shard_map/ppermute | solution.py:440
  526.5 32.5 %collective-permute-start.11 = (bf16[416,768]{1,0:T(8,128)(2,1)S(1)}, bf16[416,768]{1,0:T(8,128)(2,1)S(1)}, u32[]{:S(2)}, u32[]{:S(2)}) collective-permute-start(bf16[416,768]{1,0:T(8,128)(2,1)S(1)} %shard_map.163), channel_id=1, source_target_pairs={{0,16},{16,0},{1,17},{17,1},{2,18},{18,2},{3,19},{19,3},{4,20},{20... | collective-permute-start | bytes 1916936 | tf_op jit(solution)/shard_map/ppermute | solution.py:435
  530.7 52.1 %collective-permute-start.56 = (bf16[1536,384]{1,0:T(8,128)(2,1)}, bf16[1536,384]{1,0:T(8,128)(2,1)}, u32[]{:S(2)}, u32[]{:S(2)}) collective-permute-start(bf16[1536,384]{1,0:T(8,128)(2,1)} %bitcast.42), channel_id=1, source_target_pairs={{0,1},{1,0},{2,3},{3,2},{4,5},{5,4},{6,7},{7,6},{8,9},{9,8},{10,11... | collective-permute-start | bytes 3538952 | tf_op jit(solution)/shard_map/ppermute | solution.py:435
  533.9 10.0 %collective-permute-start.49 = (bf16[4,96,384]{2,1,0:T(8,128)(2,1)S(1)}, bf16[4,96,384]{2,1,0:T(8,128)(2,1)S(1)}, u32[]{:S(2)}, u32[]{:S(2)}) collective-permute-start(bf16[4,96,384]{2,1,0:T(8,128)(2,1)S(1)} %get-tuple-element.195.refs_1_), channel_id=1, source_target_pairs={{0,2},{2,0},{4,6},{6,4},{8,10},{10,8},{12,14},{14,12},{1,3},{3,1},... | collective-permute-start | bytes 884744 | tf_op jit(solution)/shard_map/ppermute | solution.py:440
  535.6 8.3 %collective-permute-start.50 = (bf16[4,96,384]{2,1,0:T(8,128)(2,1)S(1)}, bf16[4,96,384]{2,1,0:T(8,128)(2,1)S(1)}, u32[]{:S(2)}, u32[]{:S(2)}) collective-permute-start(bf16[4,96,384]{2,1,0:T(8,128)(2,1)S(1)} %get-tuple-element.196.refs_3_), channel_id=1, source_target_pairs={{0,4},{2,6},{4,0},{6,2},{8,12},{10,14},{12,8},{14,10},{1,5},{3,7},... | collective-permute-start | bytes 884744 | tf_op jit(solution)/shard_map/ppermute | solution.py:440
  537.1 8.6 %collective-permute-start.31 = (f32[2,10,768]{2,1,0:T(8,128)S(1)}, f32[2,10,768]{2,1,0:T(8,128)S(1)}, u32[]{:S(2)}, u32[]{:S(2)}) collective-permute-start(f32[2,10,768]{2,1,0:T(8,128)S(1)} %pad_maximum_fusion.6), channel_id=1, source_target_pairs={{0,2},{2,0},{4,6},{6,4},{8,10},{10,8},{12,14},{14,12},{1,3},{3,1},... | collective-permute-start | bytes 184328 | tf_op jit(solution)/shard_map/ppermute | solution.py:440
  545.7 37.0 %collective-permute-start.51 = (bf16[1536,384]{1,0:T(8,128)(2,1)}, bf16[1536,384]{1,0:T(8,128)(2,1)}, u32[]{:S(2)}, u32[]{:S(2)}) collective-permute-start(bf16[1536,384]{1,0:T(8,128)(2,1)} %bitcast.40), channel_id=1, source_target_pairs={{0,1},{1,0},{2,3},{3,2},{4,5},{5,4},{6,7},{7,6},{8,9},{9,8},{10,11... | collective-permute-start | bytes 3538952 | tf_op jit(solution)/shard_map/ppermute | solution.py:435
  545.8 5.3 collective-permute-start.32
  551.0 7.9 %collective-permute-start.33 = (f32[2,10,768]{2,1,0:T(8,128)S(1)}, f32[2,10,768]{2,1,0:T(8,128)S(1)}, u32[]{:S(2)}, u32[]{:S(2)}) collective-permute-start(f32[2,10,768]{2,1,0:T(8,128)S(1)} %fusion.7), channel_id=1, source_target_pairs={{0,8},{2,10},{4,12},{6,14},{8,0},{10,2},{12,4},{14,6},{1,9},{3,11}... | collective-permute-start | bytes 184328 | tf_op jit(solution)/shard_map/ppermute | solution.py:440
  558.9 4.5 collective-permute-start.34
  563.4 11.2 %collective-permute-start.35 = (f32[2,10,768]{2,1,0:T(8,128)S(1)}, f32[2,10,768]{2,1,0:T(8,128)S(1)}, u32[]{:S(2)}, u32[]{:S(2)}) collective-permute-start(f32[2,10,768]{2,1,0:T(8,128)S(1)} %add.32), channel_id=1, source_target_pairs={{0,16},{16,0},{1,17},{17,1},{2,18},{18,2},{3,19},{19,3},{4,20},{20... | collective-permute-start | bytes 184328 | tf_op jit(solution)/shard_map/ppermute | solution.py:435
  (113 other events, 843.3 us)

commit v3 on v2

--- a/solution.py
+++ b/solution.py
@@ -55,11 +55,9 @@
 ANY_SPEC = pl.BlockSpec(memory_space=pl.ANY)
 
 
-def call(body, outs, args, specs, scratch=(), flops=0, limit=40, deps=(), grid=(1,), alias=None):
+def call(body, outs, args, specs, scratch=(), micros=1.5, limit=40, deps=(), grid=(1,), alias=None):
     out_specs = [o[2] if len(o) > 2 else VMEM_SPEC for o in outs]
     outs = [jax.ShapeDtypeStruct(o[0], o[1]) for o in outs]
-    size = sum(o.size * o.dtype.itemsize for o in outs)
-    size += sum(a.size * a.dtype.itemsize for a in args)
     taken, last = len(args), len(args) + len(deps)
 
     def kernel(*refs):
@@ -74,7 +72,7 @@
         scratch_shapes=list(scratch),
         input_output_aliases=alias or {},
         compiler_params=pltpu.CompilerParams(vmem_limit_bytes=limit << 20),
-        cost_estimate=pl.CostEstimate(flops=flops, bytes_accessed=size, transcendentals=0),
+        cost_estimate=pl.CostEstimate(flops=1, bytes_accessed=int(micros * 1.8e6), transcendentals=0),
     )(*args, *deps)
 
 
@@ -426,8 +424,11 @@
         own_ref, got_ref, h_ref, gain_ref, g_ref, g_out_ref, gain_grad_ref = refs
     h_grad, gain_grad_ref[...] = norm_back(h_ref[...], gain_ref[0, 0:1, :], both(own_ref, got_ref))
     g = g_ref[...] + h_grad
-    g_out_ref[...] = g
+    if not pack:
+        for image in range(g.shape[0] // PAD):
+            g_out_ref[image * SEQ : (image + 1) * SEQ, :] = g[image * PAD : image * PAD + SEQ, :]
     if pack:
+        g_out_ref[...] = g
         send_ref[...] = mm(place_ref[0], g.astype(BF16)).astype(BF16)
 
 
@@ -438,6 +439,45 @@
 def partner(value, axis, bit):
     count = lax.axis_size(axis)
     return lax.ppermute(value, axis, [(i, i ^ (1 << bit)) for i in range(count)])
+
+
+def first_split_kernel(sides_ref, mine_ref, got_ref, *outs):
+    for i in range(2):
+        out_ref, send_ref = outs[2 * i], outs[2 * i + 1]
+        half = out_ref.shape[0]
+        side = sides_ref[i]
+        mine, other = pl.ds(side * half, half), pl.ds((1 - side) * half, half)
+        out_ref[...] = mine_ref[i, mine].astype(F32) + got_ref[i, mine].astype(F32)
+        send_ref[...] = (mine_ref[i, other].astype(F32) + got_ref[i, other].astype(F32)).astype(BF16)
+
+
+def last_join_kernel(sides_ref, own_a_ref, got_a_ref, own_b_ref, got_b_ref, out_ref):
+    for i, (own_ref, got_ref) in enumerate(((own_a_ref, got_a_ref), (own_b_ref, got_b_ref))):
+        half = own_ref.shape[0]
+        side = sides_ref[i]
+        out_ref[i, pl.ds(side * half, half)] = own_ref[...]
+        out_ref[i, pl.ds((1 - side) * half, half)] = got_ref[...]
+
+
+def layout_kernel(where_ref, mine_ref, got_ref, *refs):
+    qkv_ref, proj_ref = refs[-2:]
+    depth, width = qkv_ref.shape[2:]
+
+    def write(low_ref, high_ref):
+        qkv_ref[0, 0] = low_ref[0].astype(F32)
+        qkv_ref[0, 1] = low_ref[1].astype(F32)
+        qkv_ref[0, 2] = high_ref[0].astype(F32)
+        for c in range(depth // width):
+            rows = slice(c * width, (c + 1) * width)
+            proj_ref[0, :, rows] = high_ref[1, rows, :].astype(F32)
+
+    @pl.when(where_ref[2] == 0)
+    def _():
+        write(mine_ref, got_ref)
+
+    @pl.when(where_ref[2] == 1)
+    def _():
+        write(got_ref, mine_ref)
 
 
 def split_kernel(sides_ref, keep_a_ref, got_a_ref, keep_b_ref, got_b_ref, *outs):
@@ -473,7 +513,7 @@
         self.orders = list(zip(bits, [*bits[1::-1], *bits[2:]]))
         me = lax.axis_index("expert")
         self.sides = [jnp.stack([(me >> a) & 1, (me >> b) & 1]).astype(jnp.int32) for a, b in self.orders]
-        self.state = (mine[0], got[0], mine[1], got[1])
+        self.state = (mine, got)
         self.count, self.block, self.width = experts, block, width
         self.step = 0
 
@@ -484,10 +524,10 @@
         self.count //= 2
         a, b = self.orders[self.step]
         keep_a, send_a, keep_b, send_b = call(
-            split_kernel,
+            first_split_kernel if self.step == 0 else split_kernel,
             [(self.shape(), F32), (self.shape(), BF16)] * 2,
             (self.sides[self.step], *self.state),
-            [SMEM_SPEC] + [VMEM_SPEC] * 4,
+            [SMEM_SPEC] + [VMEM_SPEC] * len(self.state),
             deps=deps,
         )
         self.step += 1
@@ -509,8 +549,8 @@
         got_a, got_b = partner(own_a, "expert", a), partner(own_b, "expert", b)
         self.count *= 2
         self.state = call(
-            join_kernel,
-            [(self.shape(), BF16)] * 2,
+            join_kernel if self.step else last_join_kernel,
+            [(self.shape(), BF16)] * 2 if self.step else [((2, *self.shape()), BF16)],
             (self.sides[self.step], own_a, got_a, own_b, got_b),
             [SMEM_SPEC] + [VMEM_SPEC] * 4,
             deps=deps,
@@ -520,14 +560,14 @@
     def result(self):
         while self.step:
             self.join()
-        return jnp.concatenate(self.state).reshape(-1, self.width)
-
-
-def sum_all(value):
+        return self.state[0].reshape(2, -1, self.width)
+
+
+def sum_small(value):
+    value = value + swap(value, "replica")
     for bit in range(lax.axis_size("expert").bit_length() - 1):
         value = value + partner(value, "expert", bit)
-    value = value + swap(value, "replica")
-    return value + swap(value, "tensor")
+    return value
 
 
 def on_device(tokens, gains, attn_qkv, attn_out, router, expert_in, expert_out, routes, cotangent):
@@ -586,12 +626,10 @@
     def lines(size, shift=0):
         return pl.BlockSpec(size, lambda step: (step + shift, 0))
 
-    pack_flops = 2 * slots * rows * width
     weights = [pltpu.VMEM((4, width, part), BF16), pltpu.VMEM((4, part, width), BF16)]
     total = pltpu.VMEM((slots, width), F32)
     dots = pltpu.VMEM((slots, 1), F32)
     sems = pltpu.SemaphoreType.DMA((8,))
-    expert_flops = 8 * slots * width * hidden
     rows_out = ((slots, width), BF16)
     hidden_spec = columns((slots, part))
     hidden_out = ((slots, 2 * hidden), BF16, hidden_spec)
@@ -624,7 +662,7 @@
                 layer_spec((1, 3, width, local), layer),
                 layer_spec((1, local, width), layer),
             ],
-            flops=8 * rows * width * local + 4 * rows * PAD * local,
+            micros=5,
             deps=attend_deps,
         )
         if place is None:
@@ -633,7 +671,7 @@
                 [((layers, slots, rows), BF16), rows_out],
                 (where, routes_t, upstream),
                 [SMEM_SPEC, VMEM_SPEC, VMEM_SPEC],
-                flops=2 * layers * rows * rows * experts + pack_flops,
+                micros=1.5,
                 deps=(term,),
             )
             received_grad = exchange(send)
@@ -643,7 +681,7 @@
             (where, h, term, swap(term, "tensor"), gains, place, expert_out),
             [SMEM_SPEC] + [VMEM_SPEC] * 3 + [gain_spec(layer), place_spec(layer), ANY_SPEC],
             [pltpu.SemaphoreType.DMA((1,))],
-            flops=pack_flops,
+            micros=2,
         )
         whole = (expert_in, *whole_in, expert_out, *pair_of(piece))
         received = exchange(send)
@@ -656,7 +694,7 @@
                 (where, received, router_t[layer], *whole),
                 [SMEM_SPEC, VMEM_SPEC, VMEM_SPEC] + [ANY_SPEC] * 6,
                 [*weights, total, sems],
-                flops=expert_flops,
+                micros=13,
                 limit=56,
                 deps=(piece,),
                 grid=(4,),
@@ -667,16 +705,16 @@
                 [((rows, width), BF16)],
                 (place, returned),
                 [place_spec(layer), VMEM_SPEC],
-                flops=pack_flops,
+                micros=2,
             )
             stream_args = (mid, term, swap(term, "tensor"))
             saved.append((h, a, proj, mixed, mid, received, act, slope, whole))
         else:
             saved.append((h, a, proj, mixed, mid, received, None, None, whole))
 
-    small = [None] * layers
+    small, router_grads = [], []
     sums = [None] * layers
-    grad_in = grad_out = mixed_out = None
+    grad_in = grad_out = None
     finishers = []
     for layer in reversed(range(layers)):
         h, a, proj, mixed, mid, received, act, slope, whole = saved[layer]
@@ -688,7 +726,7 @@
                 (where, received_grad, received, router_t[layer], *whole),
                 [SMEM_SPEC] + [VMEM_SPEC] * 3 + [ANY_SPEC] * 6,
                 [*weights, total, total, dots, sems],
-                flops=2 * expert_flops,
+                micros=22,
                 limit=56,
                 grid=(4,),
             )
@@ -699,12 +737,16 @@
                 (where, received_grad, received, act, slope, router_t[layer], *whole),
                 [SMEM_SPEC, VMEM_SPEC, VMEM_SPEC, hidden_spec, hidden_spec, VMEM_SPEC] + [ANY_SPEC] * 6,
                 [*weights, total, dots, sems],
-                flops=expert_flops,
+                micros=13,
                 limit=56,
                 deps=(far[0], sums[last].split()),
                 grid=(4,),
             )
         returned = exchange(back)
+        router_grads.append(router_grad)
+        if layer == 0:
+            router_all = jnp.concatenate(router_grads)
+            router_all = router_all + swap(router_all, "tensor")
         if layer == last:
             term, reply = call(
                 unpack_pass_kernel,
@@ -712,7 +754,7 @@
                 (place, returned, reply),
                 [place_spec(layer), VMEM_SPEC, ANY_SPEC],
                 [pltpu.SemaphoreType.DMA((1,))],
-                flops=pack_flops,
+                micros=2,
             )
         else:
             [term] = call(
@@ -720,23 +762,30 @@
                 [((rows, width), BF16)],
                 (place, returned),
                 [place_spec(layer), VMEM_SPEC],
-                flops=pack_flops,
-                deps=(far[1], sums[last].split()),
-            )
+                micros=2,
+                deps=(far[1], sums[last].finish(), router_all),
+            )
+            finishers[0]((term,))
+            reply = exchange(reply)
         got = swap(term, "tensor")
-        in_other, out_other = call(
-            grad_other_kernel,
-            [
-                ((half, 2 * hidden), BF16, columns((half, part))),
-                ((2 * hidden, half), BF16, lines((part, half))),
-            ],
-            (where, received, scaled, pre_grad, act),
-            [SMEM_SPEC, VMEM_SPEC, VMEM_SPEC, hidden_spec, hidden_spec],
-            flops=4 * slots * hidden * width,
-            deps=(term,),
-            grid=(4,),
-        )
-        in_got, out_got = swap(in_other, "replica"), swap(out_other, "replica")
+        def other_core(dep):
+            in_other, out_other = call(
+                grad_other_kernel,
+                [
+                    ((half, 2 * hidden), BF16, columns((half, part))),
+                    ((2 * hidden, half), BF16, lines((part, half))),
+                ],
+                (where, received, scaled, pre_grad, act),
+                [SMEM_SPEC, VMEM_SPEC, VMEM_SPEC, hidden_spec, hidden_spec],
+                micros=5.5,
+                deps=(dep,),
+                grid=(4,),
+            )
+            return in_other, out_other
+
+        if layer == last:
+            in_other, out_other = other_core(term)
+
         upstream, gain_two, term, *weight_grads = call(
             attend_back_kernel,
             [
@@ -752,20 +801,12 @@
             + [VMEM_SPEC] * 4
             + [layer_spec((1, 3, width, local), layer), layer_spec((1, local, width), layer)],
             [pltpu.VMEM((3, rows, local), BF16), pltpu.VMEM((rows, local), BF16)],
-            flops=16 * rows * width * local + 10 * rows * PAD * local,
-            deps=(in_other, out_other) if layer == last else (in_other, out_other, sums[last].finish()),
-        )
-        if layer == last:
-            [done] = call(
-                unpack_kernel,
-                [((rows, width), BF16)],
-                (place, exchange(reply)),
-                [place_spec(layer), VMEM_SPEC],
-                flops=pack_flops,
-            )
-            done = done.astype(F32) + swap(done, "tensor").astype(F32)
-            mixed_out = gathered((mid + done).astype(BF16))
-
+            micros=32,
+            deps=(in_other, out_other) if layer == last else (grad_in,),
+        )
+        if layer < last:
+            in_other, out_other = other_core(term)
+        in_got, out_got = swap(in_other, "replica"), swap(out_other, "replica")
         mine, other = weight_grads
         sums[layer] = ExpertSum(mine, swap(other, "replica"), experts)
         got = swap(term, "tensor")
@@ -785,8 +826,8 @@
                 columns((half, part), 2),
                 lines((part, half), 2),
             ],
-            flops=2 * slots * hidden * width,
-            deps=(term,),
+            micros=4.5,
+            deps=(term,) if layer else (got,),
             grid=(2,),
         )
         if layer > 0:
@@ -795,21 +836,19 @@
                 [((rows, width), F32), ((1, width), F32), rows_out],
                 (term, got, h, gains, upstream, place),
                 [VMEM_SPEC] * 3 + [gain_spec(layer), VMEM_SPEC, place_spec(layer - 1)],
-                flops=pack_flops,
+                micros=2,
                 deps=(in_far, out_far, sums[last].split()),
             )
             received_grad = exchange(send)
         else:
             upstream, gain_one = call(
                 functools.partial(stream_back_kernel, False),
-                [((rows, width), F32), ((1, width), F32)],
+                [((row_count, width), F32), ((1, width), F32)],
                 (term, got, h, gains, upstream),
                 [VMEM_SPEC] * 3 + [gain_spec(layer), VMEM_SPEC],
-                deps=(in_far, out_far, sums[last].join()),
             )
         in_far, out_far = far = swap(in_far, "tensor"), swap(out_far, "tensor")
-        gain_pair = jnp.where(side == 0, jnp.concatenate([gain_one, gain_two]), 0.0)
-        small[layer] = jnp.concatenate([router_grad, gain_pair])
+        small.append(jnp.concatenate([gain_one, gain_two]))
 
         def finish_own(deps, layer=layer, args=(where, received, scaled, pre_grad, act, in_got, out_got, in_far, out_far)):
             nonlocal grad_in, grad_out
@@ -841,7 +880,7 @@
                     lines((part, half)),
                     *([ANY_SPEC] * len(stacked)),
                 ],
-                flops=2 * slots * hidden * width,
+                micros=4.5,
                 deps=deps,
                 grid=(2,),
                 alias={9: 0, 10: 1} if stacked else None,
@@ -849,30 +888,49 @@
 
         finishers.append(finish_own)
 
-    finishers[0]((term,))
     finishers[1]((upstream,))
 
-    grad_qkv, grad_proj = [], []
-    for layer in range(layers):
+    [done] = call(
+        unpack_kernel,
+        [((rows, width), BF16)],
+        (place, reply),
+        [place_spec(last), VMEM_SPEC],
+        micros=2,
+        deps=(sums[0].split(),),
+    )
+    done = done.astype(F32) + swap(done, "tensor").astype(F32)
+    mixed_out = gathered((saved[last][4] + done).astype(BF16))
+    small = sum_small(jnp.concatenate([router_all, *small]))
+
+    stacked = ()
+    for layer in reversed(range(layers)):
         if layer < last:
+            sums[layer].split((gain_one,))
             sums[layer].finish(far[:1])
-            sums[layer].join(far[1:])
+            sums[layer].join()
+            sums[layer].join((far[1], small, mixed_out))
         mine = sums[layer].result()
-        got = swap(mine, "replica")
-        lower = jnp.where(core == 0, mine, got).astype(F32)
-        upper = jnp.where(core == 0, got, mine).astype(F32)
-        grad_qkv.append(jnp.concatenate([lower, upper[:width]]).reshape(3, width, local))
-        grad_proj.append(
-            jnp.concatenate([upper[width : width + local], upper[width + local :]], axis=1)
-        )
-    small = sum_all(jnp.stack(small))
+        stacked = call(
+            layout_kernel,
+            [
+                ((layers, 3, width, local), F32, layer_spec((1, 3, width, local), layer)),
+                ((layers, local, width), F32, layer_spec((1, local, width), layer)),
+            ],
+            (where, mine, swap(mine, "replica"), *stacked),
+            [SMEM_SPEC, VMEM_SPEC, VMEM_SPEC] + [ANY_SPEC] * len(stacked),
+            micros=2,
+            alias={3: 0, 4: 1} if stacked else None,
+        )
+    grad_qkv, grad_proj = stacked
+    router_all = small[: layers * experts].reshape(layers, experts, width)[::-1]
+    small = small[layers * experts :].reshape(layers, 2, width)[::-1]
     return (
         mixed_out,
-        gathered(upstream),
-        small[:, experts:],
-        jnp.stack(grad_qkv),
-        jnp.stack(grad_proj),
-        jnp.swapaxes(small[:, :experts], 1, 2),
+        upstream,
+        small,
+        grad_qkv,
+        grad_proj,
+        jnp.swapaxes(router_all, 1, 2),
         grad_in[:, None],
         grad_out[:, None],
     )

time: 601 us -> 587 us (0.977)
  Pallas kernels: 145 us -> 158 us
  other arithmetic: 12.8 us -> 1.46 us
  starting transfers between devices: 109 us -> 100 us
  local copies, waits for them, and re-layouts: 77.4 us -> 69.9 us
    pallas_call x38 -> x40, Pallas kernels: 145 us -> 158 us  [call(): pl.pallas_call(kernel, grid=grid, out_shape=outs, in_specs=[*specs, *[ANY...]
    ppermute x27, starting transfers between devices: 44.5 us -> 36.2 us  [partner(): return lax.ppermute(value, axis, [(i, i ^ 1 << bit) for i in range(count)])]
    unnamed x226 -> x241, local copies, waits for them, and re-layouts: 59.5 us -> 61.1 us
  transfers between devices with their start and end apart: 64 -> 64, of which waited for: 33 -> 36; matrix products, arithmetic and copies ran while one was open for 3% -> 2% of each run, Pallas kernels for 12% -> 11%
where the time goes in v3:
time: 587 us; the launch traced here: 578 us
  waiting for transfers between devices  220 us (37%)
  Pallas kernels  158 us (27%)
  starting transfers between devices  100 us (17%)
  local copies, waits for them, and re-layouts  69.9 us (12%)
  blocking collectives  26.2 us (4%)
    pallas_call x40, Pallas kernels, call(): pl.pallas_call(kernel, grid=grid, out_shape=outs, in_specs=[*specs, *[ANY...  158 us
    ppermute x30, waiting for transfers between devices, swap(): return lax.ppermute(value, axis, [(0, 1), (1, 0)])  132 us
    ppermute x27, waiting for transfers between devices, partner(): return lax.ppermute(value, axis, [(i, i ^ 1 << bit) for i in range(count)])  67.4 us
    unnamed x241, local copies, waits for them, and re-layouts  61.1 us
    all_to_all x7, starting transfers between devices, exchange(): lax.all_to_all(block, 'expert', 0, 0, tiled=True).reshape(slots, width)  38 us
    ppermute x27, starting transfers between devices, partner(): return lax.ppermute(value, axis, [(i, i ^ 1 << bit) for i in range(count)])  36.2 us
    all_to_all x1, blocking collectives, exchange(): lax.all_to_all(block, 'expert', 0, 0, tiled=True).reshape(slots, width)  26.2 us
    ppermute x30, starting transfers between devices, swap(): return lax.ppermute(value, axis, [(0, 1), (1, 0)])  26 us
  transfers between devices with their start and end apart: 64, of which 36 were waited for; matrix products, arithmetic and copies ran while one was open for 2% of the time, Pallas kernels for 11%

profile of v3, /device:TPU:0, one launch (start us, length us, event | category | flops | bytes accessed | tf_op | source)
XLA Modules:
  0.0 578.2 jit_solution(17546676088852422046)
XLA Ops:
  4.1 4.3 shard_map.152
  10.9 2.9 collective-permute-start
  13.9 2.3 copy-done.2
  22.9 6.1 %collective-permute-done.refs_3_ = bf16[416,768]{1,0:T(8,128)(2,1)S(1)} collective-permute-done((bf16[416,768]{1,0:T(8,128)(2,1)S(1)}, bf16[416,768]{1,0:T(8,128)(2,1)S(1)}, u32[]{:S(2)}, u32[]{:S(2)}) %collective-permute-start) | collective-permute-done | bytes 639008 | tf_op jit(solution)/shard_map/ppermute | solution.py:436
  29.1 2.3 copy-done
  31.4 3.3 shard_map.154
  35.8 2.1 collective-permute-start.3
  37.9 5.8 %all-to-all-start = ((bf16[8,64,768]{2,1,0:T(8,128)(2,1)}), bf16[8,64,768]{2,1,0:T(8,128)(2,1)S(1)}, u32[]{:S(2)}, u32[]{:S(2)}) async-start(bf16[8,64,768]{2,1,0:T(8,128)(2,1)} %bitcast.6), calls=%async_computation | async-start | bytes 1572864 | tf_op jit(solution)/shard_map/all_to_all | solution.py:600
  43.7 10.7 %collective-permute-done.1.refs_4_.refs_7_ = bf16[768,768]{1,0:T(8,128)(2,1)} collective-permute-done((bf16[768,768]{1,0:T(8,128)(2,1)}, bf16[768,768]{1,0:T(8,128)(2,1)}, u32[]{:S(2)}, u32[]{:S(2)}) %collective-permute-start.1) | collective-permute-done | bytes 1179680 | tf_op jit(solution)/shard_map/ppermute | solution.py:436
  54.4 24.3 %collective-permute-done.3.refs_7_.refs_10_ = bf16[768,768]{1,0:T(8,128)(2,1)S(1)} collective-permute-done((bf16[768,768]{1,0:T(8,128)(2,1)}, bf16[768,768]{1,0:T(8,128)(2,1)S(1)}, u32[]{:S(2)}, u32[]{:S(2)}) %collective-permute-start.3) | collective-permute-done | bytes 1179680 | tf_op jit(solution)/shard_map/ppermute | solution.py:436
  79.5 2.6 copy-done.3
  84.8 13.1 %shard_map.157 = (bf16[512,768]{1,0:T(8,128)(2,1)}, bf16[512,3072]{1,0:T(8,128)(2,1)}, bf16[512,3072]{1,0:T(8,128)(2,1)}) custom-call(s32[3]{0:T(128)} %copy-done.88, bf16[512,768]{1,0:T(8,128)(2,1)} %bitcast.48, bf16[8,768]{1,0:T(8,128)(2,1)} %get-tuple-element.225.refs_2_.refs_5_, bf16[2,1,768,1536]{3,2,1,0:T(8,128)(2,1)} %refs_6_.7, ...), custom_call_target="tpu_custom_call" | custom-call | flops 1 | bytes 23400000 | tf_op jit(solution)/shard_map/pallas_call | solution.py:66
  97.9 6.6 %all-to-all-start.1 = ((bf16[8,64,768]{2,1,0:T(8,128)(2,1)}), bf16[8,64,768]{2,1,0:T(8,128)(2,1)}, u32[]{:S(2)}, u32[]{:S(2)}) async-start(bf16[8,64,768]{2,1,0:T(8,128)(2,1)} %bitcast.72), calls=%async_computation.1 | async-start | bytes 1572864 | tf_op jit(solution)/shard_map/all_to_all | solution.py:600
  106.1 19.2 %all-to-all-done.1 = bf16[8,64,768]{2,1,0:T(8,128)(2,1)} async-done(((bf16[8,64,768]{2,1,0:T(8,128)(2,1)}), bf16[8,64,768]{2,1,0:T(8,128)(2,1)}, u32[]{:S(2)}, u32[]{:S(2)}) %all-to-all-start.1) | async-done | bytes 786464 | tf_op jit(solution)/shard_map/all_to_all | solution.py:600
  129.8 3.9 collective-permute-done.6.refs_6_.refs_5_
  133.7 12.8 %collective-permute-done.5.refs_2_ = bf16[416,768]{1,0:T(8,128)(2,1)S(1)} collective-permute-done((bf16[416,768]{1,0:T(8,128)(2,1)S(1)}, bf16[416,768]{1,0:T(8,128)(2,1)S(1)}, u32[]{:S(2)}, u32[]{:S(2)}) %collective-permute-start.5) | collective-permute-done | bytes 639008 | tf_op jit(solution)/shard_map/ppermute | solution.py:436
  149.1 5.2 shard_map.159
  159.4 5.7 all-to-all-start.2
  165.1 8.6 %collective-permute-done.7.refs_3_ = bf16[416,768]{1,0:T(8,128)(2,1)S(1)} collective-permute-done((bf16[416,768]{1,0:T(8,128)(2,1)}, bf16[416,768]{1,0:T(8,128)(2,1)S(1)}, u32[]{:S(2)}, u32[]{:S(2)}) %collective-permute-start.7) | collective-permute-done | bytes 639008 | tf_op jit(solution)/shard_map/ppermute | solution.py:436
  173.8 2.3 copy-done.1
  177.4 3.2 shard_map.160
  184.4 4.2 all-to-all-start.3
  188.6 19.6 %collective-permute-done.9.refs_8_ = bf16[768,768]{1,0:T(8,128)(2,1)} collective-permute-done((bf16[768,768]{1,0:T(8,128)(2,1)S(1)}, bf16[768,768]{1,0:T(8,128)(2,1)}, u32[]{:S(2)}, u32[]{:S(2)}) %collective-permute-start.9) | collective-permute-done | bytes 1179680 | tf_op jit(solution)/shard_map/ppermute | solution.py:436
  208.2 3.0 collective-permute-done.10.refs_9_
  212.3 22.2 %shard_map.161 = (bf16[512,768]{1,0:T(8,128)(2,1)}, bf16[512,768]{1,0:T(8,128)(2,1)}, bf16[512,3072]{1,0:T(8,128)(2,1)}, bf16[512,3072]{1,0:T(8,128)(2,1)}, bf16[512,768]{1,0:T(8,128)(2,1)}, /*index=5*/f32[8,768]{1,0:T(8,128)}) custom-call(s32[3]{0:T(128)} %copy-done.88, bf16[512,768]{1,0:T(8,128)(2,1)} %bitcast.13.refs_1_, bf16[512,768]{1,0:T(8,128)(2,1)} %bitcast.53, ...), custom_call_target="tpu_custom_call" | custom-call | flops 1 | bytes 39600000 | tf_op jit(solution)/shard_map/pallas_call | solution.py:66
  234.5 26.2 %all_to_all.40 = bf16[8,64,768]{2,1,0:T(8,128)(2,1)S(1)} all-to-all(bf16[8,64,768]{2,1,0:T(8,128)(2,1)} %bitcast.71), channel_id=1, replica_groups=mesh['tensor'=2,'expert'=8,'replica'=2] {'expert'}, dimensions={0} | all-to-all | bytes 1572864 | tf_op jit(solution)/shard_map/all_to_all | solution.py:600
  266.4 5.6 shard_map.163
  274.0 14.8 %collective-permute-done.11.refs_2_ = bf16[416,768]{1,0:T(8,128)(2,1)S(1)} collective-permute-done((bf16[416,768]{1,0:T(8,128)(2,1)S(1)}, bf16[416,768]{1,0:T(8,128)(2,1)S(1)}, u32[]{:S(2)}, u32[]{:S(2)}) %collective-permute-start.11) | collective-permute-done | bytes 639008 | tf_op jit(solution)/shard_map/ppermute | solution.py:436
  288.8 14.3 %shard_map.164 = (f32[416,768]{1,0:T(8,128)S(1)}, f32[1,768]{1,0:T(1,128)S(1)}, bf16[416,768]{1,0:T(8,128)(2,1)}, bf16[1536,384]{1,0:T(8,128)(2,1)S(1)}, bf16[1536,384]{1,0:T(8,128)(2,1)}) custom-call(s32[3]{0:T(128)S(1)} %copy-done.90, bf16[416,768]{1,0:T(8,128)(2,1)S(1)} %get-tuple-element.124.refs_5_.refs_1_, ...), custom_call_target="tpu_custom_call" | custom-call | flops 1 | bytes 57600000 | tf_op jit(solution)/shard_map/pallas_call | solution.py:66
  315.7 3.6 shard_map.165
  319.3 3.1 collective-permute-done.12.refs_1_
  322.4 2.7 shard_map.167
  327.1 4.2 all-to-all-start.6
  336.3 12.3 %collective-permute-done.17.refs_2_ = bf16[4,96,384]{2,1,0:T(8,128)(2,1)S(1)} collective-permute-done((bf16[4,96,384]{2,1,0:T(8,128)(2,1)S(1)}, bf16[4,96,384]{2,1,0:T(8,128)(2,1)S(1)}, u32[]{:S(2)}, u32[]{:S(2)}) %collective-permute-start.17) | collective-permute-done | bytes 294944 | tf_op jit(solution)/shard_map/ppermute | solution.py:441
  348.6 4.1 collective-permute-done.18.refs_4_
  359.3 14.5 %shard_map.169 = (bf16[512,768]{1,0:T(8,128)(2,1)}, bf16[512,3072]{1,0:T(8,128)(2,1)}, bf16[512,768]{1,0:T(8,128)(2,1)}, f32[8,768]{1,0:T(8,128)}) custom-call(s32[3]{0:T(128)} %copy-done.88, bf16[512,768]{1,0:T(8,128)(2,1)} %bitcast.26.refs_1_, bf16[512,768]{1,0:T(8,128)(2,1)} %bitcast.49, bf16[512,3072]{1,0:T(8,128)(2,1)} %get-tuple-element.141.refs_3_.refs_4_, ...), custom_call_target="tpu_custom_call" | custom-call | flops 1 | bytes 23400000 | tf_op jit(solution)/shard_map/pallas_call | solution.py:66
  373.8 6.0 %all-to-all-start.7 = ((bf16[8,64,768]{2,1,0:T(8,128)(2,1)}), bf16[8,64,768]{2,1,0:T(8,128)(2,1)}, u32[]{:S(2)}, u32[]{:S(2)}) async-start(bf16[8,64,768]{2,1,0:T(8,128)(2,1)} %bitcast.70), calls=%async_computation.7 | async-start | bytes 1572864 | tf_op jit(solution)/shard_map/all_to_all | solution.py:600
  381.3 2.0 collective-permute-start.20
  384.9 9.6 %collective-permute-done.20.refs_2_ = bf16[2,96,384]{2,1,0:T(8,128)(2,1)S(1)} collective-permute-done((bf16[2,96,384]{2,1,0:T(8,128)(2,1)S(1)}, bf16[2,96,384]{2,1,0:T(8,128)(2,1)S(1)}, u32[]{:S(2)}, u32[]{:S(2)}) %collective-permute-start.20) | collective-permute-done | bytes 147488 | tf_op jit(solution)/shard_map/ppermute | solution.py:441
  396.1 4.7 collective-permute-start.22
  404.0 2.0 collective-permute-done.23.refs_3_
  411.8 5.0 shard_map.173
  416.8 6.1 %collective-permute-done.25.refs_2_ = bf16[416,768]{1,0:T(8,128)(2,1)S(1)} collective-permute-done((bf16[416,768]{1,0:T(8,128)(2,1)S(1)}, bf16[416,768]{1,0:T(8,128)(2,1)S(1)}, u32[]{:S(2)}, u32[]{:S(2)}) %collective-permute-start.25) | collective-permute-done | bytes 639008 | tf_op jit(solution)/shard_map/ppermute | solution.py:436
  423.0 14.3 %shard_map.174 = (f32[416,768]{1,0:T(8,128)S(1)}, f32[1,768]{1,0:T(1,128)S(1)}, bf16[416,768]{1,0:T(8,128)(2,1)S(1)}, bf16[1536,384]{1,0:T(8,128)(2,1)S(1)}, bf16[1536,384]{1,0:T(8,128)(2,1)}) custom-call(s32[3]{0:T(128)S(1)} %copy-done.91, bf16[416,768]{1,0:T(8,128)(2,1)S(1)} %shard_map.172.refs_9_.refs_1_, ...), custom_call_target="tpu_custom_call" | custom-call | flops 1 | bytes 57600000 | tf_op jit(solution)/shard_map/pallas_call | solution.py:66
  439.3 5.5 shard_map.180
  445.5 5.4 all-to-all-start.5
  452.5 15.2 %collective-permute-done.28.refs_1_.refs_7_ = bf16[416,768]{1,0:T(8,128)(2,1)S(1)} collective-permute-done((bf16[416,768]{1,0:T(8,128)(2,1)}, bf16[416,768]{1,0:T(8,128)(2,1)S(1)}, u32[]{:S(2)}, u32[]{:S(2)}) %collective-permute-start.28) | collective-permute-done | bytes 639008 | tf_op jit(solution)/shard_map/ppermute | solution.py:436
  469.5 4.4 shard_map.181
  480.4 2.4 collective-permute-start.50
  483.3 3.6 collective-permute-done.50.refs_2_
  486.9 3.4 collective-permute-start.51
  490.4 2.3 collective-permute-done.51.refs_4_
  493.9 3.0 collective-permute-start.52
  496.9 2.0 shard_map.177
  518.0 4.8 collective-permute-done.37.refs_1_
  523.7 2.1 collective-permute-start.31
  525.8 3.8 collective-permute-done.54.refs_2_
  529.6 5.0 collective-permute-done.31
  534.9 2.6 collective-permute-start.32
  546.0 2.2 collective-permute-done.44.refs_2_
  550.9 7.5 %collective-permute-done.47.refs_2_ = bf16[4,96,384]{2,1,0:T(8,128)(2,1)S(1)} collective-permute-done((bf16[4,96,384]{2,1,0:T(8,128)(2,1)S(1)}, bf16[4,96,384]{2,1,0:T(8,128)(2,1)S(1)}, u32[]{:S(2)}, u32[]{:S(2)}) %collective-permute-start.47) | collective-permute-done | bytes 294944 | tf_op jit(solution)/shard_map/ppermute | solution.py:441
  560.1 4.1 shard_map.189
  568.7 4.9 shard_map.191
  573.6 4.1 shard_map.190
  (373 shorter events, 136.0 us)
Async XLA Ops:
  10.9 18.2 %collective-permute-start = (bf16[416,768]{1,0:T(8,128)(2,1)S(1)}, bf16[416,768]{1,0:T(8,128)(2,1)S(1)}, u32[]{:S(2)}, u32[]{:S(2)}) collective-permute-start(bf16[416,768]{1,0:T(8,128)(2,1)S(1)} %get-tuple-element.109.refs_3_.refs_2_), channel_id=1, source_target_pairs={{0,16},{16,0},{1,17},{17,1},{2,18},{18,2},{3,19},{19,3},{4,20},{20... | collective-permute-start | bytes 1916936 | tf_op jit(solution)/shard_map/ppermute | solution.py:436
  17.8 36.6 %collective-permute-start.1 = (bf16[768,768]{1,0:T(8,128)(2,1)}, bf16[768,768]{1,0:T(8,128)(2,1)}, u32[]{:S(2)}, u32[]{:S(2)}) collective-permute-start(bf16[768,768]{1,0:T(8,128)(2,1)} %shard_map.155), channel_id=1, source_target_pairs={{0,16},{16,0},{1,17},{17,1},{2,18},{18,2},{3,19},{19,3},{4,20},{20... | collective-permute-start | bytes 3538952 | tf_op jit(solution)/shard_map/ppermute | solution.py:436
  35.8 43.0 %collective-permute-start.3 = (bf16[768,768]{1,0:T(8,128)(2,1)}, bf16[768,768]{1,0:T(8,128)(2,1)S(1)}, u32[]{:S(2)}, u32[]{:S(2)}) collective-permute-start(bf16[768,768]{1,0:T(8,128)(2,1)} %get-tuple-element.113), channel_id=1, source_target_pairs={{0,16},{16,0},{1,17},{17,1},{2,18},{18,2},{3,19},{19,3},{4,20},{20... | collective-permute-start | bytes 3538952 | tf_op jit(solution)/shard_map/ppermute | solution.py:436
  37.9 41.6 %all-to-all-start = ((bf16[8,64,768]{2,1,0:T(8,128)(2,1)}), bf16[8,64,768]{2,1,0:T(8,128)(2,1)S(1)}, u32[]{:S(2)}, u32[]{:S(2)}) async-start(bf16[8,64,768]{2,1,0:T(8,128)(2,1)} %bitcast.6), calls=%async_computation | async-start | bytes 1572864 | tf_op jit(solution)/shard_map/all_to_all | solution.py:600
  54.4 29.3 %collective-permute-start.2 = (bf16[768,768]{1,0:T(8,128)(2,1)}, bf16[768,768]{1,0:T(8,128)(2,1)S(1)}, u32[]{:S(2)}, u32[]{:S(2)}) collective-permute-start(bf16[768,768]{1,0:T(8,128)(2,1)} %collective-permute-done.1.refs_4_.refs_7_), channel_id=1, source_target_pairs={{0,1},{1,0},{2,3},{3,2},{4,5},{5,4},{6,7},{7,6},{8,9},{9,8},{10,11... | collective-permute-start | bytes 3538952 | tf_op jit(solution)/shard_map/ppermute | solution.py:436
  78.8 5.0 collective-permute-start.4
  97.9 27.4 %all-to-all-start.1 = ((bf16[8,64,768]{2,1,0:T(8,128)(2,1)}), bf16[8,64,768]{2,1,0:T(8,128)(2,1)}, u32[]{:S(2)}, u32[]{:S(2)}) async-start(bf16[8,64,768]{2,1,0:T(8,128)(2,1)} %bitcast.72), calls=%async_computation.1 | async-start | bytes 1572864 | tf_op jit(solution)/shard_map/all_to_all | solution.py:600
  104.5 29.2 %collective-permute-start.6 = (bf16[768,768]{1,0:T(8,128)(2,1)}, bf16[768,768]{1,0:T(8,128)(2,1)}, u32[]{:S(2)}, u32[]{:S(2)}) collective-permute-start(bf16[768,768]{1,0:T(8,128)(2,1)} %copy-done.42), channel_id=1, source_target_pairs={{0,16},{16,0},{1,17},{17,1},{2,18},{18,2},{3,19},{19,3},{4,20},{20... | collective-permute-start | bytes 3538952 | tf_op jit(solution)/shard_map/ppermute | solution.py:436
  128.2 18.3 %collective-permute-start.5 = (bf16[416,768]{1,0:T(8,128)(2,1)S(1)}, bf16[416,768]{1,0:T(8,128)(2,1)S(1)}, u32[]{:S(2)}, u32[]{:S(2)}) collective-permute-start(bf16[416,768]{1,0:T(8,128)(2,1)S(1)} %shard_map.158.refs_1_), channel_id=1, source_target_pairs={{0,16},{16,0},{1,17},{17,1},{2,18},{18,2},{3,19},{19,3},{4,20},{20... | collective-permute-start | bytes 1916936 | tf_op jit(solution)/shard_map/ppermute | solution.py:436
  157.9 15.8 %collective-permute-start.7 = (bf16[416,768]{1,0:T(8,128)(2,1)}, bf16[416,768]{1,0:T(8,128)(2,1)S(1)}, u32[]{:S(2)}, u32[]{:S(2)}) collective-permute-start(bf16[416,768]{1,0:T(8,128)(2,1)} %get-tuple-element.116.refs_2_), channel_id=1, source_target_pairs={{0,16},{16,0},{1,17},{17,1},{2,18},{18,2},{3,19},{19,3},{4,20},{20... | collective-permute-start | bytes 1916936 | tf_op jit(solution)/shard_map/ppermute | solution.py:436
  159.4 25.0 %all-to-all-start.2 = ((bf16[8,64,768]{2,1,0:T(8,128)(2,1)}), bf16[8,64,768]{2,1,0:T(8,128)(2,1)}, u32[]{:S(2)}, u32[]{:S(2)}) async-start(bf16[8,64,768]{2,1,0:T(8,128)(2,1)} %bitcast.65), calls=%async_computation.2 | async-start | bytes 1572864 | tf_op jit(solution)/shard_map/all_to_all | solution.py:600
  181.7 26.5 %collective-permute-start.9 = (bf16[768,768]{1,0:T(8,128)(2,1)S(1)}, bf16[768,768]{1,0:T(8,128)(2,1)}, u32[]{:S(2)}, u32[]{:S(2)}) collective-permute-start(bf16[768,768]{1,0:T(8,128)(2,1)S(1)} %get-tuple-element.120), channel_id=1, source_target_pairs={{0,16},{16,0},{1,17},{17,1},{2,18},{18,2},{3,19},{19,3},{4,20},{20... | collective-permute-start | bytes 3538952 | tf_op jit(solution)/shard_map/ppermute | solution.py:436
  184.4 23.8 %all-to-all-start.3 = ((bf16[8,64,768]{2,1,0:T(8,128)(2,1)}), bf16[8,64,768]{2,1,0:T(8,128)(2,1)S(1)}, u32[]{:S(2)}, u32[]{:S(2)}) async-start(bf16[8,64,768]{2,1,0:T(8,128)(2,1)} %bitcast.14), calls=%async_computation.3 | async-start | bytes 1572864 | tf_op jit(solution)/shard_map/all_to_all | solution.py:600
  188.6 19.6 %collective-permute-start.8 = (bf16[768,768]{1,0:T(8,128)(2,1)}, bf16[768,768]{1,0:T(8,128)(2,1)}, u32[]{:S(2)}, u32[]{:S(2)}) collective-permute-start(bf16[768,768]{1,0:T(8,128)(2,1)} %collective-permute-done.6.refs_6_.refs_5_), channel_id=1, source_target_pairs={{0,1},{1,0},{2,3},{3,2},{4,5},{5,4},{6,7},{7,6},{8,9},{9,8},{10,11... | collective-permute-start | bytes 3538952 | tf_op jit(solution)/shard_map/ppermute | solution.py:436
  208.2 3.1 collective-permute-start.10
  272.0 41.8 %collective-permute-start.13 = (bf16[384,3072]{1,0:T(8,128)(2,1)}, bf16[384,3072]{1,0:T(8,128)(2,1)}, u32[]{:S(2)}, u32[]{:S(2)}) collective-permute-start(bf16[384,3072]{1,0:T(8,128)(2,1)} %get-tuple-element.131.refs_11_), channel_id=1, source_target_pairs={{0,1},{1,0},{2,3},{3,2},{4,5},{5,4},{6,7},{7,6},{8,9},{9,8},{10,11... | collective-permute-start | bytes 7077896 | tf_op jit(solution)/shard_map/ppermute | solution.py:436
  272.0 41.8 %collective-permute-start.14 = (bf16[3072,384]{1,0:T(8,128)(2,1)}, bf16[3072,384]{1,0:T(8,128)(2,1)}, u32[]{:S(2)}, u32[]{:S(2)}) collective-permute-start(bf16[3072,384]{1,0:T(8,128)(2,1)} %get-tuple-element.132.refs_12_), channel_id=1, source_target_pairs={{0,1},{1,0},{2,3},{3,2},{4,5},{5,4},{6,7},{7,6},{8,9},{9,8},{10,11... | collective-permute-start | bytes 7077896 | tf_op jit(solution)/shard_map/ppermute | solution.py:436
  272.5 16.3 %collective-permute-start.11 = (bf16[416,768]{1,0:T(8,128)(2,1)S(1)}, bf16[416,768]{1,0:T(8,128)(2,1)S(1)}, u32[]{:S(2)}, u32[]{:S(2)}) collective-permute-start(bf16[416,768]{1,0:T(8,128)(2,1)S(1)} %get-tuple-element.124.refs_5_.refs_1_), channel_id=1, source_target_pairs={{0,16},{16,0},{1,17},{17,1},{2,18},{18,2},{3,19},{19,3},{4,20},{20... | collective-permute-start | bytes 1916936 | tf_op jit(solution)/shard_map/ppermute | solution.py:436
  305.3 3.2 collective-permute-start.15
  305.3 17.1 %collective-permute-start.12 = (bf16[416,768]{1,0:T(8,128)(2,1)}, bf16[416,768]{1,0:T(8,128)(2,1)}, u32[]{:S(2)}, u32[]{:S(2)}) collective-permute-start(bf16[416,768]{1,0:T(8,128)(2,1)} %get-tuple-element.133.refs_7_.refs_0_), channel_id=1, source_target_pairs={{0,16},{16,0},{1,17},{17,1},{2,18},{18,2},{3,19},{19,3},{4,20},{20... | collective-permute-start | bytes 1916936 | tf_op jit(solution)/shard_map/ppermute | solution.py:436
  327.1 32.2 %all-to-all-start.6 = ((bf16[8,64,768]{2,1,0:T(8,128)(2,1)}), bf16[8,64,768]{2,1,0:T(8,128)(2,1)}, u32[]{:S(2)}, u32[]{:S(2)}) async-start(bf16[8,64,768]{2,1,0:T(8,128)(2,1)} %bitcast.66), calls=%async_computation.6 | async-start | bytes 1572864 | tf_op jit(solution)/shard_map/all_to_all | solution.py:600
  331.3 28.0 %collective-permute-start.16 = (bf16[384,1536]{1,0:T(8,128)(2,1)}, bf16[384,1536]{1,0:T(8,128)(2,1)}, u32[]{:S(2)}, u32[]{:S(2)}) collective-permute-start(bf16[384,1536]{1,0:T(8,128)(2,1)} %copy-done.58), channel_id=1, source_target_pairs={{0,16},{16,0},{1,17},{17,1},{2,18},{18,2},{3,19},{19,3},{4,20},{20... | collective-permute-start | bytes 3538952 | tf_op jit(solution)/shard_map/ppermute | solution.py:436
  332.9 15.7 %collective-permute-start.17 = (bf16[4,96,384]{2,1,0:T(8,128)(2,1)S(1)}, bf16[4,96,384]{2,1,0:T(8,128)(2,1)S(1)}, u32[]{:S(2)}, u32[]{:S(2)}) collective-permute-start(bf16[4,96,384]{2,1,0:T(8,128)(2,1)S(1)} %get-tuple-element.139.refs_8_), channel_id=1, source_target_pairs={{0,2},{2,0},{4,6},{6,4},{8,10},{10,8},{12,14},{14,12},{1,3},{3,1},... | collective-permute-start | bytes 884744 | tf_op jit(solution)/shard_map/ppermute | solution.py:441
  334.7 18.0 %collective-permute-start.18 = (bf16[4,96,384]{2,1,0:T(8,128)(2,1)}, bf16[4,96,384]{2,1,0:T(8,128)(2,1)S(1)}, u32[]{:S(2)}, u32[]{:S(2)}) collective-permute-start(bf16[4,96,384]{2,1,0:T(8,128)(2,1)} %copy-done.108), channel_id=1, source_target_pairs={{0,4},{2,6},{4,0},{6,2},{8,12},{10,14},{12,8},{14,10},{1,5},{3,7},... | collective-permute-start | bytes 884744 | tf_op jit(solution)/shard_map/ppermute | solution.py:441
  373.8 33.4 %all-to-all-start.7 = ((bf16[8,64,768]{2,1,0:T(8,128)(2,1)}), bf16[8,64,768]{2,1,0:T(8,128)(2,1)}, u32[]{:S(2)}, u32[]{:S(2)}) async-start(bf16[8,64,768]{2,1,0:T(8,128)(2,1)} %bitcast.70), calls=%async_computation.7 | async-start | bytes 1572864 | tf_op jit(solution)/shard_map/all_to_all | solution.py:600
  379.8 27.5 %collective-permute-start.19 = (bf16[1536,384]{1,0:T(8,128)(2,1)}, bf16[1536,384]{1,0:T(8,128)(2,1)}, u32[]{:S(2)}, u32[]{:S(2)}) collective-permute-start(bf16[1536,384]{1,0:T(8,128)(2,1)} %copy-done.57), channel_id=1, source_target_pairs={{0,16},{16,0},{1,17},{17,1},{2,18},{18,2},{3,19},{19,3},{4,20},{20... | collective-permute-start | bytes 3538952 | tf_op jit(solution)/shard_map/ppermute | solution.py:436
  381.3 13.1 %collective-permute-start.20 = (bf16[2,96,384]{2,1,0:T(8,128)(2,1)S(1)}, bf16[2,96,384]{2,1,0:T(8,128)(2,1)S(1)}, u32[]{:S(2)}, u32[]{:S(2)}) collective-permute-start(bf16[2,96,384]{2,1,0:T(8,128)(2,1)S(1)} %copy-done.93), channel_id=1, source_target_pairs={{0,4},{2,6},{4,0},{6,2},{8,12},{10,14},{12,8},{14,10},{1,5},{3,7},... | collective-permute-start | bytes 442376 | tf_op jit(solution)/shard_map/ppermute | solution.py:441
  383.4 11.1 %collective-permute-start.21 = (bf16[2,96,384]{2,1,0:T(8,128)(2,1)}, bf16[2,96,384]{2,1,0:T(8,128)(2,1)S(1)}, u32[]{:S(2)}, u32[]{:S(2)}) collective-permute-start(bf16[2,96,384]{2,1,0:T(8,128)(2,1)} %copy-done.109), channel_id=1, source_target_pairs={{0,2},{2,0},{4,6},{6,4},{8,10},{10,8},{12,14},{14,12},{1,3},{3,1},... | collective-permute-start | bytes 442376 | tf_op jit(solution)/shard_map/ppermute | solution.py:441
  396.1 8.0 %collective-permute-start.22 = (bf16[1,96,384]{2,1,0:T(8,128)(2,1)S(1)}, bf16[1,96,384]{2,1,0:T(8,128)(2,1)S(1)}, u32[]{:S(2)}, u32[]{:S(2)}) collective-permute-start(bf16[1,96,384]{2,1,0:T(8,128)(2,1)S(1)} %get-tuple-element.152), channel_id=1, source_target_pairs={{0,8},{2,10},{4,12},{6,14},{8,0},{10,2},{12,4},{14,6},{1,9},{3,11}... | collective-permute-start | bytes 221192 | tf_op jit(solution)/shard_map/ppermute | solution.py:441
  400.8 5.3 collective-permute-start.23
  400.9 6.4 %collective-permute-start.24 = (f32[16,768]{1,0:T(8,128)S(1)}, f32[16,768]{1,0:T(8,128)S(1)}, u32[]{:S(2)}, u32[]{:S(2)}) collective-permute-start(f32[16,768]{1,0:T(8,128)S(1)} %constant_dynamic-update-slice_fusion), channel_id=1, source_target_pairs={{0,16},{16,0},{1,17},{17,1},{2,18},{18,2},{3,19},{19,3},{4,20},{20... | collective-permute-start | bytes 147464 | tf_op jit(solution)/shard_map/ppermute | solution.py:436
  409.1 13.8 %collective-permute-start.25 = (bf16[416,768]{1,0:T(8,128)(2,1)S(1)}, bf16[416,768]{1,0:T(8,128)(2,1)S(1)}, u32[]{:S(2)}, u32[]{:S(2)}) collective-permute-start(bf16[416,768]{1,0:T(8,128)(2,1)S(1)} %shard_map.172.refs_9_.refs_1_), channel_id=1, source_target_pairs={{0,16},{16,0},{1,17},{17,1},{2,18},{18,2},{3,19},{19,3},{4,20},{20... | collective-permute-start | bytes 1916936 | tf_op jit(solution)/shard_map/ppermute | solution.py:436
  444.9 22.8 %collective-permute-start.39 = (bf16[384,3072]{1,0:T(8,128)(2,1)}, bf16[384,3072]{1,0:T(8,128)(2,1)}, u32[]{:S(2)}, u32[]{:S(2)}) collective-permute-start(bf16[384,3072]{1,0:T(8,128)(2,1)} %get-tuple-element.186), channel_id=1, source_target_pairs={{0,1},{1,0},{2,3},{3,2},{4,5},{5,4},{6,7},{7,6},{8,9},{9,8},{10,11... | collective-permute-start | bytes 7077896 | tf_op jit(solution)/shard_map/ppermute | solution.py:436
  445.0 22.7 %collective-permute-start.40 = (bf16[3072,384]{1,0:T(8,128)(2,1)}, bf16[3072,384]{1,0:T(8,128)(2,1)}, u32[]{:S(2)}, u32[]{:S(2)}) collective-permute-start(bf16[3072,384]{1,0:T(8,128)(2,1)} %get-tuple-element.187), channel_id=1, source_target_pairs={{0,1},{1,0},{2,3},{3,2},{4,5},{5,4},{6,7},{7,6},{8,9},{9,8},{10,11... | collective-permute-start | bytes 7077896 | tf_op jit(solution)/shard_map/ppermute | solution.py:436
  445.5 30.0 %collective-permute-start.26 = (bf16[1536,384]{1,0:T(8,128)(2,1)}, bf16[1536,384]{1,0:T(8,128)(2,1)}, u32[]{:S(2)}, u32[]{:S(2)}) collective-permute-start(bf16[1536,384]{1,0:T(8,128)(2,1)} %get-tuple-element.164), channel_id=1, source_target_pairs={{0,1},{1,0},{2,3},{3,2},{4,5},{5,4},{6,7},{7,6},{8,9},{9,8},{10,11... | collective-permute-start | bytes 3538952 | tf_op jit(solution)/shard_map/ppermute | solution.py:436
  445.5 58.7 %all-to-all-start.5 = ((bf16[8,64,768]{2,1,0:T(8,128)(2,1)}), bf16[8,64,768]{2,1,0:T(8,128)(2,1)S(1)}, u32[]{:S(2)}, u32[]{:S(2)}) async-start(bf16[8,64,768]{2,1,0:T(8,128)(2,1)} %bitcast.64), calls=%async_computation.5 | async-start | bytes 1572864 | tf_op jit(solution)/shard_map/all_to_all | solution.py:600
  451.0 16.7 %collective-permute-start.28 = (bf16[416,768]{1,0:T(8,128)(2,1)}, bf16[416,768]{1,0:T(8,128)(2,1)S(1)}, u32[]{:S(2)}, u32[]{:S(2)}) collective-permute-start(bf16[416,768]{1,0:T(8,128)(2,1)} %copy-done.43), channel_id=1, source_target_pairs={{0,16},{16,0},{1,17},{17,1},{2,18},{18,2},{3,19},{19,3},{4,20},{20... | collective-permute-start | bytes 1916936 | tf_op jit(solution)/shard_map/ppermute | solution.py:436
  474.0 49.7 %collective-permute-start.41 = (bf16[384,1536]{1,0:T(8,128)(2,1)}, bf16[384,1536]{1,0:T(8,128)(2,1)}, u32[]{:S(2)}, u32[]{:S(2)}) collective-permute-start(bf16[384,1536]{1,0:T(8,128)(2,1)} %get-tuple-element.188), channel_id=1, source_target_pairs={{0,16},{16,0},{1,17},{17,1},{2,18},{18,2},{3,19},{19,3},{4,20},{20... | collective-permute-start | bytes 3538952 | tf_op jit(solution)/shard_map/ppermute | solution.py:436
  477.2 21.8 %collective-permute-start.33 = (bf16[4,96,384]{2,1,0:T(8,128)(2,1)S(1)}, bf16[4,96,384]{2,1,0:T(8,128)(2,1)S(1)}, u32[]{:S(2)}, u32[]{:S(2)}) collective-permute-start(bf16[4,96,384]{2,1,0:T(8,128)(2,1)S(1)} %get-tuple-element.165.refs_2_), channel_id=1, source_target_pairs={{0,2},{2,0},{4,6},{6,4},{8,10},{10,8},{12,14},{14,12},{1,3},{3,1},... | collective-permute-start | bytes 884744 | tf_op jit(solution)/shard_map/ppermute | solution.py:441
  479.0 20.0 %collective-permute-start.34 = (bf16[4,96,384]{2,1,0:T(8,128)(2,1)S(1)}, bf16[4,96,384]{2,1,0:T(8,128)(2,1)S(1)}, u32[]{:S(2)}, u32[]{:S(2)}) collective-permute-start(bf16[4,96,384]{2,1,0:T(8,128)(2,1)S(1)} %get-tuple-element.175), channel_id=1, source_target_pairs={{0,4},{2,6},{4,0},{6,2},{8,12},{10,14},{12,8},{14,10},{1,5},{3,7},... | collective-permute-start | bytes 884744 | tf_op jit(solution)/shard_map/ppermute | solution.py:441
  480.4 6.5 %collective-permute-start.50 = (bf16[1,96,384]{2,1,0:T(8,128)(2,1)S(1)}, bf16[1,96,384]{2,1,0:T(8,128)(2,1)S(1)}, u32[]{:S(2)}, u32[]{:S(2)}) collective-permute-start(bf16[1,96,384]{2,1,0:T(8,128)(2,1)S(1)} %get-tuple-element.155.refs_3_.refs_1_), channel_id=1, source_target_pairs={{0,8},{2,10},{4,12},{6,14},{8,0},{10,2},{12,4},{14,6},{1,9},{3,11}... | collective-permute-start | bytes 221192 | tf_op jit(solution)/shard_map/ppermute | solution.py:441
  482.8 63.2 %collective-permute-start.46 = (bf16[1536,384]{1,0:T(8,128)(2,1)}, bf16[1536,384]{1,0:T(8,128)(2,1)}, u32[]{:S(2)}, u32[]{:S(2)}) collective-permute-start(bf16[1536,384]{1,0:T(8,128)(2,1)} %get-tuple-element.193), channel_id=1, source_target_pairs={{0,16},{16,0},{1,17},{17,1},{2,18},{18,2},{3,19},{19,3},{4,20},{20... | collective-permute-start | bytes 3538952 | tf_op jit(solution)/shard_map/ppermute | solution.py:436
  486.9 5.7 collective-permute-start.51
  493.9 9.8 %collective-permute-start.52 = (bf16[2,96,384]{2,1,0:T(8,128)(2,1)}, bf16[2,96,384]{2,1,0:T(8,128)(2,1)}, u32[]{:S(2)}, u32[]{:S(2)}) collective-permute-start(bf16[2,96,384]{2,1,0:T(8,128)(2,1)} %get-tuple-element.197.refs_1_), channel_id=1, source_target_pairs={{0,4},{2,6},{4,0},{6,2},{8,12},{10,14},{12,8},{14,10},{1,5},{3,7},... | collective-permute-start | bytes 442376 | tf_op jit(solution)/shard_map/ppermute | solution.py:441
  502.4 5.5 collective-permute-start.35
  503.7 2.1 collective-permute-start.29
  503.7 7.0 %collective-permute-start.36 = (bf16[2,96,384]{2,1,0:T(8,128)(2,1)}, bf16[2,96,384]{2,1,0:T(8,128)(2,1)}, u32[]{:S(2)}, u32[]{:S(2)}) collective-permute-start(bf16[2,96,384]{2,1,0:T(8,128)(2,1)} %copy-done.110), channel_id=1, source_target_pairs={{0,2},{2,0},{4,6},{6,4},{8,10},{10,8},{12,14},{14,12},{1,3},{3,1},... | collective-permute-start | bytes 442376 | tf_op jit(solution)/shard_map/ppermute | solution.py:441
  505.8 37.8 %collective-permute-start.27 = (bf16[416,768]{1,0:T(8,128)(2,1)S(1)}, bf16[416,768]{1,0:T(8,128)(2,1)S(1)}, u32[]{:S(2)}, u32[]{:S(2)}) collective-permute-start(bf16[416,768]{1,0:T(8,128)(2,1)S(1)} %shard_map.176), channel_id=1, source_target_pairs={{0,16},{16,0},{1,17},{17,1},{2,18},{18,2},{3,19},{19,3},{4,20},{20... | collective-permute-start | bytes 1916936 | tf_op jit(solution)/shard_map/ppermute | solution.py:436
  507.9 6.2 %collective-permute-start.53 = (bf16[2,96,384]{2,1,0:T(8,128)(2,1)S(1)}, bf16[2,96,384]{2,1,0:T(8,128)(2,1)S(1)}, u32[]{:S(2)}, u32[]{:S(2)}) collective-permute-start(bf16[2,96,384]{2,1,0:T(8,128)(2,1)S(1)} %copy-done.95), channel_id=1, source_target_pairs={{0,2},{2,0},{4,6},{6,4},{8,10},{10,8},{12,14},{14,12},{1,3},{3,1},... | collective-permute-start | bytes 442376 | tf_op jit(solution)/shard_map/ppermute | solution.py:441
  510.7 5.0 collective-permute-start.30
  514.1 8.8 %collective-permute-start.37 = (bf16[1,96,384]{2,1,0:T(8,128)(2,1)S(1)}, bf16[1,96,384]{2,1,0:T(8,128)(2,1)S(1)}, u32[]{:S(2)}, u32[]{:S(2)}) collective-permute-start(bf16[1,96,384]{2,1,0:T(8,128)(2,1)S(1)} %get-tuple-element.181), channel_id=1, source_target_pairs={{0,8},{2,10},{4,12},{6,14},{8,0},{10,2},{12,4},{14,6},{1,9},{3,11}... | collective-permute-start | bytes 221192 | tf_op jit(solution)/shard_map/ppermute | solution.py:441
  515.7 8.0 %collective-permute-start.38 = (bf16[1,96,384]{2,1,0:T(8,128)(2,1)S(1)}, bf16[1,96,384]{2,1,0:T(8,128)(2,1)S(1)}, u32[]{:S(2)}, u32[]{:S(2)}) collective-permute-start(bf16[1,96,384]{2,1,0:T(8,128)(2,1)S(1)} %get-tuple-element.183), channel_id=1, source_target_pairs={{0,8},{2,10},{4,12},{6,14},{8,0},{10,2},{12,4},{14,6},{1,9},{3,11}... | collective-permute-start | bytes 221192 | tf_op jit(solution)/shard_map/ppermute | solution.py:441
  522.8 6.7 %collective-permute-start.54 = (bf16[4,96,384]{2,1,0:T(8,128)(2,1)S(1)}, bf16[4,96,384]{2,1,0:T(8,128)(2,1)S(1)}, u32[]{:S(2)}, u32[]{:S(2)}) collective-permute-start(bf16[4,96,384]{2,1,0:T(8,128)(2,1)S(1)} %get-tuple-element.199.refs_1_), channel_id=1, source_target_pairs={{0,2},{2,0},{4,6},{6,4},{8,10},{10,8},{12,14},{14,12},{1,3},{3,1},... | collective-permute-start | bytes 884744 | tf_op jit(solution)/shard_map/ppermute | solution.py:441
  523.6 11.3 %collective-permute-start.55 = (bf16[4,96,384]{2,1,0:T(8,128)(2,1)S(1)}, bf16[4,96,384]{2,1,0:T(8,128)(2,1)S(1)}, u32[]{:S(2)}, u32[]{:S(2)}) collective-permute-start(bf16[4,96,384]{2,1,0:T(8,128)(2,1)S(1)} %get-tuple-element.200.refs_3_), channel_id=1, source_target_pairs={{0,4},{2,6},{4,0},{6,2},{8,12},{10,14},{12,8},{14,10},{1,5},{3,7},... | collective-permute-start | bytes 884744 | tf_op jit(solution)/shard_map/ppermute | solution.py:441
  523.7 10.9 %collective-permute-start.31 = (f32[20,768]{1,0:T(8,128)S(1)}, f32[20,768]{1,0:T(8,128)S(1)}, u32[]{:S(2)}, u32[]{:S(2)}) collective-permute-start(f32[20,768]{1,0:T(8,128)S(1)} %add.31), channel_id=1, source_target_pairs={{0,4},{2,6},{4,0},{6,2},{8,12},{10,14},{12,8},{14,10},{1,5},{3,7},... | collective-permute-start | bytes 184328 | tf_op jit(solution)/shard_map/ppermute | solution.py:441
  529.6 11.7 %collective-permute-start.42 = (bf16[1,96,384]{2,1,0:T(8,128)(2,1)S(1)}, bf16[1,96,384]{2,1,0:T(8,128)(2,1)S(1)}, u32[]{:S(2)}, u32[]{:S(2)}) collective-permute-start(bf16[1,96,384]{2,1,0:T(8,128)(2,1)S(1)} %get-tuple-element.189.refs_1_), channel_id=1, source_target_pairs={{0,8},{2,10},{4,12},{6,14},{8,0},{10,2},{12,4},{14,6},{1,9},{3,11}... | collective-permute-start | bytes 221192 | tf_op jit(solution)/shard_map/ppermute | solution.py:441
  534.5 6.7 %collective-permute-start.43 = (bf16[1,96,384]{2,1,0:T(8,128)(2,1)S(1)}, bf16[1,96,384]{2,1,0:T(8,128)(2,1)S(1)}, u32[]{:S(2)}, u32[]{:S(2)}) collective-permute-start(bf16[1,96,384]{2,1,0:T(8,128)(2,1)S(1)} %get-tuple-element.190.refs_3_), channel_id=1, source_target_pairs={{0,8},{2,10},{4,12},{6,14},{8,0},{10,2},{12,4},{14,6},{1,9},{3,11}... | collective-permute-start | bytes 221192 | tf_op jit(solution)/shard_map/ppermute | solution.py:441
  534.9 6.3 %collective-permute-start.32 = (f32[20,768]{1,0:T(8,128)S(1)}, f32[20,768]{1,0:T(8,128)S(1)}, u32[]{:S(2)}, u32[]{:S(2)}) collective-permute-start(f32[20,768]{1,0:T(8,128)S(1)} %add.32), channel_id=1, source_target_pairs={{0,8},{2,10},{4,12},{6,14},{8,0},{10,2},{12,4},{14,6},{1,9},{3,11}... | collective-permute-start | bytes 184328 | tf_op jit(solution)/shard_map/ppermute | solution.py:441
  541.2 18.9 %collective-permute-start.56 = (bf16[2,768,384]{2,1,0:T(8,128)(2,1)}, bf16[2,768,384]{2,1,0:T(8,128)(2,1)}, u32[]{:S(2)}, u32[]{:S(2)}) collective-permute-start(bf16[2,768,384]{2,1,0:T(8,128)(2,1)} %bitcast.34.refs_1_), channel_id=1, source_target_pairs={{0,1},{1,0},{2,3},{3,2},{4,5},{5,4},{6,7},{7,6},{8,9},{9,8},{10,11... | collective-permute-start | bytes 3538952 | tf_op jit(solution)/shard_map/ppermute | solution.py:436
  541.9 6.3 %collective-permute-start.44 = (bf16[2,96,384]{2,1,0:T(8,128)(2,1)S(1)}, bf16[2,96,384]{2,1,0:T(8,128)(2,1)S(1)}, u32[]{:S(2)}, u32[]{:S(2)}) collective-permute-start(bf16[2,96,384]{2,1,0:T(8,128)(2,1)S(1)} %get-tuple-element.191.refs_1_), channel_id=1, source_target_pairs={{0,4},{2,6},{4,0},{6,2},{8,12},{10,14},{12,8},{14,10},{1,5},{3,7},... | collective-permute-start | bytes 442376 | tf_op jit(solution)/shard_map/ppermute | solution.py:441
  543.4 6.0 %collective-permute-start.45 = (bf16[2,96,384]{2,1,0:T(8,128)(2,1)S(1)}, bf16[2,96,384]{2,1,0:T(8,128)(2,1)S(1)}, u32[]{:S(2)}, u32[]{:S(2)}) collective-permute-start(bf16[2,96,384]{2,1,0:T(8,128)(2,1)S(1)} %get-tuple-element.192.refs_3_), channel_id=1, source_target_pairs={{0,2},{2,0},{4,6},{6,4},{8,10},{10,8},{12,14},{14,12},{1,3},{3,1},... | collective-permute-start | bytes 442376 | tf_op jit(solution)/shard_map/ppermute | solution.py:441
  550.0 8.4 %collective-permute-start.47 = (bf16[4,96,384]{2,1,0:T(8,128)(2,1)S(1)}, bf16[4,96,384]{2,1,0:T(8,128)(2,1)S(1)}, u32[]{:S(2)}, u32[]{:S(2)}) collective-permute-start(bf16[4,96,384]{2,1,0:T(8,128)(2,1)S(1)} %get-tuple-element.194.refs_1_), channel_id=1, source_target_pairs={{0,2},{2,0},{4,6},{6,4},{8,10},{10,8},{12,14},{14,12},{1,3},{3,1},... | collective-permute-start | bytes 884744 | tf_op jit(solution)/shard_map/ppermute | solution.py:441
  550.3 8.1 %collective-permute-start.48 = (bf16[4,96,384]{2,1,0:T(8,128)(2,1)S(1)}, bf16[4,96,384]{2,1,0:T(8,128)(2,1)S(1)}, u32[]{:S(2)}, u32[]{:S(2)}) collective-permute-start(bf16[4,96,384]{2,1,0:T(8,128)(2,1)S(1)} %get-tuple-element.195.refs_3_), channel_id=1, source_target_pairs={{0,4},{2,6},{4,0},{6,2},{8,12},{10,14},{12,8},{14,10},{1,5},{3,7},... | collective-permute-start | bytes 884744 | tf_op jit(solution)/shard_map/ppermute | solution.py:441
  560.1 13.5 %collective-permute-start.49 = (bf16[2,768,384]{2,1,0:T(8,128)(2,1)}, bf16[2,768,384]{2,1,0:T(8,128)(2,1)}, u32[]{:S(2)}, u32[]{:S(2)}) collective-permute-start(bf16[2,768,384]{2,1,0:T(8,128)(2,1)} %bitcast.33.refs_1_), channel_id=1, source_target_pairs={{0,1},{1,0},{2,3},{3,2},{4,5},{5,4},{6,7},{7,6},{8,9},{9,8},{10,11... | collective-permute-start | bytes 3538952 | tf_op jit(solution)/shard_map/ppermute | solution.py:436
  (120 other events, 1048.6 us)

commit v4 on v3

--- a/solution.py
+++ b/solution.py
@@ -908,7 +908,9 @@
             sums[layer].split((gain_one,))
             sums[layer].finish(far[:1])
             sums[layer].join()
-            sums[layer].join((far[1], small, mixed_out))
+            sums[layer].join((far[1],))
+            while sums[layer].step:
+                sums[layer].join((small, mixed_out) if sums[layer].step == 1 else ())
         mine = sums[layer].result()
         stacked = call(
             layout_kernel,

time: 587 us -> 589 us (level)
    unnamed x241 -> x237, local copies, waits for them, and re-layouts: 61.1 us -> 64.7 us
  transfers between devices with their start and end apart: 64 -> 64, of which waited for: 36 -> 34; matrix products, arithmetic and copies ran while one was open for 2% -> 1% of each run, Pallas kernels for 11% -> 12%
where the time goes in v4:
time: 589 us; the launch traced here: 580 us
  waiting for transfers between devices  217 us (37%)
  Pallas kernels  161 us (27%)
  starting transfers between devices  100 us (17%)
  local copies, waits for them, and re-layouts  72.3 us (12%)
  blocking collectives  26.2 us (4%)
    pallas_call x40, Pallas kernels, call(): pl.pallas_call(kernel, grid=grid, out_shape=outs, in_specs=[*specs, *[ANY...  161 us
    ppermute x30, waiting for transfers between devices, swap(): return lax.ppermute(value, axis, [(0, 1), (1, 0)])  127 us
    ppermute x27, waiting for transfers between devices, partner(): return lax.ppermute(value, axis, [(i, i ^ 1 << bit) for i in range(count)])  69.6 us
    unnamed x237, local copies, waits for them, and re-layouts  64.7 us
    all_to_all x7, starting transfers between devices, exchange(): lax.all_to_all(block, 'expert', 0, 0, tiled=True).reshape(slots, width)  38 us
    ppermute x27, starting transfers between devices, partner(): return lax.ppermute(value, axis, [(i, i ^ 1 << bit) for i in range(count)])  35.2 us
    ppermute x30, starting transfers between devices, swap(): return lax.ppermute(value, axis, [(0, 1), (1, 0)])  26.9 us
    all_to_all x1, blocking collectives, exchange(): lax.all_to_all(block, 'expert', 0, 0, tiled=True).reshape(slots, width)  26.2 us
  transfers between devices with their start and end apart: 64, of which 34 were waited for; matrix products, arithmetic and copies ran while one was open for 1% of the time, Pallas kernels for 12%

profile of v4, /device:TPU:0, one launch (start us, length us, event | category | flops | bytes accessed | tf_op | source)
XLA Modules:
  0.0 580.4 jit_solution(8758014709230243489)
XLA Ops:
  2.1 2.0 copy-done.4
  4.1 4.3 shard_map.152
  10.9 2.9 collective-permute-start
  13.9 2.3 copy-done.2
  22.9 6.1 %collective-permute-done.refs_3_ = bf16[416,768]{1,0:T(8,128)(2,1)S(1)} collective-permute-done((bf16[416,768]{1,0:T(8,128)(2,1)S(1)}, bf16[416,768]{1,0:T(8,128)(2,1)S(1)}, u32[]{:S(2)}, u32[]{:S(2)}) %collective-permute-start) | collective-permute-done | bytes 639008 | tf_op jit(solution)/shard_map/ppermute | solution.py:436
  29.0 2.3 copy-done
  31.4 3.3 shard_map.154
  35.8 2.1 collective-permute-start.3
  37.8 5.8 %all-to-all-start = ((bf16[8,64,768]{2,1,0:T(8,128)(2,1)}), bf16[8,64,768]{2,1,0:T(8,128)(2,1)S(1)}, u32[]{:S(2)}, u32[]{:S(2)}) async-start(bf16[8,64,768]{2,1,0:T(8,128)(2,1)} %bitcast.6), calls=%async_computation | async-start | bytes 1572864 | tf_op jit(solution)/shard_map/all_to_all | solution.py:600
  43.7 10.7 %collective-permute-done.1.refs_4_.refs_7_ = bf16[768,768]{1,0:T(8,128)(2,1)} collective-permute-done((bf16[768,768]{1,0:T(8,128)(2,1)}, bf16[768,768]{1,0:T(8,128)(2,1)}, u32[]{:S(2)}, u32[]{:S(2)}) %collective-permute-start.1) | collective-permute-done | bytes 1179680 | tf_op jit(solution)/shard_map/ppermute | solution.py:436
  54.4 24.3 %collective-permute-done.3.refs_7_.refs_10_ = bf16[768,768]{1,0:T(8,128)(2,1)S(1)} collective-permute-done((bf16[768,768]{1,0:T(8,128)(2,1)}, bf16[768,768]{1,0:T(8,128)(2,1)S(1)}, u32[]{:S(2)}, u32[]{:S(2)}) %collective-permute-start.3) | collective-permute-done | bytes 1179680 | tf_op jit(solution)/shard_map/ppermute | solution.py:436
  79.5 2.6 copy-done.3
  84.8 13.1 %shard_map.157 = (bf16[512,768]{1,0:T(8,128)(2,1)}, bf16[512,3072]{1,0:T(8,128)(2,1)}, bf16[512,3072]{1,0:T(8,128)(2,1)}) custom-call(s32[3]{0:T(128)} %copy-done.86, bf16[512,768]{1,0:T(8,128)(2,1)} %bitcast.48, bf16[8,768]{1,0:T(8,128)(2,1)} %get-tuple-element.225.refs_2_.refs_5_, bf16[2,1,768,1536]{3,2,1,0:T(8,128)(2,1)} %refs_6_.7, ...), custom_call_target="tpu_custom_call" | custom-call | flops 1 | bytes 23400000 | tf_op jit(solution)/shard_map/pallas_call | solution.py:66
  97.8 6.6 %all-to-all-start.1 = ((bf16[8,64,768]{2,1,0:T(8,128)(2,1)}), bf16[8,64,768]{2,1,0:T(8,128)(2,1)}, u32[]{:S(2)}, u32[]{:S(2)}) async-start(bf16[8,64,768]{2,1,0:T(8,128)(2,1)} %bitcast.72), calls=%async_computation.1 | async-start | bytes 1572864 | tf_op jit(solution)/shard_map/all_to_all | solution.py:600
  106.0 19.2 %all-to-all-done.1 = bf16[8,64,768]{2,1,0:T(8,128)(2,1)} async-done(((bf16[8,64,768]{2,1,0:T(8,128)(2,1)}), bf16[8,64,768]{2,1,0:T(8,128)(2,1)}, u32[]{:S(2)}, u32[]{:S(2)}) %all-to-all-start.1) | async-done | bytes 786464 | tf_op jit(solution)/shard_map/all_to_all | solution.py:600
  129.7 3.9 collective-permute-done.6.refs_6_.refs_5_
  133.7 12.8 %collective-permute-done.5.refs_2_ = bf16[416,768]{1,0:T(8,128)(2,1)S(1)} collective-permute-done((bf16[416,768]{1,0:T(8,128)(2,1)S(1)}, bf16[416,768]{1,0:T(8,128)(2,1)S(1)}, u32[]{:S(2)}, u32[]{:S(2)}) %collective-permute-start.5) | collective-permute-done | bytes 639008 | tf_op jit(solution)/shard_map/ppermute | solution.py:436
  149.1 5.2 shard_map.159
  159.4 5.7 all-to-all-start.2
  165.1 8.6 %collective-permute-done.7.refs_3_ = bf16[416,768]{1,0:T(8,128)(2,1)S(1)} collective-permute-done((bf16[416,768]{1,0:T(8,128)(2,1)}, bf16[416,768]{1,0:T(8,128)(2,1)S(1)}, u32[]{:S(2)}, u32[]{:S(2)}) %collective-permute-start.7) | collective-permute-done | bytes 639008 | tf_op jit(solution)/shard_map/ppermute | solution.py:436
  173.7 2.3 copy-done.1
  177.4 3.2 shard_map.160
  184.4 4.2 all-to-all-start.3
  188.6 19.6 %collective-permute-done.9.refs_8_ = bf16[768,768]{1,0:T(8,128)(2,1)} collective-permute-done((bf16[768,768]{1,0:T(8,128)(2,1)S(1)}, bf16[768,768]{1,0:T(8,128)(2,1)}, u32[]{:S(2)}, u32[]{:S(2)}) %collective-permute-start.9) | collective-permute-done | bytes 1179680 | tf_op jit(solution)/shard_map/ppermute | solution.py:436
  208.2 3.0 collective-permute-done.10.refs_9_
  212.2 22.2 %shard_map.161 = (bf16[512,768]{1,0:T(8,128)(2,1)}, bf16[512,768]{1,0:T(8,128)(2,1)}, bf16[512,3072]{1,0:T(8,128)(2,1)}, bf16[512,3072]{1,0:T(8,128)(2,1)}, bf16[512,768]{1,0:T(8,128)(2,1)}, /*index=5*/f32[8,768]{1,0:T(8,128)}) custom-call(s32[3]{0:T(128)} %copy-done.86, bf16[512,768]{1,0:T(8,128)(2,1)} %bitcast.13.refs_1_, bf16[512,768]{1,0:T(8,128)(2,1)} %bitcast.53, ...), custom_call_target="tpu_custom_call" | custom-call | flops 1 | bytes 39600000 | tf_op jit(solution)/shard_map/pallas_call | solution.py:66
  234.5 26.2 %all_to_all.40 = bf16[8,64,768]{2,1,0:T(8,128)(2,1)S(1)} all-to-all(bf16[8,64,768]{2,1,0:T(8,128)(2,1)} %bitcast.71), channel_id=1, replica_groups=mesh['tensor'=2,'expert'=8,'replica'=2] {'expert'}, dimensions={0} | all-to-all | bytes 1572864 | tf_op jit(solution)/shard_map/all_to_all | solution.py:600
  266.4 5.6 shard_map.163
  273.9 14.8 %collective-permute-done.11.refs_2_ = bf16[416,768]{1,0:T(8,128)(2,1)S(1)} collective-permute-done((bf16[416,768]{1,0:T(8,128)(2,1)S(1)}, bf16[416,768]{1,0:T(8,128)(2,1)S(1)}, u32[]{:S(2)}, u32[]{:S(2)}) %collective-permute-start.11) | collective-permute-done | bytes 639008 | tf_op jit(solution)/shard_map/ppermute | solution.py:436
  288.8 14.4 %shard_map.164 = (f32[416,768]{1,0:T(8,128)S(1)}, f32[1,768]{1,0:T(1,128)S(1)}, bf16[416,768]{1,0:T(8,128)(2,1)}, bf16[1536,384]{1,0:T(8,128)(2,1)S(1)}, bf16[1536,384]{1,0:T(8,128)(2,1)}) custom-call(s32[3]{0:T(128)S(1)} %copy-done.88, bf16[416,768]{1,0:T(8,128)(2,1)S(1)} %get-tuple-element.124.refs_5_.refs_1_, ...), custom_call_target="tpu_custom_call" | custom-call | flops 1 | bytes 57600000 | tf_op jit(solution)/shard_map/pallas_call | solution.py:66
  315.7 3.6 shard_map.165
  319.3 3.1 collective-permute-done.12.refs_1_
  322.4 2.7 shard_map.167
  327.1 4.2 all-to-all-start.6
  336.2 12.3 %collective-permute-done.17.refs_2_ = bf16[4,96,384]{2,1,0:T(8,128)(2,1)S(1)} collective-permute-done((bf16[4,96,384]{2,1,0:T(8,128)(2,1)S(1)}, bf16[4,96,384]{2,1,0:T(8,128)(2,1)S(1)}, u32[]{:S(2)}, u32[]{:S(2)}) %collective-permute-start.17) | collective-permute-done | bytes 294944 | tf_op jit(solution)/shard_map/ppermute | solution.py:441
  348.6 4.1 collective-permute-done.18.refs_4_
  359.3 14.5 %shard_map.169 = (bf16[512,768]{1,0:T(8,128)(2,1)}, bf16[512,3072]{1,0:T(8,128)(2,1)}, bf16[512,768]{1,0:T(8,128)(2,1)}, f32[8,768]{1,0:T(8,128)}) custom-call(s32[3]{0:T(128)} %copy-done.86, bf16[512,768]{1,0:T(8,128)(2,1)} %bitcast.26.refs_1_, bf16[512,768]{1,0:T(8,128)(2,1)} %bitcast.49, bf16[512,3072]{1,0:T(8,128)(2,1)} %get-tuple-element.141.refs_3_.refs_4_, ...), custom_call_target="tpu_custom_call" | custom-call | flops 1 | bytes 23400000 | tf_op jit(solution)/shard_map/pallas_call | solution.py:66
  373.8 6.0 %all-to-all-start.7 = ((bf16[8,64,768]{2,1,0:T(8,128)(2,1)}), bf16[8,64,768]{2,1,0:T(8,128)(2,1)}, u32[]{:S(2)}, u32[]{:S(2)}) async-start(bf16[8,64,768]{2,1,0:T(8,128)(2,1)} %bitcast.70), calls=%async_computation.7 | async-start | bytes 1572864 | tf_op jit(solution)/shard_map/all_to_all | solution.py:600
  381.3 2.0 collective-permute-start.20
  384.9 9.6 %collective-permute-done.20.refs_2_ = bf16[2,96,384]{2,1,0:T(8,128)(2,1)S(1)} collective-permute-done((bf16[2,96,384]{2,1,0:T(8,128)(2,1)S(1)}, bf16[2,96,384]{2,1,0:T(8,128)(2,1)S(1)}, u32[]{:S(2)}, u32[]{:S(2)}) %collective-permute-start.20) | collective-permute-done | bytes 147488 | tf_op jit(solution)/shard_map/ppermute | solution.py:441
  396.0 4.7 collective-permute-start.22
  404.0 2.0 collective-permute-done.23.refs_3_
  411.8 5.0 shard_map.173
  416.8 6.0 %collective-permute-done.25.refs_2_ = bf16[416,768]{1,0:T(8,128)(2,1)S(1)} collective-permute-done((bf16[416,768]{1,0:T(8,128)(2,1)S(1)}, bf16[416,768]{1,0:T(8,128)(2,1)S(1)}, u32[]{:S(2)}, u32[]{:S(2)}) %collective-permute-start.25) | collective-permute-done | bytes 639008 | tf_op jit(solution)/shard_map/ppermute | solution.py:436
  422.9 14.5 %shard_map.174 = (f32[416,768]{1,0:T(8,128)S(1)}, f32[1,768]{1,0:T(1,128)S(1)}, bf16[416,768]{1,0:T(8,128)(2,1)}, bf16[1536,384]{1,0:T(8,128)(2,1)S(1)}, bf16[1536,384]{1,0:T(8,128)(2,1)}) custom-call(s32[3]{0:T(128)S(1)} %copy-done.89, bf16[416,768]{1,0:T(8,128)(2,1)S(1)} %shard_map.172.refs_9_.refs_1_, ...), custom_call_target="tpu_custom_call" | custom-call | flops 1 | bytes 57600000 | tf_op jit(solution)/shard_map/pallas_call | solution.py:66
  439.5 5.5 shard_map.180
  447.1 5.4 all-to-all-start.5
  452.5 10.1 %collective-permute-done.28.refs_1_.refs_7_ = bf16[416,768]{1,0:T(8,128)(2,1)} collective-permute-done((bf16[416,768]{1,0:T(8,128)(2,1)}, bf16[416,768]{1,0:T(8,128)(2,1)}, u32[]{:S(2)}, u32[]{:S(2)}) %collective-permute-start.28) | collective-permute-done | bytes 639008 | tf_op jit(solution)/shard_map/ppermute | solution.py:436
  464.6 4.3 shard_map.181
  475.6 2.4 collective-permute-start.50
  478.0 4.5 collective-permute-done.50.refs_2_
  482.5 3.4 collective-permute-start.51
  485.9 2.3 collective-permute-done.51.refs_4_
  489.5 3.0 collective-permute-start.52
  492.5 3.3 shard_map.177
  514.5 3.4 collective-permute-done.37.refs_1_
  520.0 6.0 %collective-permute-done.30 = f32[20,768]{1,0:T(8,128)S(1)} collective-permute-done((f32[20,768]{1,0:T(8,128)S(1)}, f32[20,768]{1,0:T(8,128)S(1)}, u32[]{:S(2)}, u32[]{:S(2)}) %collective-permute-start.30) | collective-permute-done | bytes 61472 | tf_op jit(solution)/shard_map/ppermute | solution.py:441
  526.6 6.2 %collective-permute-done.42.refs_2_ = bf16[1,96,384]{2,1,0:T(8,128)(2,1)S(1)} collective-permute-done((bf16[1,96,384]{2,1,0:T(8,128)(2,1)S(1)}, bf16[1,96,384]{2,1,0:T(8,128)(2,1)S(1)}, u32[]{:S(2)}, u32[]{:S(2)}) %collective-permute-start.42) | collective-permute-done | bytes 73760 | tf_op jit(solution)/shard_map/ppermute | solution.py:441
  532.8 5.8 %collective-permute-done.43.refs_4_ = bf16[1,96,384]{2,1,0:T(8,128)(2,1)S(1)} collective-permute-done((bf16[1,96,384]{2,1,0:T(8,128)(2,1)S(1)}, bf16[1,96,384]{2,1,0:T(8,128)(2,1)S(1)}, u32[]{:S(2)}, u32[]{:S(2)}) %collective-permute-start.43) | collective-permute-done | bytes 73760 | tf_op jit(solution)/shard_map/ppermute | solution.py:441
  545.4 3.5 collective-permute-done.32
  555.0 4.1 collective-permute-done.47.refs_2_
  562.3 4.1 shard_map.189
  570.9 4.9 shard_map.191
  575.8 4.1 shard_map.190
  (369 shorter events, 137.9 us)
Async XLA Ops:
  10.9 18.2 %collective-permute-start = (bf16[416,768]{1,0:T(8,128)(2,1)S(1)}, bf16[416,768]{1,0:T(8,128)(2,1)S(1)}, u32[]{:S(2)}, u32[]{:S(2)}) collective-permute-start(bf16[416,768]{1,0:T(8,128)(2,1)S(1)} %get-tuple-element.109.refs_3_.refs_2_), channel_id=1, source_target_pairs={{0,16},{16,0},{1,17},{17,1},{2,18},{18,2},{3,19},{19,3},{4,20},{20... | collective-permute-start | bytes 1916936 | tf_op jit(solution)/shard_map/ppermute | solution.py:436
  17.8 36.6 %collective-permute-start.1 = (bf16[768,768]{1,0:T(8,128)(2,1)}, bf16[768,768]{1,0:T(8,128)(2,1)}, u32[]{:S(2)}, u32[]{:S(2)}) collective-permute-start(bf16[768,768]{1,0:T(8,128)(2,1)} %shard_map.155), channel_id=1, source_target_pairs={{0,16},{16,0},{1,17},{17,1},{2,18},{18,2},{3,19},{19,3},{4,20},{20... | collective-permute-start | bytes 3538952 | tf_op jit(solution)/shard_map/ppermute | solution.py:436
  35.8 43.0 %collective-permute-start.3 = (bf16[768,768]{1,0:T(8,128)(2,1)}, bf16[768,768]{1,0:T(8,128)(2,1)S(1)}, u32[]{:S(2)}, u32[]{:S(2)}) collective-permute-start(bf16[768,768]{1,0:T(8,128)(2,1)} %get-tuple-element.113), channel_id=1, source_target_pairs={{0,16},{16,0},{1,17},{17,1},{2,18},{18,2},{3,19},{19,3},{4,20},{20... | collective-permute-start | bytes 3538952 | tf_op jit(solution)/shard_map/ppermute | solution.py:436
  37.8 41.6 %all-to-all-start = ((bf16[8,64,768]{2,1,0:T(8,128)(2,1)}), bf16[8,64,768]{2,1,0:T(8,128)(2,1)S(1)}, u32[]{:S(2)}, u32[]{:S(2)}) async-start(bf16[8,64,768]{2,1,0:T(8,128)(2,1)} %bitcast.6), calls=%async_computation | async-start | bytes 1572864 | tf_op jit(solution)/shard_map/all_to_all | solution.py:600
  54.4 29.3 %collective-permute-start.2 = (bf16[768,768]{1,0:T(8,128)(2,1)}, bf16[768,768]{1,0:T(8,128)(2,1)S(1)}, u32[]{:S(2)}, u32[]{:S(2)}) collective-permute-start(bf16[768,768]{1,0:T(8,128)(2,1)} %collective-permute-done.1.refs_4_.refs_7_), channel_id=1, source_target_pairs={{0,1},{1,0},{2,3},{3,2},{4,5},{5,4},{6,7},{7,6},{8,9},{9,8},{10,11... | collective-permute-start | bytes 3538952 | tf_op jit(solution)/shard_map/ppermute | solution.py:436
  78.8 5.0 collective-permute-start.4
  97.8 27.4 %all-to-all-start.1 = ((bf16[8,64,768]{2,1,0:T(8,128)(2,1)}), bf16[8,64,768]{2,1,0:T(8,128)(2,1)}, u32[]{:S(2)}, u32[]{:S(2)}) async-start(bf16[8,64,768]{2,1,0:T(8,128)(2,1)} %bitcast.72), calls=%async_computation.1 | async-start | bytes 1572864 | tf_op jit(solution)/shard_map/all_to_all | solution.py:600
  104.5 29.2 %collective-permute-start.6 = (bf16[768,768]{1,0:T(8,128)(2,1)}, bf16[768,768]{1,0:T(8,128)(2,1)}, u32[]{:S(2)}, u32[]{:S(2)}) collective-permute-start(bf16[768,768]{1,0:T(8,128)(2,1)} %copy-done.42), channel_id=1, source_target_pairs={{0,16},{16,0},{1,17},{17,1},{2,18},{18,2},{3,19},{19,3},{4,20},{20... | collective-permute-start | bytes 3538952 | tf_op jit(solution)/shard_map/ppermute | solution.py:436
  128.2 18.3 %collective-permute-start.5 = (bf16[416,768]{1,0:T(8,128)(2,1)S(1)}, bf16[416,768]{1,0:T(8,128)(2,1)S(1)}, u32[]{:S(2)}, u32[]{:S(2)}) collective-permute-start(bf16[416,768]{1,0:T(8,128)(2,1)S(1)} %shard_map.158.refs_1_), channel_id=1, source_target_pairs={{0,16},{16,0},{1,17},{17,1},{2,18},{18,2},{3,19},{19,3},{4,20},{20... | collective-permute-start | bytes 1916936 | tf_op jit(solution)/shard_map/ppermute | solution.py:436
  157.9 15.8 %collective-permute-start.7 = (bf16[416,768]{1,0:T(8,128)(2,1)}, bf16[416,768]{1,0:T(8,128)(2,1)S(1)}, u32[]{:S(2)}, u32[]{:S(2)}) collective-permute-start(bf16[416,768]{1,0:T(8,128)(2,1)} %get-tuple-element.116.refs_2_), channel_id=1, source_target_pairs={{0,16},{16,0},{1,17},{17,1},{2,18},{18,2},{3,19},{19,3},{4,20},{20... | collective-permute-start | bytes 1916936 | tf_op jit(solution)/shard_map/ppermute | solution.py:436
  159.4 25.0 %all-to-all-start.2 = ((bf16[8,64,768]{2,1,0:T(8,128)(2,1)}), bf16[8,64,768]{2,1,0:T(8,128)(2,1)}, u32[]{:S(2)}, u32[]{:S(2)}) async-start(bf16[8,64,768]{2,1,0:T(8,128)(2,1)} %bitcast.65), calls=%async_computation.2 | async-start | bytes 1572864 | tf_op jit(solution)/shard_map/all_to_all | solution.py:600
  181.7 26.5 %collective-permute-start.9 = (bf16[768,768]{1,0:T(8,128)(2,1)S(1)}, bf16[768,768]{1,0:T(8,128)(2,1)}, u32[]{:S(2)}, u32[]{:S(2)}) collective-permute-start(bf16[768,768]{1,0:T(8,128)(2,1)S(1)} %get-tuple-element.120), channel_id=1, source_target_pairs={{0,16},{16,0},{1,17},{17,1},{2,18},{18,2},{3,19},{19,3},{4,20},{20... | collective-permute-start | bytes 3538952 | tf_op jit(solution)/shard_map/ppermute | solution.py:436
  184.4 23.8 %all-to-all-start.3 = ((bf16[8,64,768]{2,1,0:T(8,128)(2,1)}), bf16[8,64,768]{2,1,0:T(8,128)(2,1)S(1)}, u32[]{:S(2)}, u32[]{:S(2)}) async-start(bf16[8,64,768]{2,1,0:T(8,128)(2,1)} %bitcast.14), calls=%async_computation.3 | async-start | bytes 1572864 | tf_op jit(solution)/shard_map/all_to_all | solution.py:600
  188.6 19.6 %collective-permute-start.8 = (bf16[768,768]{1,0:T(8,128)(2,1)}, bf16[768,768]{1,0:T(8,128)(2,1)}, u32[]{:S(2)}, u32[]{:S(2)}) collective-permute-start(bf16[768,768]{1,0:T(8,128)(2,1)} %collective-permute-done.6.refs_6_.refs_5_), channel_id=1, source_target_pairs={{0,1},{1,0},{2,3},{3,2},{4,5},{5,4},{6,7},{7,6},{8,9},{9,8},{10,11... | collective-permute-start | bytes 3538952 | tf_op jit(solution)/shard_map/ppermute | solution.py:436
  208.2 3.1 collective-permute-start.10
  271.9 41.8 %collective-permute-start.13 = (bf16[384,3072]{1,0:T(8,128)(2,1)}, bf16[384,3072]{1,0:T(8,128)(2,1)}, u32[]{:S(2)}, u32[]{:S(2)}) collective-permute-start(bf16[384,3072]{1,0:T(8,128)(2,1)} %get-tuple-element.131.refs_11_), channel_id=1, source_target_pairs={{0,1},{1,0},{2,3},{3,2},{4,5},{5,4},{6,7},{7,6},{8,9},{9,8},{10,11... | collective-permute-start | bytes 7077896 | tf_op jit(solution)/shard_map/ppermute | solution.py:436
  271.9 41.8 %collective-permute-start.14 = (bf16[3072,384]{1,0:T(8,128)(2,1)}, bf16[3072,384]{1,0:T(8,128)(2,1)}, u32[]{:S(2)}, u32[]{:S(2)}) collective-permute-start(bf16[3072,384]{1,0:T(8,128)(2,1)} %get-tuple-element.132.refs_12_), channel_id=1, source_target_pairs={{0,1},{1,0},{2,3},{3,2},{4,5},{5,4},{6,7},{7,6},{8,9},{9,8},{10,11... | collective-permute-start | bytes 7077896 | tf_op jit(solution)/shard_map/ppermute | solution.py:436
  272.4 16.3 %collective-permute-start.11 = (bf16[416,768]{1,0:T(8,128)(2,1)S(1)}, bf16[416,768]{1,0:T(8,128)(2,1)S(1)}, u32[]{:S(2)}, u32[]{:S(2)}) collective-permute-start(bf16[416,768]{1,0:T(8,128)(2,1)S(1)} %get-tuple-element.124.refs_5_.refs_1_), channel_id=1, source_target_pairs={{0,16},{16,0},{1,17},{17,1},{2,18},{18,2},{3,19},{19,3},{4,20},{20... | collective-permute-start | bytes 1916936 | tf_op jit(solution)/shard_map/ppermute | solution.py:436
  305.2 3.2 collective-permute-start.15
  305.2 17.1 %collective-permute-start.12 = (bf16[416,768]{1,0:T(8,128)(2,1)}, bf16[416,768]{1,0:T(8,128)(2,1)}, u32[]{:S(2)}, u32[]{:S(2)}) collective-permute-start(bf16[416,768]{1,0:T(8,128)(2,1)} %get-tuple-element.133.refs_7_.refs_0_), channel_id=1, source_target_pairs={{0,16},{16,0},{1,17},{17,1},{2,18},{18,2},{3,19},{19,3},{4,20},{20... | collective-permute-start | bytes 1916936 | tf_op jit(solution)/shard_map/ppermute | solution.py:436
  327.1 32.2 %all-to-all-start.6 = ((bf16[8,64,768]{2,1,0:T(8,128)(2,1)}), bf16[8,64,768]{2,1,0:T(8,128)(2,1)}, u32[]{:S(2)}, u32[]{:S(2)}) async-start(bf16[8,64,768]{2,1,0:T(8,128)(2,1)} %bitcast.66), calls=%async_computation.6 | async-start | bytes 1572864 | tf_op jit(solution)/shard_map/all_to_all | solution.py:600
  331.3 28.0 %collective-permute-start.16 = (bf16[384,1536]{1,0:T(8,128)(2,1)}, bf16[384,1536]{1,0:T(8,128)(2,1)}, u32[]{:S(2)}, u32[]{:S(2)}) collective-permute-start(bf16[384,1536]{1,0:T(8,128)(2,1)} %copy-done.56), channel_id=1, source_target_pairs={{0,16},{16,0},{1,17},{17,1},{2,18},{18,2},{3,19},{19,3},{4,20},{20... | collective-permute-start | bytes 3538952 | tf_op jit(solution)/shard_map/ppermute | solution.py:436
  332.8 15.7 %collective-permute-start.17 = (bf16[4,96,384]{2,1,0:T(8,128)(2,1)S(1)}, bf16[4,96,384]{2,1,0:T(8,128)(2,1)S(1)}, u32[]{:S(2)}, u32[]{:S(2)}) collective-permute-start(bf16[4,96,384]{2,1,0:T(8,128)(2,1)S(1)} %get-tuple-element.139.refs_8_), channel_id=1, source_target_pairs={{0,2},{2,0},{4,6},{6,4},{8,10},{10,8},{12,14},{14,12},{1,3},{3,1},... | collective-permute-start | bytes 884744 | tf_op jit(solution)/shard_map/ppermute | solution.py:441
  334.7 18.0 %collective-permute-start.18 = (bf16[4,96,384]{2,1,0:T(8,128)(2,1)}, bf16[4,96,384]{2,1,0:T(8,128)(2,1)S(1)}, u32[]{:S(2)}, u32[]{:S(2)}) collective-permute-start(bf16[4,96,384]{2,1,0:T(8,128)(2,1)} %copy-done.108), channel_id=1, source_target_pairs={{0,4},{2,6},{4,0},{6,2},{8,12},{10,14},{12,8},{14,10},{1,5},{3,7},... | collective-permute-start | bytes 884744 | tf_op jit(solution)/shard_map/ppermute | solution.py:441
  373.8 33.5 %all-to-all-start.7 = ((bf16[8,64,768]{2,1,0:T(8,128)(2,1)}), bf16[8,64,768]{2,1,0:T(8,128)(2,1)}, u32[]{:S(2)}, u32[]{:S(2)}) async-start(bf16[8,64,768]{2,1,0:T(8,128)(2,1)} %bitcast.70), calls=%async_computation.7 | async-start | bytes 1572864 | tf_op jit(solution)/shard_map/all_to_all | solution.py:600
  379.8 27.5 %collective-permute-start.19 = (bf16[1536,384]{1,0:T(8,128)(2,1)}, bf16[1536,384]{1,0:T(8,128)(2,1)}, u32[]{:S(2)}, u32[]{:S(2)}) collective-permute-start(bf16[1536,384]{1,0:T(8,128)(2,1)} %copy-done.55), channel_id=1, source_target_pairs={{0,16},{16,0},{1,17},{17,1},{2,18},{18,2},{3,19},{19,3},{4,20},{20... | collective-permute-start | bytes 3538952 | tf_op jit(solution)/shard_map/ppermute | solution.py:436
  381.3 13.1 %collective-permute-start.20 = (bf16[2,96,384]{2,1,0:T(8,128)(2,1)S(1)}, bf16[2,96,384]{2,1,0:T(8,128)(2,1)S(1)}, u32[]{:S(2)}, u32[]{:S(2)}) collective-permute-start(bf16[2,96,384]{2,1,0:T(8,128)(2,1)S(1)} %copy-done.91), channel_id=1, source_target_pairs={{0,4},{2,6},{4,0},{6,2},{8,12},{10,14},{12,8},{14,10},{1,5},{3,7},... | collective-permute-start | bytes 442376 | tf_op jit(solution)/shard_map/ppermute | solution.py:441
  383.3 11.1 %collective-permute-start.21 = (bf16[2,96,384]{2,1,0:T(8,128)(2,1)}, bf16[2,96,384]{2,1,0:T(8,128)(2,1)S(1)}, u32[]{:S(2)}, u32[]{:S(2)}) collective-permute-start(bf16[2,96,384]{2,1,0:T(8,128)(2,1)} %copy-done.109), channel_id=1, source_target_pairs={{0,2},{2,0},{4,6},{6,4},{8,10},{10,8},{12,14},{14,12},{1,3},{3,1},... | collective-permute-start | bytes 442376 | tf_op jit(solution)/shard_map/ppermute | solution.py:441
  396.0 7.9 %collective-permute-start.22 = (bf16[1,96,384]{2,1,0:T(8,128)(2,1)S(1)}, bf16[1,96,384]{2,1,0:T(8,128)(2,1)S(1)}, u32[]{:S(2)}, u32[]{:S(2)}) collective-permute-start(bf16[1,96,384]{2,1,0:T(8,128)(2,1)S(1)} %get-tuple-element.152), channel_id=1, source_target_pairs={{0,8},{2,10},{4,12},{6,14},{8,0},{10,2},{12,4},{14,6},{1,9},{3,11}... | collective-permute-start | bytes 221192 | tf_op jit(solution)/shard_map/ppermute | solution.py:441
  400.8 5.3 collective-permute-start.23
  400.9 6.4 %collective-permute-start.24 = (f32[16,768]{1,0:T(8,128)S(1)}, f32[16,768]{1,0:T(8,128)S(1)}, u32[]{:S(2)}, u32[]{:S(2)}) collective-permute-start(f32[16,768]{1,0:T(8,128)S(1)} %constant_dynamic-update-slice_fusion), channel_id=1, source_target_pairs={{0,16},{16,0},{1,17},{17,1},{2,18},{18,2},{3,19},{19,3},{4,20},{20... | collective-permute-start | bytes 147464 | tf_op jit(solution)/shard_map/ppermute | solution.py:436
  409.1 13.8 %collective-permute-start.25 = (bf16[416,768]{1,0:T(8,128)(2,1)S(1)}, bf16[416,768]{1,0:T(8,128)(2,1)S(1)}, u32[]{:S(2)}, u32[]{:S(2)}) collective-permute-start(bf16[416,768]{1,0:T(8,128)(2,1)S(1)} %shard_map.172.refs_9_.refs_1_), channel_id=1, source_target_pairs={{0,16},{16,0},{1,17},{17,1},{2,18},{18,2},{3,19},{19,3},{4,20},{20... | collective-permute-start | bytes 1916936 | tf_op jit(solution)/shard_map/ppermute | solution.py:436
  445.0 17.6 %collective-permute-start.39 = (bf16[384,3072]{1,0:T(8,128)(2,1)}, bf16[384,3072]{1,0:T(8,128)(2,1)}, u32[]{:S(2)}, u32[]{:S(2)}) collective-permute-start(bf16[384,3072]{1,0:T(8,128)(2,1)} %get-tuple-element.186), channel_id=1, source_target_pairs={{0,1},{1,0},{2,3},{3,2},{4,5},{5,4},{6,7},{7,6},{8,9},{9,8},{10,11... | collective-permute-start | bytes 7077896 | tf_op jit(solution)/shard_map/ppermute | solution.py:436
  445.0 17.6 %collective-permute-start.40 = (bf16[3072,384]{1,0:T(8,128)(2,1)}, bf16[3072,384]{1,0:T(8,128)(2,1)}, u32[]{:S(2)}, u32[]{:S(2)}) collective-permute-start(bf16[3072,384]{1,0:T(8,128)(2,1)} %get-tuple-element.187), channel_id=1, source_target_pairs={{0,1},{1,0},{2,3},{3,2},{4,5},{5,4},{6,7},{7,6},{8,9},{9,8},{10,11... | collective-permute-start | bytes 7077896 | tf_op jit(solution)/shard_map/ppermute | solution.py:436
  445.5 25.4 %collective-permute-start.26 = (bf16[1536,384]{1,0:T(8,128)(2,1)}, bf16[1536,384]{1,0:T(8,128)(2,1)}, u32[]{:S(2)}, u32[]{:S(2)}) collective-permute-start(bf16[1536,384]{1,0:T(8,128)(2,1)} %get-tuple-element.164), channel_id=1, source_target_pairs={{0,1},{1,0},{2,3},{3,2},{4,5},{5,4},{6,7},{7,6},{8,9},{9,8},{10,11... | collective-permute-start | bytes 3538952 | tf_op jit(solution)/shard_map/ppermute | solution.py:436
  445.6 17.0 %collective-permute-start.28 = (bf16[416,768]{1,0:T(8,128)(2,1)}, bf16[416,768]{1,0:T(8,128)(2,1)}, u32[]{:S(2)}, u32[]{:S(2)}) collective-permute-start(bf16[416,768]{1,0:T(8,128)(2,1)} %get-tuple-element.166.refs_0_.refs_5_), channel_id=1, source_target_pairs={{0,16},{16,0},{1,17},{17,1},{2,18},{18,2},{3,19},{19,3},{4,20},{20... | collective-permute-start | bytes 1916936 | tf_op jit(solution)/shard_map/ppermute | solution.py:436
  447.1 54.2 %all-to-all-start.5 = ((bf16[8,64,768]{2,1,0:T(8,128)(2,1)}), bf16[8,64,768]{2,1,0:T(8,128)(2,1)S(1)}, u32[]{:S(2)}, u32[]{:S(2)}) async-start(bf16[8,64,768]{2,1,0:T(8,128)(2,1)} %bitcast.64), calls=%async_computation.5 | async-start | bytes 1572864 | tf_op jit(solution)/shard_map/all_to_all | solution.py:600
  468.9 51.1 %collective-permute-start.41 = (bf16[384,1536]{1,0:T(8,128)(2,1)}, bf16[384,1536]{1,0:T(8,128)(2,1)}, u32[]{:S(2)}, u32[]{:S(2)}) collective-permute-start(bf16[384,1536]{1,0:T(8,128)(2,1)} %get-tuple-element.188), channel_id=1, source_target_pairs={{0,16},{16,0},{1,17},{17,1},{2,18},{18,2},{3,19},{19,3},{4,20},{20... | collective-permute-start | bytes 3538952 | tf_op jit(solution)/shard_map/ppermute | solution.py:436
  470.4 78.6 %collective-permute-start.46 = (bf16[1536,384]{1,0:T(8,128)(2,1)}, bf16[1536,384]{1,0:T(8,128)(2,1)}, u32[]{:S(2)}, u32[]{:S(2)}) collective-permute-start(bf16[1536,384]{1,0:T(8,128)(2,1)} %get-tuple-element.193), channel_id=1, source_target_pairs={{0,16},{16,0},{1,17},{17,1},{2,18},{18,2},{3,19},{19,3},{4,20},{20... | collective-permute-start | bytes 3538952 | tf_op jit(solution)/shard_map/ppermute | solution.py:436
  472.6 23.2 %collective-permute-start.33 = (bf16[4,96,384]{2,1,0:T(8,128)(2,1)S(1)}, bf16[4,96,384]{2,1,0:T(8,128)(2,1)S(1)}, u32[]{:S(2)}, u32[]{:S(2)}) collective-permute-start(bf16[4,96,384]{2,1,0:T(8,128)(2,1)S(1)} %get-tuple-element.165.refs_2_), channel_id=1, source_target_pairs={{0,2},{2,0},{4,6},{6,4},{8,10},{10,8},{12,14},{14,12},{1,3},{3,1},... | collective-permute-start | bytes 884744 | tf_op jit(solution)/shard_map/ppermute | solution.py:441
  474.2 21.6 %collective-permute-start.34 = (bf16[4,96,384]{2,1,0:T(8,128)(2,1)S(1)}, bf16[4,96,384]{2,1,0:T(8,128)(2,1)S(1)}, u32[]{:S(2)}, u32[]{:S(2)}) collective-permute-start(bf16[4,96,384]{2,1,0:T(8,128)(2,1)S(1)} %get-tuple-element.175), channel_id=1, source_target_pairs={{0,4},{2,6},{4,0},{6,2},{8,12},{10,14},{12,8},{14,10},{1,5},{3,7},... | collective-permute-start | bytes 884744 | tf_op jit(solution)/shard_map/ppermute | solution.py:441
  475.6 6.9 %collective-permute-start.50 = (bf16[1,96,384]{2,1,0:T(8,128)(2,1)S(1)}, bf16[1,96,384]{2,1,0:T(8,128)(2,1)S(1)}, u32[]{:S(2)}, u32[]{:S(2)}) collective-permute-start(bf16[1,96,384]{2,1,0:T(8,128)(2,1)S(1)} %get-tuple-element.155.refs_3_.refs_1_), channel_id=1, source_target_pairs={{0,8},{2,10},{4,12},{6,14},{8,0},{10,2},{12,4},{14,6},{1,9},{3,11}... | collective-permute-start | bytes 221192 | tf_op jit(solution)/shard_map/ppermute | solution.py:441
  482.5 5.7 collective-permute-start.51
  489.5 9.7 %collective-permute-start.52 = (bf16[2,96,384]{2,1,0:T(8,128)(2,1)S(1)}, bf16[2,96,384]{2,1,0:T(8,128)(2,1)S(1)}, u32[]{:S(2)}, u32[]{:S(2)}) collective-permute-start(bf16[2,96,384]{2,1,0:T(8,128)(2,1)S(1)} %get-tuple-element.197.refs_1_), channel_id=1, source_target_pairs={{0,4},{2,6},{4,0},{6,2},{8,12},{10,14},{12,8},{14,10},{1,5},{3,7},... | collective-permute-start | bytes 442376 | tf_op jit(solution)/shard_map/ppermute | solution.py:441
  498.6 5.5 collective-permute-start.35
  498.6 6.9 %collective-permute-start.36 = (bf16[2,96,384]{2,1,0:T(8,128)(2,1)}, bf16[2,96,384]{2,1,0:T(8,128)(2,1)}, u32[]{:S(2)}, u32[]{:S(2)}) collective-permute-start(bf16[2,96,384]{2,1,0:T(8,128)(2,1)} %get-tuple-element.179), channel_id=1, source_target_pairs={{0,2},{2,0},{4,6},{6,4},{8,10},{10,8},{12,14},{14,12},{1,3},{3,1},... | collective-permute-start | bytes 442376 | tf_op jit(solution)/shard_map/ppermute | solution.py:441
  499.9 8.8 %collective-permute-start.53 = (bf16[2,96,384]{2,1,0:T(8,128)(2,1)}, bf16[2,96,384]{2,1,0:T(8,128)(2,1)}, u32[]{:S(2)}, u32[]{:S(2)}) collective-permute-start(bf16[2,96,384]{2,1,0:T(8,128)(2,1)} %get-tuple-element.198.refs_3_), channel_id=1, source_target_pairs={{0,2},{2,0},{4,6},{6,4},{8,10},{10,8},{12,14},{14,12},{1,3},{3,1},... | collective-permute-start | bytes 442376 | tf_op jit(solution)/shard_map/ppermute | solution.py:441
  504.0 47.5 %collective-permute-start.27 = (bf16[416,768]{1,0:T(8,128)(2,1)}, bf16[416,768]{1,0:T(8,128)(2,1)}, u32[]{:S(2)}, u32[]{:S(2)}) collective-permute-start(bf16[416,768]{1,0:T(8,128)(2,1)} %shard_map.176), channel_id=1, source_target_pairs={{0,16},{16,0},{1,17},{17,1},{2,18},{18,2},{3,19},{19,3},{4,20},{20... | collective-permute-start | bytes 1916936 | tf_op jit(solution)/shard_map/ppermute | solution.py:436
  505.6 4.7 collective-permute-start.29
  508.7 9.2 %collective-permute-start.37 = (bf16[1,96,384]{2,1,0:T(8,128)(2,1)S(1)}, bf16[1,96,384]{2,1,0:T(8,128)(2,1)S(1)}, u32[]{:S(2)}, u32[]{:S(2)}) collective-permute-start(bf16[1,96,384]{2,1,0:T(8,128)(2,1)S(1)} %get-tuple-element.181), channel_id=1, source_target_pairs={{0,8},{2,10},{4,12},{6,14},{8,0},{10,2},{12,4},{14,6},{1,9},{3,11}... | collective-permute-start | bytes 221192 | tf_op jit(solution)/shard_map/ppermute | solution.py:441
  510.3 8.8 %collective-permute-start.38 = (bf16[1,96,384]{2,1,0:T(8,128)(2,1)S(1)}, bf16[1,96,384]{2,1,0:T(8,128)(2,1)S(1)}, u32[]{:S(2)}, u32[]{:S(2)}) collective-permute-start(bf16[1,96,384]{2,1,0:T(8,128)(2,1)S(1)} %get-tuple-element.183), channel_id=1, source_target_pairs={{0,8},{2,10},{4,12},{6,14},{8,0},{10,2},{12,4},{14,6},{1,9},{3,11}... | collective-permute-start | bytes 221192 | tf_op jit(solution)/shard_map/ppermute | solution.py:441
  517.9 21.5 %collective-permute-start.54 = (bf16[4,96,384]{2,1,0:T(8,128)(2,1)S(1)}, bf16[4,96,384]{2,1,0:T(8,128)(2,1)S(1)}, u32[]{:S(2)}, u32[]{:S(2)}) collective-permute-start(bf16[4,96,384]{2,1,0:T(8,128)(2,1)S(1)} %get-tuple-element.199.refs_1_), channel_id=1, source_target_pairs={{0,2},{2,0},{4,6},{6,4},{8,10},{10,8},{12,14},{14,12},{1,3},{3,1},... | collective-permute-start | bytes 884744 | tf_op jit(solution)/shard_map/ppermute | solution.py:441
  519.0 7.0 %collective-permute-start.30 = (f32[20,768]{1,0:T(8,128)S(1)}, f32[20,768]{1,0:T(8,128)S(1)}, u32[]{:S(2)}, u32[]{:S(2)}) collective-permute-start(f32[20,768]{1,0:T(8,128)S(1)} %add.30), channel_id=1, source_target_pairs={{0,2},{2,0},{4,6},{6,4},{8,10},{10,8},{12,14},{14,12},{1,3},{3,1},... | collective-permute-start | bytes 184328 | tf_op jit(solution)/shard_map/ppermute | solution.py:441
  520.0 23.6 %collective-permute-start.55 = (bf16[4,96,384]{2,1,0:T(8,128)(2,1)S(1)}, bf16[4,96,384]{2,1,0:T(8,128)(2,1)S(1)}, u32[]{:S(2)}, u32[]{:S(2)}) collective-permute-start(bf16[4,96,384]{2,1,0:T(8,128)(2,1)S(1)} %get-tuple-element.200.refs_3_), channel_id=1, source_target_pairs={{0,4},{2,6},{4,0},{6,2},{8,12},{10,14},{12,8},{14,10},{1,5},{3,7},... | collective-permute-start | bytes 884744 | tf_op jit(solution)/shard_map/ppermute | solution.py:441
  526.0 6.7 %collective-permute-start.42 = (bf16[1,96,384]{2,1,0:T(8,128)(2,1)S(1)}, bf16[1,96,384]{2,1,0:T(8,128)(2,1)S(1)}, u32[]{:S(2)}, u32[]{:S(2)}) collective-permute-start(bf16[1,96,384]{2,1,0:T(8,128)(2,1)S(1)} %get-tuple-element.189.refs_1_), channel_id=1, source_target_pairs={{0,8},{2,10},{4,12},{6,14},{8,0},{10,2},{12,4},{14,6},{1,9},{3,11}... | collective-permute-start | bytes 221192 | tf_op jit(solution)/shard_map/ppermute | solution.py:441
  532.7 5.8 %collective-permute-start.43 = (bf16[1,96,384]{2,1,0:T(8,128)(2,1)S(1)}, bf16[1,96,384]{2,1,0:T(8,128)(2,1)S(1)}, u32[]{:S(2)}, u32[]{:S(2)}) collective-permute-start(bf16[1,96,384]{2,1,0:T(8,128)(2,1)S(1)} %get-tuple-element.190.refs_3_), channel_id=1, source_target_pairs={{0,8},{2,10},{4,12},{6,14},{8,0},{10,2},{12,4},{14,6},{1,9},{3,11}... | collective-permute-start | bytes 221192 | tf_op jit(solution)/shard_map/ppermute | solution.py:441
  538.6 4.4 collective-permute-start.31
  539.4 9.6 %collective-permute-start.44 = (bf16[2,96,384]{2,1,0:T(8,128)(2,1)S(1)}, bf16[2,96,384]{2,1,0:T(8,128)(2,1)S(1)}, u32[]{:S(2)}, u32[]{:S(2)}) collective-permute-start(bf16[2,96,384]{2,1,0:T(8,128)(2,1)S(1)} %get-tuple-element.191.refs_1_), channel_id=1, source_target_pairs={{0,4},{2,6},{4,0},{6,2},{8,12},{10,14},{12,8},{14,10},{1,5},{3,7},... | collective-permute-start | bytes 442376 | tf_op jit(solution)/shard_map/ppermute | solution.py:441
  542.9 6.0 %collective-permute-start.45 = (bf16[2,96,384]{2,1,0:T(8,128)(2,1)S(1)}, bf16[2,96,384]{2,1,0:T(8,128)(2,1)S(1)}, u32[]{:S(2)}, u32[]{:S(2)}) collective-permute-start(bf16[2,96,384]{2,1,0:T(8,128)(2,1)S(1)} %get-tuple-element.192.refs_3_), channel_id=1, source_target_pairs={{0,2},{2,0},{4,6},{6,4},{8,10},{10,8},{12,14},{14,12},{1,3},{3,1},... | collective-permute-start | bytes 442376 | tf_op jit(solution)/shard_map/ppermute | solution.py:441
  543.6 5.3 collective-permute-start.32
  548.9 13.4 %collective-permute-start.56 = (bf16[2,768,384]{2,1,0:T(8,128)(2,1)}, bf16[2,768,384]{2,1,0:T(8,128)(2,1)}, u32[]{:S(2)}, u32[]{:S(2)}) collective-permute-start(bf16[2,768,384]{2,1,0:T(8,128)(2,1)} %bitcast.34.refs_1_), channel_id=1, source_target_pairs={{0,1},{1,0},{2,3},{3,2},{4,5},{5,4},{6,7},{7,6},{8,9},{9,8},{10,11... | collective-permute-start | bytes 3538952 | tf_op jit(solution)/shard_map/ppermute | solution.py:436
  549.6 9.6 %collective-permute-start.47 = (bf16[4,96,384]{2,1,0:T(8,128)(2,1)S(1)}, bf16[4,96,384]{2,1,0:T(8,128)(2,1)S(1)}, u32[]{:S(2)}, u32[]{:S(2)}) collective-permute-start(bf16[4,96,384]{2,1,0:T(8,128)(2,1)S(1)} %get-tuple-element.194.refs_1_), channel_id=1, source_target_pairs={{0,2},{2,0},{4,6},{6,4},{8,10},{10,8},{12,14},{14,12},{1,3},{3,1},... | collective-permute-start | bytes 884744 | tf_op jit(solution)/shard_map/ppermute | solution.py:441
  551.5 9.1 %collective-permute-start.48 = (bf16[4,96,384]{2,1,0:T(8,128)(2,1)S(1)}, bf16[4,96,384]{2,1,0:T(8,128)(2,1)S(1)}, u32[]{:S(2)}, u32[]{:S(2)}) collective-permute-start(bf16[4,96,384]{2,1,0:T(8,128)(2,1)S(1)} %get-tuple-element.195.refs_3_), channel_id=1, source_target_pairs={{0,4},{2,6},{4,0},{6,2},{8,12},{10,14},{12,8},{14,10},{1,5},{3,7},... | collective-permute-start | bytes 884744 | tf_op jit(solution)/shard_map/ppermute | solution.py:441
  562.3 13.5 %collective-permute-start.49 = (bf16[2,768,384]{2,1,0:T(8,128)(2,1)}, bf16[2,768,384]{2,1,0:T(8,128)(2,1)}, u32[]{:S(2)}, u32[]{:S(2)}) collective-permute-start(bf16[2,768,384]{2,1,0:T(8,128)(2,1)} %bitcast.33.refs_1_), channel_id=1, source_target_pairs={{0,1},{1,0},{2,3},{3,2},{4,5},{5,4},{6,7},{7,6},{8,9},{9,8},{10,11... | collective-permute-start | bytes 3538952 | tf_op jit(solution)/shard_map/ppermute | solution.py:436
  (118 other events, 985.1 us)
